TPU v7x, 512 devices: a whole 4x4x16 slice. The times are simulated.
512 devices in a mesh: member: 32 (over x, z_lo), tile: 16 (over y, z_hi, core).
Axes of the slice: x: 4, y: 4, z: 16 (z_hi: 2, z_lo: 8; z = z_hi * 8 + z_lo), core: 2. Of those that a mesh axis runs over, the one named last changes fastest.
Arguments:
- saturation: float32 [32, 128, 64, 128], P('member', 'tile'), may hold values from 0.05 to 0.95
- mobility: float32 [32, 128, 64, 128], P('member', 'tile'), may hold values from 0.5 to 4
- pore_scale: float32 [32, 128, 64, 128], P('member', 'tile'), may hold values from 0.5 to 1.5
- flux_x: float32 [32, 128, 64, 128], P('member', 'tile'), may hold values from -0.15 to 0.15
- flux_y: float32 [32, 128, 64, 128], P('member', 'tile'), may hold values from -0.15 to 0.15
- flux_z: float32 [32, 128, 64, 128], P('member', 'tile'), may hold values from -0.15 to 0.15
- conn_cell: int32 [4096], P('tile'), may hold values from 0 to 65535
- conn_well: int32 [4096], P('tile'), may hold values from 0 to 127
- conn_factor: float32 [4096], P('tile'), may hold values from 0.02 to 0.2
- obs_error: float32 [128, 3], P('tile'), may hold values from 0.3 to 3
Outputs:
- new_saturation: float32 [32, 128, 64, 128], P('member', 'tile')
- well_rates: float32 [32, 128, 3], P('member', 'tile')
- gram: float32 [32, 32], P('member')
Inputs may be any that keep to these rules, and one draw needn't show every extreme that they name: `conn_cell`: a cell index within the block of grid rows of the tile that holds the connection, flattened over (row, layer, column). `conn_well`: a well index; any tile may hold connections of any well.
All inputs are finite; a program needn't handle non-finite values.
Results may differ from a plain program's by a relative error of at most 0.0003.
Values sent between devices are 32-bit elements; how exact they have to be, the bound alone decides.
No kernel may reach another device: no remote copies, remote signals or barrier semaphores. Data moves between devices by JAX's collectives and lax.ppermute only.
A program may use at most 64 MiB of HBM per device.

v0:
```python
import jax
import jax.numpy as jnp
from jax import lax
from jax.sharding import PartitionSpec as P

SUBSTEPS = 3


def with_halo(cells, sides, width):
    for axis, dim in sides:
        count = lax.axis_size(axis)
        ends = count - 1
        head = lax.slice_in_dim(cells, 0, width, axis=dim)
        tail = lax.slice_in_dim(cells, cells.shape[dim] - width, cells.shape[dim], axis=dim)
        cells = jnp.concatenate(
            [
                lax.ppermute(tail, axis, [(i, (i + 1) % count) for i in range(ends)]),
                cells,
                lax.ppermute(head, axis, [((i + 1) % count, i) for i in range(ends)]),
            ],
            axis=dim,
        )
    return cells


def frac(sat, mob):
    wet = sat * sat
    dry = (1.0 - sat) * (1.0 - sat)
    return wet / (wet + mob * dry)


def lower(field, axis):
    count = field.shape[axis]
    zero = jnp.zeros_like(lax.slice_in_dim(field, 0, 1, axis=axis))
    return jnp.concatenate([zero, lax.slice_in_dim(field, 0, count - 1, axis=axis)], axis=axis)


def upper(field, axis):
    count = field.shape[axis]
    zero = jnp.zeros_like(lax.slice_in_dim(field, 0, 1, axis=axis))
    return jnp.concatenate([lax.slice_in_dim(field, 1, count, axis=axis), zero], axis=axis)


def divergence(flow, flux, axis):
    face = jnp.maximum(flux, 0.0) * lower(flow, axis) + jnp.minimum(flux, 0.0) * flow
    return upper(face, axis) - face


def advance(sat_ext, mob_ext, qx_ext, qy_in, qz_in, pore_in):
    flow_ext = frac(sat_ext, mob_ext)
    crossing = qx_ext[:, 1:]
    face = (
        jnp.maximum(crossing, 0.0) * flow_ext[:, :-1] + jnp.minimum(crossing, 0.0) * flow_ext[:, 1:]
    )
    flow_in = flow_ext[:, 1:-1]
    total = (
        face[:, 1:] - face[:, :-1] + divergence(flow_in, qz_in, 2) + divergence(flow_in, qy_in, 3)
    )
    return sat_ext[:, 1:-1] - pore_in * total


def body(
    saturation,
    mobility,
    pore_scale,
    flux_x,
    flux_y,
    flux_z,
    conn_cell,
    conn_well,
    conn_factor,
    obs_error,
):
    members, rows, layers, columns = saturation.shape
    tiles = lax.axis_size("tile")
    first = lax.axis_index("tile") * rows
    total_rows = rows * tiles

    def place(shape, axis):
        return lax.broadcasted_iota(jnp.int32, shape, axis)

    row_ids = first + place(flux_x.shape, 1)
    qx = jnp.where(row_ids > 0, flux_x, jnp.zeros_like(flux_x))
    qz = jnp.where(place(flux_z.shape, 2) > 0, flux_z, jnp.zeros_like(flux_z))
    qy = jnp.where(place(flux_y.shape, 3) > 0, flux_y, jnp.zeros_like(flux_y))
    states = []
    fixed = with_halo(jnp.stack((qx, mobility)), (("tile", 2),), 1)
    qx_ext = fixed[0]
    mob_ext = fixed[1]
    global_rows = first - 1 + place(mob_ext.shape, 1)
    inside = (global_rows >= 0) & (global_rows < total_rows)
    mob_ext = jnp.where(inside, mob_ext, jnp.ones_like(mob_ext))
    current = saturation
    for step in range(SUBSTEPS):
        sat_ext = with_halo(current, (("tile", 1),), 1)
        current = advance(sat_ext, mob_ext, qx_ext, qy, qz, pore_scale)
        states.append(current)
    new_saturation = states[-1]
    mob_flat = jnp.take(mobility.reshape(members, -1), conn_cell, axis=1)
    parts = []
    for state in states:
        picked = jnp.take(state.reshape(members, -1), conn_cell, axis=1)
        parts.append(conn_factor[None, :] * frac(picked, mob_flat))
    contrib = jnp.stack(parts, -1)
    table = jnp.transpose(contrib, (1, 0, 2)).reshape(conn_cell.shape[0], -1)
    wells_dev = obs_error.shape[0]
    targets = lax.iota(jnp.int32, wells_dev * tiles)
    onehot = (conn_well[None, :] == targets[:, None]).astype(jnp.float32)
    whole = lax.psum(jnp.dot(onehot, table, precision=lax.Precision.HIGHEST), "tile")
    mine = lax.dynamic_slice_in_dim(whole, lax.axis_index("tile") * wells_dev, wells_dev, 0)
    well_rates = jnp.transpose(mine.reshape(wells_dev, members, SUBSTEPS), (1, 0, 2))
    scaled = (well_rates / obs_error[None]).reshape(members, -1)
    ensemble = members * lax.axis_size("member")
    gathered = lax.all_gather(scaled, "member", axis=0, tiled=True)
    centered = gathered - jnp.mean(gathered, axis=0, keepdims=True)
    own = lax.dynamic_slice_in_dim(centered, lax.axis_index("member") * members, members, 0)
    partial_gram = jnp.dot(own, centered.T, precision=lax.Precision.HIGHEST)
    gram = lax.psum(partial_gram, "tile") / (ensemble - 1.0)
    return (new_saturation, well_rates, gram)


def solution(mesh):
    in_specs = (
        P("member", "tile", None, None),
        P("member", "tile", None, None),
        P("member", "tile", None, None),
        P("member", "tile", None, None),
        P("member", "tile", None, None),
        P("member", "tile", None, None),
        P("tile"),
        P("tile"),
        P("tile"),
        P("tile", None),
    )
    out_specs = (P("member", "tile", None, None), P("member", "tile", None), P("member", None))
    return jax.shard_map(body, mesh=mesh, in_specs=in_specs, out_specs=out_specs, check_vma=False)
```

profile of v0, /device:TPU:1, one launch (start us, length us, event | category | flops | bytes accessed | tf_op | source)
XLA Modules:
  0.0 324.9 jit_solution(17395099698311845910)
XLA Ops:
  0.6 0.8 fusion.35
  1.4 8.8 %collective-permute-start.3 = (f32[1,1,64,128]{3,2,1,0:T(8,128)S(1)}, f32[1,1,64,128]{3,2,1,0:T(8,128)S(1)}, u32[]{:S(2)}, u32[]{:S(2)}) collective-permute-start(f32[1,1,64,128]{3,2,1,0:T(8,128)S(1)} %get-tuple-element.27), channel_id=1, source_target_pairs={{1,0},{2,1},{3,2},{4,3},{5,4},{6,5},{7,6},{8,7},{9,8},{10,9},{11,1... | collective-permute-start | bytes 98312 | tf_op jit(solution)/shard_map/ppermute | solution.py:19
  10.2 10.0 %collective-permute-start.2 = (f32[1,1,64,128]{3,2,1,0:T(8,128)S(1)}, f32[1,1,64,128]{3,2,1,0:T(8,128)S(1)}, u32[]{:S(2)}, u32[]{:S(2)}) collective-permute-start(f32[1,1,64,128]{3,2,1,0:T(8,128)S(1)} %get-tuple-element.28), channel_id=1, source_target_pairs={{0,1},{1,2},{2,3},{3,4},{4,5},{5,6},{6,7},{7,8},{8,9},{9,10},{10,1... | collective-permute-start | bytes 98312 | tf_op jit(solution)/shard_map/ppermute | solution.py:17
  20.2 1.1 select_bitcast_fusion
  21.3 2.5 collective-permute-start
  23.9 1.9 collective-permute-start.1
  25.8 0.7 copy-done.6
  26.6 11.8 %collective-permute-done.1 = f32[2,1,1,64,128]{4,3,2,1,0:T(8,128)S(1)} collective-permute-done((f32[2,1,1,64,128]{4,3,2,1,0:T(8,128)S(1)}, f32[2,1,1,64,128]{4,3,2,1,0:T(8,128)S(1)}, u32[]{:S(2)}, u32[]{:S(2)}) %collective-permute-start.1) | collective-permute-done | bytes 65568 | tf_op jit(solution)/shard_map/ppermute | solution.py:19
  38.7 0.9 copy-done.2
  40.1 0.9 copy-done.4
  41.2 1.9 collective-permute-start.4
  43.1 2.4 collective-permute-start.5
  45.5 1.7 gather_fusion.1
  47.2 1.7 gather_fusion
  49.0 9.0 %collective-permute-done.5 = f32[1,1,64,128]{3,2,1,0:T(8,128)S(1)} collective-permute-done((f32[1,1,64,128]{3,2,1,0:T(8,128)S(1)}, f32[1,1,64,128]{3,2,1,0:T(8,128)S(1)}, u32[]{:S(2)}, u32[]{:S(2)}) %collective-permute-start.5) | collective-permute-done | bytes 32800 | tf_op jit(solution)/shard_map/ppermute | solution.py:19
  58.7 3.8 %collective-permute-start.6 = (f32[1,1,64,128]{3,2,1,0:T(8,128)S(1)}, f32[1,1,64,128]{3,2,1,0:T(8,128)S(1)}, u32[]{:S(2)}, u32[]{:S(2)}) collective-permute-start(f32[1,1,64,128]{3,2,1,0:T(8,128)S(1)} %get-tuple-element.23), channel_id=1, source_target_pairs={{0,1},{1,2},{2,3},{3,4},{4,5},{5,6},{6,7},{7,8},{8,9},{9,10},{10,1... | collective-permute-start | bytes 98312 | tf_op jit(solution)/shard_map/ppermute | solution.py:17
  62.6 1.9 collective-permute-start.7
  64.5 1.7 gather_fusion.2
  66.2 10.3 %collective-permute-done.7 = f32[1,1,64,128]{3,2,1,0:T(8,128)S(1)} collective-permute-done((f32[1,1,64,128]{3,2,1,0:T(8,128)S(1)}, f32[1,1,64,128]{3,2,1,0:T(8,128)S(1)}, u32[]{:S(2)}, u32[]{:S(2)}) %collective-permute-start.7) | collective-permute-done | bytes 32800 | tf_op jit(solution)/shard_map/ppermute | solution.py:19
  77.3 1.7 gather_fusion.3
  79.0 0.7 copy-done.8
  80.5 57.0 %psum.14 = f32[128,3]{0,1:T(4,128)S(1)} all-reduce(f32[128,3]{0,1:T(4,128)S(1)} %fusion.16), channel_id=1, replica_groups=mesh['member'=32,'tile'=16] {'tile'}, use_global_device_ids=true, to_apply=%region_0.2 | all-reduce | flops 384 | bytes 3072 | tf_op jit(solution)/shard_map/psum | solution.py:109
  138.3 103.2 %all-gather = f32[32,1,24]{2,1,0:T(1,128)S(1)} all-gather(f32[1,1,24]{2,1,0:T(1,128)S(1)} %reshape.408), channel_id=1, replica_groups=mesh['member'=32,'tile'=16] {'member'}, dimensions={0}, use_global_device_ids=true | all-gather | bytes 3168 | tf_op jit(solution)/shard_map/all_gather | solution.py:114
  241.8 82.7 %psum.15 = f32[1,32]{1,0:T(1,128)S(1)} all-reduce(f32[1,32]{1,0:T(1,128)S(1)} %fusion.28), channel_id=1, replica_groups=mesh['member'=32,'tile'=16] {'tile'}, use_global_device_ids=true, to_apply=%region_2.4 | all-reduce | flops 32 | bytes 256 | tf_op jit(solution)/shard_map/psum | solution.py:118
  (72 shorter events, 4.7 us)
Async XLA Ops:
  1.4 25.2 %collective-permute-start.3 = (f32[1,1,64,128]{3,2,1,0:T(8,128)S(1)}, f32[1,1,64,128]{3,2,1,0:T(8,128)S(1)}, u32[]{:S(2)}, u32[]{:S(2)}) collective-permute-start(f32[1,1,64,128]{3,2,1,0:T(8,128)S(1)} %get-tuple-element.27), channel_id=1, source_target_pairs={{1,0},{2,1},{3,2},{4,3},{5,4},{6,5},{7,6},{8,7},{9,8},{10,9},{11,1... | collective-permute-start | bytes 98312 | tf_op jit(solution)/shard_map/ppermute | solution.py:19
  10.2 16.3 %collective-permute-start.2 = (f32[1,1,64,128]{3,2,1,0:T(8,128)S(1)}, f32[1,1,64,128]{3,2,1,0:T(8,128)S(1)}, u32[]{:S(2)}, u32[]{:S(2)}) collective-permute-start(f32[1,1,64,128]{3,2,1,0:T(8,128)S(1)} %get-tuple-element.28), channel_id=1, source_target_pairs={{0,1},{1,2},{2,3},{3,4},{4,5},{5,6},{6,7},{7,8},{8,9},{9,10},{10,1... | collective-permute-start | bytes 98312 | tf_op jit(solution)/shard_map/ppermute | solution.py:17
  20.2 1.1 copy-start
  21.3 5.2 %copy-start.5 = (f32[1,8,64,128]{3,2,1,0:T(8,128)S(1)}, f32[1,8,64,128]{3,2,1,0:T(8,128)}, u32[]{:S(2)}) copy-start(f32[1,8,64,128]{3,2,1,0:T(8,128)} %param.12) | copy-start | bytes 786436
  21.3 5.3 %collective-permute-start = (f32[2,1,1,64,128]{4,3,2,1,0:T(8,128)S(1)}, f32[2,1,1,64,128]{4,3,2,1,0:T(8,128)S(1)}, u32[]{:S(2)}, u32[]{:S(2)}) collective-permute-start(f32[2,1,1,64,128]{4,3,2,1,0:T(8,128)S(1)} %get-tuple-element.15), channel_id=1, source_target_pairs={{0,1},{1,2},{2,3},{3,4},{4,5},{5,6},{6,7},{7,8},{8,9},{9,10},{10,1... | collective-permute-start | bytes 196616 | tf_op jit(solution)/shard_map/ppermute | solution.py:17
  23.9 14.5 %collective-permute-start.1 = (f32[2,1,1,64,128]{4,3,2,1,0:T(8,128)S(1)}, f32[2,1,1,64,128]{4,3,2,1,0:T(8,128)S(1)}, u32[]{:S(2)}, u32[]{:S(2)}) collective-permute-start(f32[2,1,1,64,128]{4,3,2,1,0:T(8,128)S(1)} %get-tuple-element.16), channel_id=1, source_target_pairs={{1,0},{2,1},{3,2},{4,3},{5,4},{6,5},{7,6},{8,7},{9,8},{10,9},{11,1... | collective-permute-start | bytes 196616 | tf_op jit(solution)/shard_map/ppermute | solution.py:19
  25.8 0.7 copy-start.6
  38.7 1.0 copy-start.2
  38.7 1.0 copy-start.3
  40.0 1.0 copy-start.4
  41.2 7.8 %collective-permute-start.4 = (f32[1,1,64,128]{3,2,1,0:T(8,128)S(1)}, f32[1,1,64,128]{3,2,1,0:T(8,128)S(1)}, u32[]{:S(2)}, u32[]{:S(2)}) collective-permute-start(f32[1,1,64,128]{3,2,1,0:T(8,128)S(1)} %get-tuple-element.25), channel_id=1, source_target_pairs={{0,1},{1,2},{2,3},{3,4},{4,5},{5,6},{6,7},{7,8},{8,9},{9,10},{10,1... | collective-permute-start | bytes 98312 | tf_op jit(solution)/shard_map/ppermute | solution.py:17
  43.1 14.9 %collective-permute-start.5 = (f32[1,1,64,128]{3,2,1,0:T(8,128)S(1)}, f32[1,1,64,128]{3,2,1,0:T(8,128)S(1)}, u32[]{:S(2)}, u32[]{:S(2)}) collective-permute-start(f32[1,1,64,128]{3,2,1,0:T(8,128)S(1)} %get-tuple-element.26), channel_id=1, source_target_pairs={{1,0},{2,1},{3,2},{4,3},{5,4},{6,5},{7,6},{8,7},{9,8},{10,9},{11,1... | collective-permute-start | bytes 98312 | tf_op jit(solution)/shard_map/ppermute | solution.py:19
  58.7 7.5 %collective-permute-start.6 = (f32[1,1,64,128]{3,2,1,0:T(8,128)S(1)}, f32[1,1,64,128]{3,2,1,0:T(8,128)S(1)}, u32[]{:S(2)}, u32[]{:S(2)}) collective-permute-start(f32[1,1,64,128]{3,2,1,0:T(8,128)S(1)} %get-tuple-element.23), channel_id=1, source_target_pairs={{0,1},{1,2},{2,3},{3,4},{4,5},{5,6},{6,7},{7,8},{8,9},{9,10},{10,1... | collective-permute-start | bytes 98312 | tf_op jit(solution)/shard_map/ppermute | solution.py:17
  62.6 13.9 %collective-permute-start.7 = (f32[1,1,64,128]{3,2,1,0:T(8,128)S(1)}, f32[1,1,64,128]{3,2,1,0:T(8,128)S(1)}, u32[]{:S(2)}, u32[]{:S(2)}) collective-permute-start(f32[1,1,64,128]{3,2,1,0:T(8,128)S(1)} %get-tuple-element.24), channel_id=1, source_target_pairs={{1,0},{2,1},{3,2},{4,3},{5,4},{6,5},{7,6},{8,7},{9,8},{10,9},{11,1... | collective-permute-start | bytes 98312 | tf_op jit(solution)/shard_map/ppermute | solution.py:19
  77.2 1.7 copy-start.1
  79.0 0.7 copy-start.8
  79.7 0.7 copy-start.9
  80.5 57.0 %copy-start.7 = (f32[8,3]{0,1:T(4,128)S(1)}, f32[8,3]{0,1:T(4,128)}, u32[]{:S(2)}) copy-start(f32[8,3]{0,1:T(4,128)} %param.21) | copy-start | bytes 292
where the time goes:
time: 325 us
  blocking collectives  243 us (75%)
  starting transfers between devices  33.3 us (10%)
  waiting for transfers between devices  31 us (10%)
  local copies, waits for them, and re-layouts  12.9 us (4%)
  other arithmetic  3.39 us (1%)
    all_gather x1, blocking collectives, body(): gathered = lax.all_gather(scaled, 'member', axis=0, tiled=True)  103 us
    psum x1, blocking collectives, body(): gram = lax.psum(partial_gram, 'tile') / (ensemble - 1.0)  82.7 us
    psum x1, blocking collectives, body(): lax.psum(jnp.dot(onehot, table, precision=lax.Precision.HIGHEST), 'tile')  57 us
    ppermute x4, waiting for transfers between devices, with_halo(): lax.ppermute(head, axis, [((i + 1) % count, i) for i in range(ends)])  31 us
    ppermute x4, starting transfers between devices, with_halo(): lax.ppermute(tail, axis, [(i, (i + 1) % count) for i in range(ends)])  18.3 us
    ppermute x4, starting transfers between devices, with_halo(): lax.ppermute(head, axis, [((i + 1) % count, i) for i in range(ends)])  15 us
  transfers between devices with their start and end apart: 8, of which 3 were waited for; matrix products, arithmetic and copies ran while one was open for 2% of the time, Pallas kernels for 0%

commit v1 on v0

v1 whole, which is shorter than its diff:
```python
import jax
import jax.numpy as jnp
from jax import lax
from jax.experimental import pallas as pl
from jax.experimental.pallas import tpu as pltpu
from jax.sharding import Mesh
from jax.sharding import PartitionSpec as P

SUBSTEPS = 3
AXES = ("x", "zl", "y", "zh", "c")
SIZES = (4, 8, 4, 2, 2)
MEMBER = ("x", "zl")
TILE = ("y", "zh", "c")
LINE = ("zl", "zh", "c")
PLANE = ("x", "y")
UP_ROWS = 8
DOWN_ROWS = 9
HIGHEST = lax.Precision.HIGHEST


def frac(sat, mob):
    wet = sat * sat
    dry = (1.0 - sat) * (1.0 - sat)
    return wet / (wet + mob * dry)


def inner(flux, axis):
    return jnp.where(lax.broadcasted_iota(jnp.int32, flux.shape, axis) > 0, flux, 0.0)


def spread(flow, flux, axis):
    count = flow.shape[axis]
    face = jnp.maximum(flux, 0.0) * pltpu.roll(flow, 1, axis) + jnp.minimum(flux, 0.0) * flow
    return pltpu.roll(face, count - 1, axis) - face


def across(flux, below, here):
    return jnp.maximum(flux, 0.0) * below + jnp.minimum(flux, 0.0) * here


def edge_kernel(sat, mob, pore, qx, qy, qz, up, down):
    f = {i: frac(sat[i], mob[i]) for i in (0, 1, 2, 5, 6, 7)}

    def face(i):
        return across(qx[i], f[i - 1], f[i])

    def advanced(i, low, high):
        total = (
            high - low + spread(f[i], inner(qz[i], 0), 0) + spread(f[i], inner(qy[i], 1), 1)
        )
        return frac(sat[i] - pore[i] * total, mob[i])

    face_1 = face(1)
    face_7 = face(7)
    flow_1 = advanced(1, face_1, face(2))
    flow_6 = advanced(6, face(6), face_7)
    for row, out in ((7, up), (0, down)):
        out[0] = sat[row]
        out[1] = mob[row]
        out[2] = pore[row]
        out[3] = qz[row]
        out[4] = qy[row]
    up[5] = face_7
    up[6] = jnp.maximum(qx[7], 0.0) * flow_6
    up[7] = jnp.minimum(qx[7], 0.0)
    down[5] = qx[0]
    down[6] = face_1
    down[7] = jnp.maximum(qx[1], 0.0)
    down[8] = jnp.minimum(qx[1], 0.0) * flow_1


def main_kernel(
    sat, mob, pore, qx, qy, qz, low, high, cell, well, factor, obs, where, new_sat, shares, s, f
):
    tile = where[0]
    last = where[1]
    rows = sat.shape[0]
    layers, columns = sat.shape[1], sat.shape[2]
    cells = rows * layers

    def at(i, own, k):
        if i < 0:
            return low[k]
        if i == rows:
            return high[k]
        return own[i]

    def mob_at(i):
        if i < 0:
            return jnp.where(tile > 0, low[1], 1.0)
        if i == rows:
            return jnp.where(tile < last, high[1], 1.0)
        return mob[i]

    def qx_at(i):
        if i == 0:
            return jnp.where(tile > 0, qx[0], 0.0)
        if i == rows:
            return high[5]
        return qx[i]

    row_of = cell[...] // columns
    column_of = cell[...] - row_of * columns
    count = cell.shape[1]
    pick_row = (lax.broadcasted_iota(jnp.int32, (cells, count), 0) == row_of).astype(jnp.float32)
    pick_column = lax.broadcasted_iota(jnp.int32, (columns, count), 0) == column_of
    picked = []
    for step in range(SUBSTEPS):
        for i in range(-1, rows + 1):
            now = at(i, sat, 0) if step == 0 else s[i + 1]
            f[i + 1] = frac(now, mob_at(i))
        first, stop = (0, rows) if step == SUBSTEPS - 1 else (-1, rows + 1)
        if first == 0:
            face = across(qx_at(0), f[0], f[1])
        elif step == 0:
            face = low[5]
        else:
            face = low[6] + low[7] * f[0]
        for i in range(first, stop):
            if i < rows:
                above = across(qx_at(i + 1), f[i + 1], f[i + 2])
            elif step == 0:
                above = high[6]
            else:
                above = high[7] * f[i + 1] + high[8]
            flow = f[i + 1]
            total = (
                above
                - face
                + spread(flow, inner(at(i, qz, 3), 0), 0)
                + spread(flow, inner(at(i, qy, 4), 1), 1)
            )
            face = above
            now = at(i, sat, 0) if step == 0 else s[i + 1]
            moved = now - at(i, pore, 2) * total
            if step < SUBSTEPS - 1:
                s[i + 1] = moved
            else:
                new_sat[i] = moved
                f[i + 1] = frac(moved, mob[i])
        if step < SUBSTEPS - 1:
            flows = jnp.concatenate([frac(s[i + 1], mob[i]) for i in range(rows)], axis=0)
        else:
            flows = jnp.concatenate([f[i + 1] for i in range(rows)], axis=0)
        rows_of = lax.dot_general(
            flows, pick_row, (((0,), (0,)), ((), ())), precision=HIGHEST,
            preferred_element_type=jnp.float32,
        )
        picked.append(jnp.sum(jnp.where(pick_column, rows_of, 0.0), axis=0, keepdims=True))
    contrib = jnp.concatenate(picked, axis=0) * factor[...]
    wells = shares.shape[2]
    by_well = (lax.broadcasted_iota(jnp.int32, (wells, count), 0) == well[...]).astype(jnp.float32)
    rates = lax.dot_general(
        contrib, by_well, (((1,), (1,)), ((), ())), precision=HIGHEST,
        preferred_element_type=jnp.float32,
    )
    mine = obs.shape[0]
    lane = lax.broadcasted_iota(jnp.int32, (mine, wells), 1)
    sublane = lax.broadcasted_iota(jnp.int32, (mine, wells), 0)
    place = lane == sublane + tile * mine
    errors = [
        jnp.sum(jnp.where(place, obs[:, k : k + 1], 0.0), axis=0, keepdims=True)
        for k in range(SUBSTEPS)
    ]
    share = jnp.concatenate([rates] + errors + [jnp.zeros((2, wells), jnp.float32)], axis=0)
    shares[...] = jnp.broadcast_to(share[None], shares.shape)


def line_kernel(parts, out, t):
    members = 8
    per = parts.shape[0] // members
    for m in range(members):
        total = parts[m * per]
        for j in range(1, per):
            total = total + parts[m * per + j]
        t[8 * m : 8 * m + 8] = total
    block = jnp.concatenate(
        [t[pl.ds(k, members, stride=8), :] for k in range(SUBSTEPS)]
        + [t[SUBSTEPS : 2 * SUBSTEPS], jnp.zeros((5, t.shape[1]), jnp.float32)],
        axis=0,
    )
    out[...] = jnp.broadcast_to(block[None], out.shape)


def gram_kernel(parts, where, rates_out, gram):
    tile = where[0]
    own_x = where[2]
    own_z = where[3]
    groups, per, layer = 4, 4, 8
    sums = []
    for g in range(groups):
        total = parts[g * per]
        for j in range(1, per):
            total = total + parts[g * per + j]
        sums.append(total)
    ensemble = groups * layer
    mask_z = lax.broadcasted_iota(jnp.int32, (layer, sums[0].shape[1]), 0) == own_z
    line = jnp.zeros(gram.shape, jnp.float32)
    wells = rates_out.shape[2]
    pick = (
        lax.broadcasted_iota(jnp.int32, (wells, sums[0].shape[1]), 1)
        == lax.broadcasted_iota(jnp.int32, (wells, sums[0].shape[1]), 0) + tile * wells
    ).astype(jnp.float32)
    for k in range(SUBSTEPS):
        rates = [total[k * layer : (k + 1) * layer] for total in sums]
        error = sums[0][SUBSTEPS * layer + k : SUBSTEPS * layer + k + 1]
        mine = jnp.zeros_like(rates[0])
        for g in range(groups):
            mine = jnp.where(jnp.logical_and(mask_z, own_x == g), rates[g], mine)
        mine = jnp.sum(mine, axis=0, keepdims=True)
        rates_out[k] = lax.dot_general(
            mine, pick, (((1,), (1,)), ((), ())), precision=HIGHEST,
            preferred_element_type=jnp.float32,
        )
        data = [rate / error for rate in rates]
        mean = jnp.sum(sum(data[1:], data[0]), axis=0, keepdims=True) / ensemble
        centered = jnp.concatenate(data, axis=0) - mean
        own = mine / error - mean
        line = line + lax.dot_general(
            own, centered, (((1,), (1,)), ((), ())), precision=HIGHEST,
            preferred_element_type=jnp.float32,
        )
    gram[...] = line / (ensemble - 1.0)


VMEM = pl.BlockSpec(memory_space=pltpu.VMEM)
SMEM = pl.BlockSpec(memory_space=pltpu.SMEM)


def shape(*dims):
    return jax.ShapeDtypeStruct(dims, jnp.float32)


def body(
    saturation,
    mobility,
    pore_scale,
    flux_x,
    flux_y,
    flux_z,
    conn_cell,
    conn_well,
    conn_factor,
    obs_error,
):
    rows, layers, columns = saturation.shape[1:]
    fields = [
        a.reshape(rows, layers, columns)
        for a in (saturation, mobility, pore_scale, flux_x, flux_y, flux_z)
    ]
    tiles = lax.axis_size(TILE)
    tile = lax.axis_index(TILE)
    where = jnp.stack(
        [tile, jnp.full_like(tile, tiles - 1), lax.axis_index("x"), lax.axis_index("zl")]
    ).astype(jnp.int32)
    up, down = pl.pallas_call(
        edge_kernel,
        out_shape=(shape(UP_ROWS, layers, columns), shape(DOWN_ROWS, layers, columns)),
        in_specs=[VMEM] * 6,
        out_specs=(VMEM, VMEM),
        name="edges",
    )(*fields)
    low = lax.ppermute(up, TILE, [(i, i + 1) for i in range(tiles - 1)])
    high = lax.ppermute(down, TILE, [(i + 1, i) for i in range(tiles - 1)])
    wells = obs_error.shape[0] * tiles
    count = conn_cell.shape[0]
    new_saturation, shares = pl.pallas_call(
        main_kernel,
        out_shape=(shape(rows, layers, columns), shape(32, 8, wells)),
        in_specs=[VMEM] * 12 + [SMEM],
        out_specs=(VMEM, VMEM),
        scratch_shapes=[
            pltpu.VMEM((rows + 2, layers, columns), jnp.float32),
            pltpu.VMEM((rows + 2, layers, columns), jnp.float32),
        ],
        compiler_params=pltpu.CompilerParams(vmem_limit_bytes=32 * 1024 * 1024),
        name="transport",
    )(
        *fields,
        low,
        high,
        conn_cell.reshape(1, count),
        conn_well.reshape(1, count),
        conn_factor.reshape(1, count),
        obs_error,
        where,
    )
    line = lax.all_to_all(shares, LINE, 0, 0)
    spreads = pl.pallas_call(
        line_kernel,
        out_shape=shape(16, 32, wells),
        in_specs=[VMEM],
        out_specs=VMEM,
        scratch_shapes=[pltpu.VMEM((64, wells), jnp.float32)],
        name="line_sums",
    )(line)
    plane = lax.all_to_all(spreads, PLANE, 0, 0)
    rates, gram = pl.pallas_call(
        gram_kernel,
        out_shape=(shape(SUBSTEPS, 1, obs_error.shape[0]), shape(1, 32)),
        in_specs=[VMEM, SMEM],
        out_specs=(VMEM, VMEM),
        name="gram_row",
    )(plane, where)
    return (
        new_saturation.reshape(saturation.shape),
        jnp.transpose(rates, (1, 2, 0)),
        gram,
    )


def solution(mesh):
    split = Mesh(mesh.devices.reshape(SIZES), AXES)
    in_specs = (P(MEMBER, TILE, None, None),) * 6 + (P(TILE),) * 3 + (P(TILE, None),)
    out_specs = (P(MEMBER, TILE, None, None), P(MEMBER, TILE, None), P(MEMBER, None))
    return jax.shard_map(body, mesh=split, in_specs=in_specs, out_specs=out_specs, check_vma=False)
```

time: 325 us -> 94.9 us (0.29)
  blocking collectives: 243 us -> 52.4 us
  waiting for transfers between devices: 31 us -> 11.9 us
  starting transfers between devices: 33.3 us -> 18.7 us
  local copies, waits for them, and re-layouts: 12.9 us -> 1.4 us
  Pallas kernels: 0 us -> 9.14 us
  other arithmetic: 3.39 us -> 0.08 us
    psum x2 -> x0, blocking collectives: 140 us -> none  [the longest x1 82.7 us: body(): gram = lax.psum(partial_gram, 'tile') / (ensemble - 1.0)]
    all_gather x1 -> x0, blocking collectives: 103 us -> none  [body(): gathered = lax.all_gather(scaled, 'member', axis=0, tiled=True)]
    all_to_all x0 -> x2, blocking collectives: none -> 52.4 us  [the longest x1 35.4 us: body(): line = lax.all_to_all(shares, LINE, 0, 0)]
    ppermute x8 -> x2, waiting for transfers between devices: 31 us -> 11.9 us  [the longest x1 11.9 us: body(): low = lax.ppermute(up, TILE, [(i, i + 1) for i in range(tiles - 1)])]
    ppermute x8 -> x2, starting transfers between devices: 33.3 us -> 18.7 us  [the longest x1 9.97 us: body(): low = lax.ppermute(up, TILE, [(i, i + 1) for i in range(tiles - 1)])]
    pallas_call x0 -> x4, Pallas kernels: none -> 9.14 us  [the longest x1 3.28 us: body(): pl.pallas_call(main_kernel, out_shape=(shape(rows, layers, columns), shap...]
    gather x4 -> x0, local copies, waits for them, and re-layouts: 6.89 us -> none  [the longest x3 5.17 us: body(): picked = jnp.take(state.reshape(members, -1), conn_cell, axis=1)]
  transfers between devices with their start and end apart: 8 -> 2, of which waited for: 3 -> 1; matrix products, arithmetic and copies ran while one was open for 2% -> 0% of each run, Pallas kernels for 0% -> 0%
where the time goes in v1:
time: 94.9 us; the launch traced here: 94.5 us
  blocking collectives  52.4 us (55%)
  starting transfers between devices  18.7 us (20%)
  waiting for transfers between devices  11.9 us (13%)
  Pallas kernels  9.14 us (10%)
  local copies, waits for them, and re-layouts  1.4 us (1%)
    all_to_all x1, blocking collectives, body(): line = lax.all_to_all(shares, LINE, 0, 0)  35.4 us
    all_to_all x1, blocking collectives, body(): plane = lax.all_to_all(spreads, PLANE, 0, 0)  17.1 us
    ppermute x1, waiting for transfers between devices, body(): low = lax.ppermute(up, TILE, [(i, i + 1) for i in range(tiles - 1)])  11.9 us
    ppermute x1, starting transfers between devices, body(): low = lax.ppermute(up, TILE, [(i, i + 1) for i in range(tiles - 1)])  9.97 us
    ppermute x1, starting transfers between devices, body(): high = lax.ppermute(down, TILE, [(i + 1, i) for i in range(tiles - 1)])  8.77 us
    pallas_call x1, Pallas kernels, body(): pl.pallas_call(main_kernel, out_shape=(shape(rows, layers, columns), shap...  3.28 us
    pallas_call x1, Pallas kernels, body(): pl.pallas_call(edge_kernel, out_shape=(shape(UP_ROWS, layers, columns), s...  2.44 us
  transfers between devices with their start and end apart: 2, of which 1 were waited for; matrix products, arithmetic and copies ran while one was open for 0% of the time, Pallas kernels for 0%

profile of v1, /device:TPU:1, one launch (start us, length us, event | category | flops | bytes accessed | tf_op | source)
XLA Modules:
  0.0 94.5 jit_solution(15210992400671608563)
XLA Ops:
  0.6 0.0 copy-start
  0.7 2.4 %edges.1 = (f32[8,64,128]{2,1,0:T(8,128)}, f32[9,64,128]{2,1,0:T(8,128)}) custom-call(f32[8,64,128]{2,1,0:T(8,128)} %bitcast.14, f32[8,64,128]{2,1,0:T(8,128)} %bitcast.16, f32[8,64,128]{2,1,0:T(8,128)} %bitcast.18, f32[8,64,128]{2,1,0:T(8,128)} %bitcast.20, f32[8,64,128]{2,1,0:T(8,128)} %bitcast.22, f32[8,64,128]{2,1,0:T(8,128)} %bitcast.24), custom_call_target="tpu_custom_call" | custom-call | tf_op jit(solution)/shard_map/edges/pallas_call | solution.py:256
  3.1 8.8 %collective-permute-start.1 = (f32[9,64,128]{2,1,0:T(8,128)}, f32[9,64,128]{2,1,0:T(8,128)S(1)}, u32[]{:S(2)}, u32[]{:S(2)}) collective-permute-start(f32[9,64,128]{2,1,0:T(8,128)} %get-tuple-element.10), channel_id=1, source_target_pairs={{1,0},{2,1},{3,2},{4,3},{5,4},{6,5},{7,6},{8,7},{9,8},{10,9},{11,1... | collective-permute-start | bytes 884744 | tf_op jit(solution)/shard_map/ppermute | solution.py:264
  11.9 10.0 %collective-permute-start = (f32[8,64,128]{2,1,0:T(8,128)}, f32[8,64,128]{2,1,0:T(8,128)S(1)}, u32[]{:S(2)}, u32[]{:S(2)}) collective-permute-start(f32[8,64,128]{2,1,0:T(8,128)} %get-tuple-element.9), channel_id=1, source_target_pairs={{0,1},{1,2},{2,3},{3,4},{4,5},{5,6},{6,7},{7,8},{8,9},{9,10},{10,1... | collective-permute-start | bytes 786440 | tf_op jit(solution)/shard_map/ppermute | solution.py:263
  21.9 0.0 copy-start.10
  21.9 0.7 copy-done.10
  22.6 0.1 copy.13.obs
  22.7 0.1 pad_add_fusion.where
  22.7 11.9 %collective-permute-done.low = f32[8,64,128]{2,1,0:T(8,128)S(1)} collective-permute-done((f32[8,64,128]{2,1,0:T(8,128)}, f32[8,64,128]{2,1,0:T(8,128)S(1)}, u32[]{:S(2)}, u32[]{:S(2)}) %collective-permute-start) | collective-permute-done | bytes 262176 | tf_op jit(solution)/shard_map/ppermute | solution.py:263
  34.7 0.0 collective-permute-done.1.high
  34.7 0.0 copy-done
  34.7 0.0 copy-done.1
  34.7 0.0 copy-done.2
  34.7 0.0 copy-done.3
  34.7 0.0 copy-done.4
  34.7 0.0 copy-done.5
  34.8 0.0 copy-done.8
  34.8 0.0 copy-done.9
  34.8 0.6 copy-done.7
  35.4 3.3 %transport.1 = (f32[8,64,128]{2,1,0:T(8,128)}, f32[32,8,128]{2,1,0:T(8,128)S(1)}) custom-call(f32[8,64,128]{2,1,0:T(8,128)S(1)} %bitcast.15, f32[8,64,128]{2,1,0:T(8,128)S(1)} %bitcast.17, f32[8,64,128]{2,1,0:T(8,128)S(1)} %bitcast.19, f32[8,64,128]{2,1,0:T(8,128)S(1)} %bitcast.21, f32[8,64,128]{2,1,0:T(8,128)S(1)} %bitcast.23, f32[8,64,128]{2,1,0:T(8,128)S(1)} %bitcast.25, ...), custom_call_target="tpu_custom_call" | custom-call | tf_op jit(solution)/shard_map/transport/pallas_call | solution.py:267
  38.7 35.4 %all_to_all.10.parts = f32[32,8,128]{2,1,0:T(8,128)} all-to-all(f32[32,8,128]{2,1,0:T(8,128)S(1)} %get-tuple-element.12), channel_id=1, replica_groups=mesh['x'=4,'zl'=8,'y'=4,'zh'=2,'c'=2] {'zl','zh','c'}, dimensions={0} | all-to-all | bytes 262144 | tf_op jit(solution)/shard_map/all_to_all | solution.py:288
  74.0 1.6 %line_sums.1 = f32[16,32,128]{2,1,0:T(8,128)} custom-call(f32[32,8,128]{2,1,0:T(8,128)} %all_to_all.10.parts), custom_call_target="tpu_custom_call" | custom-call | tf_op jit(solution)/shard_map/line_sums/pallas_call | solution.py:289
  75.7 17.1 %all_to_all.11.parts = f32[16,32,128]{2,1,0:T(8,128)} all-to-all(f32[16,32,128]{2,1,0:T(8,128)} %line_sums.1), channel_id=1, replica_groups=mesh['x'=4,'zl'=8,'y'=4,'zh'=2,'c'=2] {'x','y'}, dimensions={0} | all-to-all | bytes 524288 | tf_op jit(solution)/shard_map/all_to_all | solution.py:297
  92.7 1.8 %gram_row.1 = (f32[3,1,8]{2,1,0:T(1,128)}, f32[1,32]{1,0:T(1,128)}) custom-call(f32[16,32,128]{2,1,0:T(8,128)} %all_to_all.11.parts, s32[4]{0:T(128)} %copy-done.6), custom_call_target="tpu_custom_call" | custom-call | tf_op jit(solution)/shard_map/gram_row/pallas_call | solution.py:298
  (10 shorter events, 0.0 us)
Async XLA Ops:
  0.6 34.1 %copy-start = (f32[1,8,64,128]{3,2,1,0:T(8,128)S(1)}, f32[1,8,64,128]{3,2,1,0:T(8,128)}, u32[]{:S(2)}) copy-start(f32[1,8,64,128]{3,2,1,0:T(8,128)} %param.10) | copy-start | bytes 786436
  0.6 34.1 %copy-start.1 = (f32[1,8,64,128]{3,2,1,0:T(8,128)S(1)}, f32[1,8,64,128]{3,2,1,0:T(8,128)}, u32[]{:S(2)}) copy-start(f32[1,8,64,128]{3,2,1,0:T(8,128)} %param.11) | copy-start | bytes 786436
  0.7 34.1 %copy-start.2 = (f32[1,8,64,128]{3,2,1,0:T(8,128)S(1)}, f32[1,8,64,128]{3,2,1,0:T(8,128)}, u32[]{:S(2)}) copy-start(f32[1,8,64,128]{3,2,1,0:T(8,128)} %param.12) | copy-start | bytes 786436
  0.7 34.1 %copy-start.3 = (f32[1,8,64,128]{3,2,1,0:T(8,128)S(1)}, f32[1,8,64,128]{3,2,1,0:T(8,128)}, u32[]{:S(2)}) copy-start(f32[1,8,64,128]{3,2,1,0:T(8,128)} %param.13) | copy-start | bytes 786436
  0.7 34.1 %copy-start.4 = (f32[1,8,64,128]{3,2,1,0:T(8,128)S(1)}, f32[1,8,64,128]{3,2,1,0:T(8,128)}, u32[]{:S(2)}) copy-start(f32[1,8,64,128]{3,2,1,0:T(8,128)} %param.14) | copy-start | bytes 786436
  0.7 34.1 %copy-start.5 = (f32[1,8,64,128]{3,2,1,0:T(8,128)S(1)}, f32[1,8,64,128]{3,2,1,0:T(8,128)}, u32[]{:S(2)}) copy-start(f32[1,8,64,128]{3,2,1,0:T(8,128)} %param.15) | copy-start | bytes 786436
  3.1 31.6 %collective-permute-start.1 = (f32[9,64,128]{2,1,0:T(8,128)}, f32[9,64,128]{2,1,0:T(8,128)S(1)}, u32[]{:S(2)}, u32[]{:S(2)}) collective-permute-start(f32[9,64,128]{2,1,0:T(8,128)} %get-tuple-element.10), channel_id=1, source_target_pairs={{1,0},{2,1},{3,2},{4,3},{5,4},{6,5},{7,6},{8,7},{9,8},{10,9},{11,1... | collective-permute-start | bytes 884744 | tf_op jit(solution)/shard_map/ppermute | solution.py:264
  11.9 22.8 %collective-permute-start = (f32[8,64,128]{2,1,0:T(8,128)}, f32[8,64,128]{2,1,0:T(8,128)S(1)}, u32[]{:S(2)}, u32[]{:S(2)}) collective-permute-start(f32[8,64,128]{2,1,0:T(8,128)} %get-tuple-element.9), channel_id=1, source_target_pairs={{0,1},{1,2},{2,3},{3,4},{4,5},{5,6},{6,7},{7,8},{8,9},{9,10},{10,1... | collective-permute-start | bytes 786440 | tf_op jit(solution)/shard_map/ppermute | solution.py:263
  21.9 0.7 copy-start.10
  22.7 12.1 %copy-start.8 = (s32[256]{0:T(256)S(1)}, s32[256]{0:T(256)}, u32[]{:S(2)}) copy-start(s32[256]{0:T(256)} %param.17) | copy-start | bytes 3076
  22.7 12.1 %copy-start.9 = (f32[256]{0:T(256)S(1)}, f32[256]{0:T(256)}, u32[]{:S(2)}) copy-start(f32[256]{0:T(256)} %param.18) | copy-start | bytes 3076
  22.7 12.0 %copy-start.6 = (s32[4]{0:T(128)}, s32[4]{0:T(128)S(1)}, u32[]{:S(2)}) copy-start(s32[4]{0:T(128)S(1)} %pad_add_fusion.where) | copy-start | bytes 52
  34.7 0.7 copy-start.7

commit v2 on v1

v2 whole, which is shorter than its diff:
```python
import jax
import jax.numpy as jnp
from jax import lax
from jax.experimental import pallas as pl
from jax.experimental.pallas import tpu as pltpu
from jax.sharding import Mesh
from jax.sharding import PartitionSpec as P

SUBSTEPS = 3
AXES = ("x", "zl", "y", "zh", "c")
SIZES = (4, 8, 4, 2, 2)
MEMBER = ("x", "zl")
TILE = ("y", "zh", "c")
LINE = ("zl", "zh", "c")
PLANE = ("x", "y")
UP_ROWS = 7
DOWN_ROWS = 8
HIGHEST = lax.Precision.HIGHEST


def frac(sat, mob):
    wet = sat * sat
    dry = (1.0 - sat) * (1.0 - sat)
    return wet / (wet + mob * dry)


def inner(flux, axis):
    return jnp.where(lax.broadcasted_iota(jnp.int32, flux.shape, axis) > 0, flux, 0.0)


def across(flux, below, here):
    return flux * jnp.where(flux > 0.0, below, here)


def spread(flow, flux, axis):
    face = across(flux, pltpu.roll(flow, 1, axis), flow)
    return pltpu.roll(face, flow.shape[axis] - 1, axis) - face


def edge_kernel(sat, mob, pore, qx, qy, qz, up, down, s, m, p, x, y, z, made, raw_sem, in_sem, out_sem):
    loads = [
        pltpu.make_async_copy(sat, s, in_sem.at[0]),
        pltpu.make_async_copy(mob, m, in_sem.at[1]),
        pltpu.make_async_copy(qx.at[pl.ds(1, 7)], x.at[pl.ds(1, 7)], in_sem.at[2]),
    ]
    for k, (field, held) in enumerate(((pore, p), (qy, y), (qz, z))):
        for j, row in enumerate((1, 6)):
            loads.append(
                pltpu.make_async_copy(field.at[row], held.at[j], in_sem.at[3 + 2 * k + j])
            )
    for load in loads:
        load.start()
    raws = []
    for row, out, base in ((7, up, 0), (0, down, UP_ROWS)):
        for k, field in enumerate((sat, mob, pore, qz, qy)):
            raws.append(pltpu.make_async_copy(field.at[row], out.at[k], raw_sem.at[base + k]))
    raws.append(pltpu.make_async_copy(qx.at[0], down.at[5], raw_sem.at[5]))
    for raw in raws:
        raw.start()
    for load in loads:
        load.wait()
    f = {i: frac(s[i], m[i]) for i in (0, 1, 2, 5, 6, 7)}

    def face(i):
        return across(x[i], f[i - 1], f[i])

    def advanced(i, j, low, high):
        total = (
            high - low + spread(f[i], inner(z[j], 0), 0) + spread(f[i], inner(y[j], 1), 1)
        )
        return frac(s[i] - p[j] * total, m[i])

    face_1 = face(1)
    face_7 = face(7)
    made[0] = face_7
    made[1] = jnp.maximum(x[7], 0.0) * advanced(6, 1, face(6), face_7)
    up_copy = pltpu.make_async_copy(made.at[pl.ds(0, 2)], up.at[pl.ds(5, 2)], out_sem.at[0])
    up_copy.start()
    made[2] = face_1
    made[3] = jnp.minimum(x[1], 0.0) * advanced(1, 0, face_1, face(2))
    down_copy = pltpu.make_async_copy(made.at[pl.ds(2, 2)], down.at[pl.ds(6, 2)], out_sem.at[1])
    down_copy.start()
    for raw in raws:
        raw.wait()
    up_copy.wait()
    down_copy.wait()


def main_kernel(
    sat, mob, pore, qx, qy, qz, low, high, cell, well, factor, obs, where, new_sat, shares, s, f, outer
):
    tile = where[0]
    last = where[1]
    rows, layers, columns = sat.shape
    cells = rows * layers

    def at(i, own, k):
        if i < 0:
            return low[k]
        if i == rows:
            return high[k]
        return own[i]

    def guarded(i, own, k, missing):
        if i < 0:
            return jnp.where(tile > 0, low[k], missing)
        if i == rows:
            return jnp.where(tile < last, high[k], missing)
        return own[i]

    def mob_at(i):
        return guarded(i, mob, 1, 1.0)

    def qx_at(i):
        if i == 0:
            return jnp.where(tile > 0, qx[0], 0.0)
        if i == rows:
            return high[5]
        return qx[i]

    count = cell.shape[1]
    row_of = cell[...] // columns
    column_of = cell[...] - row_of * columns
    pick_row = (lax.broadcasted_iota(jnp.int32, (cells, count), 0) == row_of).astype(jnp.float32)
    pick_column = lax.broadcasted_iota(jnp.int32, (columns, count), 0) == column_of
    picked = []
    for step in range(SUBSTEPS):
        for i in range(-1, rows + 1):
            if step == 0:
                f[i + 1] = frac(guarded(i, sat, 0, 0.5), mob_at(i))
            elif step == 1 or i in (-1, rows):
                f[i + 1] = frac(s[i + 1], mob_at(i))
            else:
                f[i + 1] = frac(s[i + 1], mob[i])
        if step == 0:
            outer[0] = jnp.minimum(low[5], 0.0) / f[0]
            outer[1] = jnp.maximum(high[6], 0.0) / f[rows + 1]
        if step > 0:
            flows = jnp.concatenate([f[i + 1] for i in range(rows)], axis=0)
            picked.append(pick(flows, pick_row, pick_column))
        first, stop = (0, rows) if step == SUBSTEPS - 1 else (-1, rows + 1)
        if first == 0:
            face = across(qx_at(0), f[0], f[1])
        elif step == 0:
            face = low[5]
        else:
            face = low[6] + outer[0] * f[0]
        for i in range(first, stop):
            if i < rows:
                above = across(qx_at(i + 1), f[i + 1], f[i + 2])
            elif step == 0:
                above = high[6]
            else:
                above = outer[1] * f[i + 1] + high[7]
            flow = f[i + 1]
            total = (
                above
                - face
                + spread(flow, inner(at(i, qz, 3), 0), 0)
                + spread(flow, inner(at(i, qy, 4), 1), 1)
            )
            face = above
            now = guarded(i, sat, 0, 0.5) if step == 0 else s[i + 1]
            moved = now - at(i, pore, 2) * total
            if step < SUBSTEPS - 1:
                s[i + 1] = moved
            else:
                new_sat[i] = moved
                f[i + 1] = frac(moved, mob[i])
    flows = jnp.concatenate([f[i + 1] for i in range(rows)], axis=0)
    picked.append(pick(flows, pick_row, pick_column))
    contrib = jnp.concatenate(picked, axis=0) * factor[...]
    wells = shares.shape[1]
    by_well = (lax.broadcasted_iota(jnp.int32, (wells, count), 0) == well[...]).astype(jnp.float32)
    rates = lax.dot_general(
        contrib, by_well, (((1,), (1,)), ((), ())), precision=HIGHEST,
        preferred_element_type=jnp.float32,
    )
    mine = obs.shape[1]
    errors = jnp.concatenate(
        [obs[k : k + 1, :] for k in range(SUBSTEPS)]
        + [jnp.zeros((1, wells - SUBSTEPS * mine), jnp.float32)],
        axis=1,
    )
    share = jnp.concatenate([rates, errors] * 2, axis=0)
    for j in range(shares.shape[0] // 8):
        shares[8 * j : 8 * j + 8, :] = share


def pick(flows, pick_row, pick_column):
    rows_of = lax.dot_general(
        flows, pick_row, (((0,), (0,)), ((), ())), precision=HIGHEST,
        preferred_element_type=jnp.float32,
    )
    return jnp.sum(jnp.where(pick_column, rows_of, 0.0), axis=0, keepdims=True)


def line_kernel(parts, out):
    members, per = 8, 4
    width = SUBSTEPS + 1
    rows = []
    for k in range(SUBSTEPS):
        total = parts[pl.ds(k, members, stride=per * width), :]
        for j in range(1, per):
            total = total + parts[pl.ds(width * j + k, members, stride=per * width), :]
        rows.append(total)
    errors = [parts[width * j + SUBSTEPS : width * j + SUBSTEPS + 1, :] for j in range(per)]
    rows.append(jnp.concatenate(errors * 2, axis=0))
    for j in range(out.shape[0]):
        for k, row in enumerate(rows):
            out[j, members * k : members * (k + 1), :] = row


def gram_kernel(parts, where, rates_out, gram):
    tile = where[0]
    own_x = where[2]
    own_z = where[3]
    groups, per, layer = 4, 4, 8
    rows = SUBSTEPS * layer
    wells = parts.shape[2]
    mine = rates_out.shape[2]
    sums = []
    for g in range(groups):
        total = parts[g * per, :rows]
        for j in range(1, per):
            total = total + parts[g * per + j, :rows]
        sums.append(total)
    packed = jnp.concatenate([parts[y, rows : rows + per] for y in range(per)], axis=0)
    tiles = packed.shape[0]
    lane = lax.broadcasted_iota(jnp.int32, packed.shape, 1)
    home = lane // mine == lax.broadcasted_iota(jnp.int32, packed.shape, 0)
    errors = []
    for k in range(SUBSTEPS):
        front = packed if k == 0 else pltpu.roll(packed, wells - mine * k, 1)
        moved = pltpu.roll(front, 0, 1, stride=mine, stride_axis=0)
        errors.append(jnp.sum(jnp.where(home, moved, 0.0), axis=0, keepdims=True))
    ensemble = groups * layer
    own = sums[0]
    for g in range(1, groups):
        own = jnp.where(own_x == g, sums[g], own)
    mask_z = lax.broadcasted_iota(jnp.int32, (layer, wells), 0) == own_z
    own_rates = []
    own_centered = []
    centered = []
    for k in range(SUBSTEPS):
        part = slice(k * layer, (k + 1) * layer)
        data = [total[part] / errors[k] for total in sums]
        mean = jnp.sum(data[0] + data[1] + data[2] + data[3], axis=0, keepdims=True) / ensemble
        centered.append(jnp.concatenate([d - mean for d in data], axis=0))
        row = jnp.sum(jnp.where(mask_z, own[part], 0.0), axis=0, keepdims=True)
        own_rates.append(row)
        own_centered.append(row / errors[k] - mean)
    gram[...] = lax.dot_general(
        jnp.concatenate(own_centered, axis=1),
        jnp.concatenate(centered, axis=1),
        (((1,), (1,)), ((), ())),
        precision=HIGHEST,
        preferred_element_type=jnp.float32,
    ) / (ensemble - 1.0)
    select = (
        lax.broadcasted_iota(jnp.int32, (mine, wells), 1)
        == lax.broadcasted_iota(jnp.int32, (mine, wells), 0) + tile * mine
    ).astype(jnp.float32)
    chosen = lax.dot_general(
        jnp.concatenate(own_rates, axis=0), select, (((1,), (1,)), ((), ())), precision=HIGHEST,
        preferred_element_type=jnp.float32,
    )
    for k in range(SUBSTEPS):
        rates_out[k] = chosen[k : k + 1]


VMEM = pl.BlockSpec(memory_space=pltpu.VMEM)
ANY = pl.BlockSpec(memory_space=pl.ANY)
SMEM = pl.BlockSpec(memory_space=pltpu.SMEM)


def shape(*dims):
    return jax.ShapeDtypeStruct(dims, jnp.float32)


def body(
    saturation,
    mobility,
    pore_scale,
    flux_x,
    flux_y,
    flux_z,
    conn_cell,
    conn_well,
    conn_factor,
    obs_error,
):
    rows, layers, columns = saturation.shape[1:]
    fields = [
        a.reshape(rows, layers, columns)
        for a in (saturation, mobility, pore_scale, flux_x, flux_y, flux_z)
    ]
    tiles = lax.axis_size(TILE)
    tile = lax.axis_index(TILE)
    where = jnp.stack(
        [tile, jnp.full_like(tile, tiles - 1), lax.axis_index("x"), lax.axis_index("zl")]
    ).astype(jnp.int32)
    up, down = pl.pallas_call(
        edge_kernel,
        out_shape=(shape(UP_ROWS, layers, columns), shape(DOWN_ROWS, layers, columns)),
        in_specs=[ANY] * 6,
        out_specs=(ANY, ANY),
        scratch_shapes=[pltpu.VMEM((rows, layers, columns), jnp.float32)] * 2
        + [pltpu.VMEM((2, layers, columns), jnp.float32)]
        + [pltpu.VMEM((rows, layers, columns), jnp.float32)]
        + [pltpu.VMEM((2, layers, columns), jnp.float32)] * 2
        + [pltpu.VMEM((4, layers, columns), jnp.float32)]
        + [pltpu.SemaphoreType.DMA((12,)), pltpu.SemaphoreType.DMA((9,)), pltpu.SemaphoreType.DMA((2,))],
        name="edges",
    )(*fields)
    low = lax.ppermute(up, TILE, [(i, i + 1) for i in range(tiles - 1)])
    high = lax.ppermute(down, TILE, [(i + 1, i) for i in range(tiles - 1)])
    wells = obs_error.shape[0] * tiles
    count = conn_cell.shape[0]
    new_saturation, shares = pl.pallas_call(
        main_kernel,
        out_shape=(shape(rows, layers, columns), shape(128, wells)),
        in_specs=[VMEM] * 12 + [SMEM],
        out_specs=(VMEM, VMEM),
        scratch_shapes=[
            pltpu.VMEM((rows + 2, layers, columns), jnp.float32),
            pltpu.VMEM((rows + 2, layers, columns), jnp.float32),
            pltpu.VMEM((2, layers, columns), jnp.float32),
        ],
        compiler_params=pltpu.CompilerParams(vmem_limit_bytes=32 * 1024 * 1024),
        name="transport",
    )(
        *fields,
        low,
        high,
        conn_cell.reshape(1, count),
        conn_well.reshape(1, count),
        conn_factor.reshape(1, count),
        obs_error.T,
        where,
    )
    line = lax.all_to_all(shares.reshape(32, 4, wells), LINE, 0, 0)
    spreads = pl.pallas_call(
        line_kernel,
        out_shape=shape(16, 32, wells),
        in_specs=[VMEM],
        out_specs=VMEM,
        name="line_sums",
    )(line.reshape(128, wells))
    plane = lax.all_to_all(spreads, PLANE, 0, 0)
    rates, gram = pl.pallas_call(
        gram_kernel,
        out_shape=(shape(SUBSTEPS, 1, obs_error.shape[0]), shape(1, 32)),
        in_specs=[VMEM, SMEM],
        out_specs=(VMEM, VMEM),
        name="gram_row",
    )(plane, where)
    return (
        new_saturation.reshape(saturation.shape),
        jnp.transpose(rates, (1, 2, 0)),
        gram,
    )


def solution(mesh):
    split = Mesh(mesh.devices.reshape(SIZES), AXES)
    in_specs = (P(MEMBER, TILE, None, None),) * 6 + (P(TILE),) * 3 + (P(TILE, None),)
    out_specs = (P(MEMBER, TILE, None, None), P(MEMBER, TILE, None), P(MEMBER, None))
    return jax.shard_map(body, mesh=split, in_specs=in_specs, out_specs=out_specs, check_vma=False)
```

time: 94.9 us -> 99.1 us (1.044)
  Pallas kernels: 9.14 us -> 18.4 us
  blocking collectives: 52.4 us -> 43.2 us
  waiting for transfers between devices: 11.9 us -> 16.8 us
    pallas_call x1, Pallas kernels: 2.44 us -> 12.2 us  [body(): pl.pallas_call(edge_kernel, out_shape=(shape(UP_ROWS, layers, columns), s...]
    all_to_all x1, blocking collectives: 35.4 us -> 27.9 us  [body(): line = lax.all_to_all(shares.reshape(32, 4, wells), LINE, 0, 0)]
    ppermute x1, waiting for transfers between devices: 11.9 us -> 16.8 us  [body(): low = lax.ppermute(up, TILE, [(i, i + 1) for i in range(tiles - 1)])]
    all_to_all x1, blocking collectives: 17.1 us -> 15.3 us  [body(): plane = lax.all_to_all(spreads, PLANE, 0, 0)]
where the time goes in v2:
time: 99.1 us; the launch traced here: 98.8 us
  blocking collectives  43.2 us (44%)
  starting transfers between devices  18.8 us (19%)
  Pallas kernels  18.4 us (19%)
  waiting for transfers between devices  16.8 us (17%)
    all_to_all x1, blocking collectives, body(): line = lax.all_to_all(shares.reshape(32, 4, wells), LINE, 0, 0)  27.9 us
    ppermute x1, waiting for transfers between devices, body(): low = lax.ppermute(up, TILE, [(i, i + 1) for i in range(tiles - 1)])  16.8 us
    all_to_all x1, blocking collectives, body(): plane = lax.all_to_all(spreads, PLANE, 0, 0)  15.3 us
    pallas_call x1, Pallas kernels, body(): pl.pallas_call(edge_kernel, out_shape=(shape(UP_ROWS, layers, columns), s...  12.2 us
    ppermute x1, starting transfers between devices, body(): low = lax.ppermute(up, TILE, [(i, i + 1) for i in range(tiles - 1)])  9.97 us
    ppermute x1, starting transfers between devices, body(): high = lax.ppermute(down, TILE, [(i + 1, i) for i in range(tiles - 1)])  8.79 us
    pallas_call x1, Pallas kernels, body(): pl.pallas_call(main_kernel, out_shape=(shape(rows, layers, columns), shap...  2.72 us
  transfers between devices with their start and end apart: 2, of which 1 were waited for; matrix products, arithmetic and copies ran while one was open for 0% of the time, Pallas kernels for 0%

profile of v2, /device:TPU:1, one launch (start us, length us, event | category | flops | bytes accessed | tf_op | source)
XLA Modules:
  0.0 98.8 jit_solution(7158345810708964096)
XLA Ops:
  0.6 0.0 copy-start
  0.6 0.0 copy-start.1
  0.7 0.0 copy-start.2
  0.7 0.0 copy-start.3
  0.7 0.0 copy-start.4
  0.7 0.0 copy-start.5
  0.7 12.2 %edges.1 = (f32[7,64,128]{2,1,0:T(8,128)}, f32[8,64,128]{2,1,0:T(8,128)}) custom-call(f32[8,64,128]{2,1,0:T(8,128)} %bitcast.17, f32[8,64,128]{2,1,0:T(8,128)} %bitcast.19, f32[8,64,128]{2,1,0:T(8,128)} %bitcast.21, f32[8,64,128]{2,1,0:T(8,128)} %bitcast.23, f32[8,64,128]{2,1,0:T(8,128)} %bitcast.25, f32[8,64,128]{2,1,0:T(8,128)} %bitcast.27), custom_call_target="tpu_custom_call" | custom-call | tf_op jit(solution)/shard_map/edges/pallas_call | solution.py:303
  12.9 8.8 %collective-permute-start.1 = (f32[8,64,128]{2,1,0:T(8,128)}, f32[8,64,128]{2,1,0:T(8,128)S(1)}, u32[]{:S(2)}, u32[]{:S(2)}) collective-permute-start(f32[8,64,128]{2,1,0:T(8,128)} %get-tuple-element.10), channel_id=1, source_target_pairs={{1,0},{2,1},{3,2},{4,3},{5,4},{6,5},{7,6},{8,7},{9,8},{10,9},{11,1... | collective-permute-start | bytes 786440 | tf_op jit(solution)/shard_map/ppermute | solution.py:317
  21.7 10.0 %collective-permute-start = (f32[7,64,128]{2,1,0:T(8,128)}, f32[7,64,128]{2,1,0:T(8,128)S(1)}, u32[]{:S(2)}, u32[]{:S(2)}) collective-permute-start(f32[7,64,128]{2,1,0:T(8,128)} %get-tuple-element.9), channel_id=1, source_target_pairs={{0,1},{1,2},{2,3},{3,4},{4,5},{5,6},{6,7},{7,8},{8,9},{9,10},{10,1... | collective-permute-start | bytes 688136 | tf_op jit(solution)/shard_map/ppermute | solution.py:316
  31.7 0.0 copy-start.9
  31.7 0.0 copy-start.10
  31.7 0.1 pad_add_fusion.where
  31.8 16.8 %collective-permute-done.low = f32[7,64,128]{2,1,0:T(8,128)S(1)} collective-permute-done((f32[7,64,128]{2,1,0:T(8,128)}, f32[7,64,128]{2,1,0:T(8,128)S(1)}, u32[]{:S(2)}, u32[]{:S(2)}) %collective-permute-start) | collective-permute-done | bytes 229408 | tf_op jit(solution)/shard_map/ppermute | solution.py:316
  48.7 0.0 collective-permute-done.1.high
  48.7 0.0 copy-done.6
  48.7 0.0 copy-done
  48.7 0.0 copy-done.1
  48.8 0.6 copy-done.7
  49.3 0.0 copy-done.8
  49.4 2.7 %transport.1 = (f32[8,64,128]{2,1,0:T(8,128)}, f32[128,128]{1,0:T(8,128)S(1)}) custom-call(f32[8,64,128]{2,1,0:T(8,128)S(1)} %bitcast.18, f32[8,64,128]{2,1,0:T(8,128)S(1)} %bitcast.20, f32[8,64,128]{2,1,0:T(8,128)S(1)} %bitcast.22, f32[8,64,128]{2,1,0:T(8,128)S(1)} %bitcast.24, f32[8,64,128]{2,1,0:T(8,128)S(1)} %bitcast.26, f32[8,64,128]{2,1,0:T(8,128)S(1)} %bitcast.28, ...), custom_call_target="tpu_custom_call" | custom-call | tf_op jit(solution)/shard_map/transport/pallas_call | solution.py:320
  52.1 27.9 %all_to_all.10 = f32[32,4,128]{2,1,0:T(4,128)} all-to-all(f32[32,4,128]{2,1,0:T(4,128)S(1)} %bitcast.29), channel_id=1, replica_groups=mesh['x'=4,'zl'=8,'y'=4,'zh'=2,'c'=2] {'zl','zh','c'}, dimensions={0} | all-to-all | bytes 131072 | tf_op jit(solution)/shard_map/all_to_all | solution.py:342
  80.0 1.6 %line_sums.1 = f32[16,32,128]{2,1,0:T(8,128)} custom-call(f32[128,128]{1,0:T(8,128)} %bitcast.34), custom_call_target="tpu_custom_call" | custom-call | tf_op jit(solution)/shard_map/line_sums/pallas_call | solution.py:343
  81.6 15.3 %all_to_all.11.parts = f32[16,32,128]{2,1,0:T(8,128)} all-to-all(f32[16,32,128]{2,1,0:T(8,128)} %line_sums.1), channel_id=1, replica_groups=mesh['x'=4,'zl'=8,'y'=4,'zh'=2,'c'=2] {'x','y'}, dimensions={0} | all-to-all | bytes 524288 | tf_op jit(solution)/shard_map/all_to_all | solution.py:350
  96.9 1.9 %gram_row.1 = (f32[3,1,8]{2,1,0:T(1,128)}, f32[1,32]{1,0:T(1,128)}) custom-call(f32[16,32,128]{2,1,0:T(8,128)} %all_to_all.11.parts, s32[4]{0:T(128)} %copy-done.6), custom_call_target="tpu_custom_call" | custom-call | tf_op jit(solution)/shard_map/gram_row/pallas_call | solution.py:351
  (9 shorter events, 0.0 us)
Async XLA Ops:
  0.6 48.0 %copy-start = (f32[1,8,64,128]{3,2,1,0:T(8,128)S(1)}, f32[1,8,64,128]{3,2,1,0:T(8,128)}, u32[]{:S(2)}) copy-start(f32[1,8,64,128]{3,2,1,0:T(8,128)} %param.10) | copy-start | bytes 786436
  0.6 48.0 %copy-start.1 = (f32[1,8,64,128]{3,2,1,0:T(8,128)S(1)}, f32[1,8,64,128]{3,2,1,0:T(8,128)}, u32[]{:S(2)}) copy-start(f32[1,8,64,128]{3,2,1,0:T(8,128)} %param.11) | copy-start | bytes 786436
  0.7 48.0 %copy-start.2 = (f32[1,8,64,128]{3,2,1,0:T(8,128)S(1)}, f32[1,8,64,128]{3,2,1,0:T(8,128)}, u32[]{:S(2)}) copy-start(f32[1,8,64,128]{3,2,1,0:T(8,128)} %param.12) | copy-start | bytes 786436
  0.7 48.0 %copy-start.3 = (f32[1,8,64,128]{3,2,1,0:T(8,128)S(1)}, f32[1,8,64,128]{3,2,1,0:T(8,128)}, u32[]{:S(2)}) copy-start(f32[1,8,64,128]{3,2,1,0:T(8,128)} %param.13) | copy-start | bytes 786436
  0.7 48.0 %copy-start.4 = (f32[1,8,64,128]{3,2,1,0:T(8,128)S(1)}, f32[1,8,64,128]{3,2,1,0:T(8,128)}, u32[]{:S(2)}) copy-start(f32[1,8,64,128]{3,2,1,0:T(8,128)} %param.14) | copy-start | bytes 786436
  0.7 48.0 %copy-start.5 = (f32[1,8,64,128]{3,2,1,0:T(8,128)S(1)}, f32[1,8,64,128]{3,2,1,0:T(8,128)}, u32[]{:S(2)}) copy-start(f32[1,8,64,128]{3,2,1,0:T(8,128)} %param.15) | copy-start | bytes 786436
  12.9 35.7 %collective-permute-start.1 = (f32[8,64,128]{2,1,0:T(8,128)}, f32[8,64,128]{2,1,0:T(8,128)S(1)}, u32[]{:S(2)}, u32[]{:S(2)}) collective-permute-start(f32[8,64,128]{2,1,0:T(8,128)} %get-tuple-element.10), channel_id=1, source_target_pairs={{1,0},{2,1},{3,2},{4,3},{5,4},{6,5},{7,6},{8,7},{9,8},{10,9},{11,1... | collective-permute-start | bytes 786440 | tf_op jit(solution)/shard_map/ppermute | solution.py:317
  21.7 26.9 %collective-permute-start = (f32[7,64,128]{2,1,0:T(8,128)}, f32[7,64,128]{2,1,0:T(8,128)S(1)}, u32[]{:S(2)}, u32[]{:S(2)}) collective-permute-start(f32[7,64,128]{2,1,0:T(8,128)} %get-tuple-element.9), channel_id=1, source_target_pairs={{0,1},{1,2},{2,3},{3,4},{4,5},{5,6},{6,7},{7,8},{8,9},{9,10},{10,1... | collective-permute-start | bytes 688136 | tf_op jit(solution)/shard_map/ppermute | solution.py:316
  31.7 17.0 %copy-start.9 = (s32[256]{0:T(256)S(1)}, s32[256]{0:T(256)}, u32[]{:S(2)}) copy-start(s32[256]{0:T(256)} %param.17) | copy-start | bytes 3076
  31.7 17.0 %copy-start.10 = (f32[256]{0:T(256)S(1)}, f32[256]{0:T(256)}, u32[]{:S(2)}) copy-start(f32[256]{0:T(256)} %param.18) | copy-start | bytes 3076
  31.8 16.9 %copy-start.6 = (s32[4]{0:T(128)}, s32[4]{0:T(128)S(1)}, u32[]{:S(2)}) copy-start(s32[4]{0:T(128)S(1)} %pad_add_fusion.where) | copy-start | bytes 52
  48.7 0.7 copy-start.7
  48.7 0.7 copy-start.8

commit v3 on v2

v3 whole, which is shorter than its diff:
```python
import jax
import jax.numpy as jnp
from jax import lax
from jax.experimental import pallas as pl
from jax.experimental.pallas import tpu as pltpu
from jax.sharding import Mesh
from jax.sharding import PartitionSpec as P

SUBSTEPS = 3
AXES = ("x", "zl", "y", "zh", "c")
SIZES = (4, 8, 4, 2, 2)
MEMBER = ("x", "zl")
TILE = ("y", "zh", "c")
LINE = ("zl", "zh", "c")
PLANE = ("x", "y")
UP_ROWS = 7
DOWN_ROWS = 8
HIGHEST = lax.Precision.HIGHEST


def frac(sat, mob):
    wet = sat * sat
    dry = (1.0 - sat) * (1.0 - sat)
    return wet / (wet + mob * dry)


def inner(flux, axis):
    return jnp.where(lax.broadcasted_iota(jnp.int32, flux.shape, axis) > 0, flux, 0.0)


def across(flux, below, here):
    return flux * jnp.where(flux > 0.0, below, here)


def spread(flow, flux, axis):
    face = across(flux, pltpu.roll(flow, 1, axis), flow)
    return pltpu.roll(face, flow.shape[axis] - 1, axis) - face


def moved(sat, pore, net, flow, flux_z, flux_y):
    return sat - pore * (
        net + spread(flow, inner(flux_z, 0), 0) + spread(flow, inner(flux_y, 1), 1)
    )


def edge_kernel(sat, mob, pore, qx, qy, qz, up, down, s, m, p, x, y, z, made, in_sem, out_sem):
    loads = []
    for k, (field, held) in enumerate(((sat, s), (mob, m), (qx, x), (pore, p), (qy, y), (qz, z))):
        for j, start in enumerate((0, 5)):
            part = pl.ds(start, 3)
            loads.append(
                pltpu.make_async_copy(field.at[part], held.at[part], in_sem.at[2 * k + j])
            )
    for load in loads:
        load.start()
    for load in loads:
        load.wait()

    f = [frac(s[i], m[i]) for i in range(3)]
    face_1 = across(x[1], f[0], f[1])
    flow_1 = frac(moved(s[1], p[1], across(x[2], f[1], f[2]) - face_1, f[1], z[1], y[1]), m[1])
    for k, held in enumerate((s, m, p, z, y, x)):
        made[k] = held[0]
    made[6] = face_1
    made[7] = jnp.minimum(x[1], 0.0) * flow_1
    down_copy = pltpu.make_async_copy(made.at[pl.ds(0, DOWN_ROWS)], down, out_sem.at[0])
    down_copy.start()

    f = {i: frac(s[i], m[i]) for i in range(5, 8)}
    face_7 = across(x[7], f[6], f[7])
    flow_6 = frac(moved(s[6], p[6], face_7 - across(x[6], f[5], f[6]), f[6], z[6], y[6]), m[6])
    for k, held in enumerate((s, m, p, z, y)):
        made[DOWN_ROWS + k] = held[7]
    made[DOWN_ROWS + 5] = face_7
    made[DOWN_ROWS + 6] = jnp.maximum(x[7], 0.0) * flow_6
    up_copy = pltpu.make_async_copy(made.at[pl.ds(DOWN_ROWS, UP_ROWS)], up, out_sem.at[1])
    up_copy.start()
    down_copy.wait()
    up_copy.wait()


OUTER = ((0, 7), (1, 6), (2, 5))
INNER = ((3, 4), (2, 5), (1, 6))


def one_hot(row_of, pairs, layers):
    lane = lax.broadcasted_iota(jnp.int32, row_of.shape, 1)
    hots = []
    for first, second in pairs:
        target = jnp.where(lane < layers, lane + first * layers, lane + (second - 1) * layers)
        hots.append(jnp.where(row_of == target, 1.0, 0.0).astype(jnp.bfloat16))
    return jnp.concatenate(hots, axis=1)


def rates_of(flows, hot, mask, weight):
    stack = jnp.concatenate(flows, axis=0)
    big = stack.astype(jnp.bfloat16)
    rest = stack - big.astype(jnp.float32)
    middle = rest.astype(jnp.bfloat16)
    small = (rest - middle.astype(jnp.float32)).astype(jnp.bfloat16)
    found = mask * sum(
        jnp.dot(hot[:, : stack.shape[0]], part, preferred_element_type=jnp.float32)
        for part in (small, middle, big)
    )
    picked = jnp.sum(found, axis=1, keepdims=True)
    return jnp.sum(weight * picked, axis=0, keepdims=True)


def inside_kernel(
    sat, mob, pore, qx, qy, qz, cell, well, factor, obs, after, mids, middle, early, hot, mask, weight
):
    rows, layers, columns = sat.shape
    count = cell.shape[1]

    def column_of(row):
        return jnp.concatenate(
            [
                jnp.transpose(jnp.broadcast_to(row[:, j : j + columns], (columns, columns)))
                for j in range(0, count, columns)
            ],
            axis=0,
        )

    cells = column_of(cell[...])
    row_of = lax.div(cells, columns)
    lane = lax.broadcasted_iota(jnp.int32, cells.shape, 1)
    mask[...] = jnp.where(cells - row_of * columns == lane, 1.0, 0.0)
    hot[...] = one_hot(row_of, OUTER, layers)
    near = one_hot(row_of, INNER, layers)
    weight[...] = jnp.where(column_of(well[...]) == lane, column_of(factor[...]), 0.0)

    f = [frac(sat[i], mob[i]) for i in range(rows)]
    face = {i: across(qx[i], f[i - 1], f[i]) for i in range(1, rows)}
    mids[0] = f[0]
    mids[1] = f[7]
    mids[2] = moved(sat[0], pore[0], face[1], f[0], qz[0], qy[0])
    mids[3] = moved(sat[7], pore[7], -face[7], f[7], qz[7], qy[7])
    s = {i: moved(sat[i], pore[i], face[i + 1] - face[i], f[i], qz[i], qy[i]) for i in range(1, 7)}
    f = {i: frac(s[i], mob[i]) for i in range(1, 7)}
    rates = [rates_of([f[i] for pair in INNER for i in pair], near, mask[...], weight[...])]
    face = {i: across(qx[i], f[i - 1], f[i]) for i in range(2, 7)}
    mids[4] = f[1]
    mids[5] = f[6]
    mids[6] = moved(s[1], pore[1], face[2], f[1], qz[1], qy[1])
    mids[7] = moved(s[6], pore[6], -face[6], f[6], qz[6], qy[6])
    s = {i: moved(s[i], pore[i], face[i + 1] - face[i], f[i], qz[i], qy[i]) for i in range(2, 6)}
    f = {i: frac(s[i], mob[i]) for i in range(2, 6)}
    rates.append(rates_of([f[i] for pair in INNER[:2] for i in pair], near, mask[...], weight[...]))
    face = {i: across(qx[i], f[i - 1], f[i]) for i in range(3, 6)}
    mids[8] = f[2]
    mids[9] = f[5]
    mids[10] = moved(s[2], pore[2], face[3], f[2], qz[2], qy[2])
    mids[11] = moved(s[5], pore[5], -face[5], f[5], qz[5], qy[5])
    last = [moved(s[i], pore[i], face[i + 1] - face[i], f[i], qz[i], qy[i]) for i in (3, 4)]
    for j in range(2):
        middle[j] = last[j]
    flows = [frac(last[j], mob[3 + j]) for j in range(2)]
    rates.append(rates_of(flows, near, mask[...], weight[...]))
    errors = jnp.concatenate(
        [obs[k : k + 1, :] for k in range(SUBSTEPS)]
        + [jnp.zeros((1, columns - SUBSTEPS * obs.shape[1]), jnp.float32)],
        axis=1,
    )
    early[...] = jnp.concatenate(rates + [errors], axis=0)


def outside_kernel(
    mob, pore, qx, qy, qz, low, high, mids, middle, early, hot, mask, weight, where, new_sat, shares
):
    tile = where[0]
    last = where[1]
    has_low = tile > 0
    has_high = tile < last
    below = jnp.where(has_low, low[0], 0.5)
    below_mob = jnp.where(has_low, low[1], 1.0)
    above = jnp.where(has_high, high[0], 0.5)
    above_mob = jnp.where(has_high, high[1], 1.0)
    x = {i: qx[i] for i in range(1, 8)}
    x[0] = jnp.where(has_low, qx[0], 0.0)
    x[8] = high[5]
    z = {i: qz[i] for i in (0, 1, 6, 7)}
    z[-1], z[8] = low[3], high[3]
    y = {i: qy[i] for i in (0, 1, 6, 7)}
    y[-1], y[8] = low[4], high[4]
    p = {i: pore[i] for i in (0, 1, 2, 5, 6, 7)}
    p[-1], p[8] = low[2], high[2]
    m = {i: mob[i] for i in (0, 1, 2, 5, 6, 7)}
    m[-1], m[8] = below_mob, above_mob

    f = {-1: frac(below, below_mob), 0: mids[0], 7: mids[1], 8: frac(above, above_mob)}
    out_low = jnp.minimum(low[5], 0.0) / f[-1]
    out_high = jnp.maximum(high[6], 0.0) / f[8]
    face = {i: across(x[i], f[i - 1], f[i]) for i in (0, 8)}
    s = {
        -1: moved(below, p[-1], face[0] - low[5], f[-1], z[-1], y[-1]),
        0: mids[2] + p[0] * face[0],
        7: mids[3] - p[7] * face[8],
        8: moved(above, p[8], high[6] - face[8], f[8], z[8], y[8]),
    }

    f = {i: frac(s[i], m[i]) for i in (-1, 0, 7, 8)}
    rates = [rates_of([f[0], f[7]], hot, mask[...], weight[...])]
    f[1], f[6] = mids[4], mids[5]
    face = {i: across(x[i], f[i - 1], f[i]) for i in (0, 1, 7, 8)}
    face[-1] = low[6] + out_low * f[-1]
    face[9] = out_high * f[8] + high[7]
    s = {i: moved(s[i], p[i], face[i + 1] - face[i], f[i], z[i], y[i]) for i in (-1, 0, 7, 8)}
    s[1] = mids[6] + p[1] * face[1]
    s[6] = mids[7] - p[6] * face[7]

    f = {i: frac(s[i], m[i]) for i in (-1, 0, 1, 6, 7, 8)}
    rates.append(rates_of([f[0], f[7], f[1], f[6]], hot, mask[...], weight[...]))
    f[2], f[5] = mids[8], mids[9]
    face = {i: across(x[i], f[i - 1], f[i]) for i in (0, 1, 2, 6, 7, 8)}
    s = {i: moved(s[i], p[i], face[i + 1] - face[i], f[i], z[i], y[i]) for i in (0, 1, 6, 7)}
    s[2] = mids[10] + p[2] * face[2]
    s[5] = mids[11] - p[5] * face[6]
    for i in (0, 1, 2, 5, 6, 7):
        new_sat[i] = s[i]
    for j in range(2):
        new_sat[3 + j] = middle[j]
    f = {i: frac(s[i], m[i]) for i in (0, 1, 2, 5, 6, 7)}
    rates.append(
        rates_of([f[i] for pair in OUTER for i in pair], hot, mask[...], weight[...])
    )
    zero = jnp.zeros_like(rates[0])
    share = early[...] + jnp.concatenate(rates + [zero], axis=0)
    share = jnp.concatenate([share, share], axis=0)
    for j in range(shares.shape[0] // 8):
        shares[8 * j : 8 * j + 8, :] = share


def line_kernel(parts, out):
    members, per = 8, 4
    width = SUBSTEPS + 1
    rows = []
    for k in range(SUBSTEPS):
        total = parts[pl.ds(k, members, stride=per * width), :]
        for j in range(1, per):
            total = total + parts[pl.ds(width * j + k, members, stride=per * width), :]
        rows.append(total)
    errors = [parts[width * j + SUBSTEPS : width * j + SUBSTEPS + 1, :] for j in range(per)]
    rows.append(jnp.concatenate(errors * 2, axis=0))
    for j in range(out.shape[0]):
        for k, row in enumerate(rows):
            out[j, members * k : members * (k + 1), :] = row


def gram_kernel(parts, where, rates_out, gram):
    tile = where[0]
    own_x = where[2]
    own_z = where[3]
    groups, per, layer = 4, 4, 8
    rows = SUBSTEPS * layer
    wells = parts.shape[2]
    mine = rates_out.shape[2]
    sums = []
    for g in range(groups):
        total = parts[g * per, :rows]
        for j in range(1, per):
            total = total + parts[g * per + j, :rows]
        sums.append(total)
    packed = jnp.concatenate([parts[y, rows : rows + per] for y in range(per)], axis=0)
    tiles = packed.shape[0]
    lane = lax.broadcasted_iota(jnp.int32, packed.shape, 1)
    home = lane // mine == lax.broadcasted_iota(jnp.int32, packed.shape, 0)
    errors = []
    for k in range(SUBSTEPS):
        front = packed if k == 0 else pltpu.roll(packed, wells - mine * k, 1)
        moved = pltpu.roll(front, 0, 1, stride=mine, stride_axis=0)
        errors.append(jnp.sum(jnp.where(home, moved, 0.0), axis=0, keepdims=True))
    ensemble = groups * layer
    own = sums[0]
    for g in range(1, groups):
        own = jnp.where(own_x == g, sums[g], own)
    mask_z = lax.broadcasted_iota(jnp.int32, (layer, wells), 0) == own_z
    own_rates = []
    own_centered = []
    centered = []
    for k in range(SUBSTEPS):
        part = slice(k * layer, (k + 1) * layer)
        data = [total[part] / errors[k] for total in sums]
        mean = jnp.sum(data[0] + data[1] + data[2] + data[3], axis=0, keepdims=True) / ensemble
        centered.append(jnp.concatenate([d - mean for d in data], axis=0))
        row = jnp.sum(jnp.where(mask_z, own[part], 0.0), axis=0, keepdims=True)
        own_rates.append(row)
        own_centered.append(row / errors[k] - mean)
    gram[...] = lax.dot_general(
        jnp.concatenate(own_centered, axis=1),
        jnp.concatenate(centered, axis=1),
        (((1,), (1,)), ((), ())),
        precision=HIGHEST,
        preferred_element_type=jnp.float32,
    ) / (ensemble - 1.0)
    select = (
        lax.broadcasted_iota(jnp.int32, (mine, wells), 1)
        == lax.broadcasted_iota(jnp.int32, (mine, wells), 0) + tile * mine
    ).astype(jnp.float32)
    chosen = lax.dot_general(
        jnp.concatenate(own_rates, axis=0), select, (((1,), (1,)), ((), ())), precision=HIGHEST,
        preferred_element_type=jnp.float32,
    )
    for k in range(SUBSTEPS):
        rates_out[k] = chosen[k : k + 1]


VMEM = pl.BlockSpec(memory_space=pltpu.VMEM)
ANY = pl.BlockSpec(memory_space=pl.ANY)
SMEM = pl.BlockSpec(memory_space=pltpu.SMEM)


def shape(*dims):
    return jax.ShapeDtypeStruct(dims, jnp.float32)


def body(
    saturation,
    mobility,
    pore_scale,
    flux_x,
    flux_y,
    flux_z,
    conn_cell,
    conn_well,
    conn_factor,
    obs_error,
):
    rows, layers, columns = saturation.shape[1:]
    fields = [
        a.reshape(rows, layers, columns)
        for a in (saturation, mobility, pore_scale, flux_x, flux_y, flux_z)
    ]
    tiles = lax.axis_size(TILE)
    tile = lax.axis_index(TILE)
    where = jnp.stack(
        [tile, jnp.full_like(tile, tiles - 1), lax.axis_index("x"), lax.axis_index("zl")]
    ).astype(jnp.int32)
    up, down = pl.pallas_call(
        edge_kernel,
        out_shape=(shape(UP_ROWS, layers, columns), shape(DOWN_ROWS, layers, columns)),
        in_specs=[ANY] * 6,
        out_specs=(ANY, ANY),
        scratch_shapes=[pltpu.VMEM((rows, layers, columns), jnp.float32)] * 6
        + [pltpu.VMEM((UP_ROWS + DOWN_ROWS, layers, columns), jnp.float32)]
        + [pltpu.SemaphoreType.DMA((12,)), pltpu.SemaphoreType.DMA((2,))],
        name="edges",
    )(*fields)
    low = lax.ppermute(up, TILE, [(i, i + 1) for i in range(tiles - 1)])
    high = lax.ppermute(down, TILE, [(i + 1, i) for i in range(tiles - 1)])
    wells = obs_error.shape[0] * tiles
    count = conn_cell.shape[0]
    sat, mob, pore, qx, qy, qz = fields
    mids, middle, early, hot, mask, weight = pl.pallas_call(
        inside_kernel,
        out_shape=(
            shape(12, layers, columns),
            shape(2, layers, columns),
            shape(SUBSTEPS + 1, wells),
            jax.ShapeDtypeStruct((count, 6 * layers), jnp.bfloat16),
            shape(count, columns),
            shape(count, wells),
        ),
        in_specs=[VMEM] * 10 + [ANY],
        out_specs=(VMEM,) * 6,
        compiler_params=pltpu.CompilerParams(vmem_limit_bytes=32 * 1024 * 1024),
        name="inside",
    )(
        *fields,
        conn_cell.reshape(1, count),
        conn_well.reshape(1, count),
        conn_factor.reshape(1, count),
        obs_error.T,
        up,
    )
    new_saturation, shares = pl.pallas_call(
        outside_kernel,
        out_shape=(shape(rows, layers, columns), shape(128, wells)),
        in_specs=[VMEM] * 13 + [SMEM],
        out_specs=(VMEM, VMEM),
        compiler_params=pltpu.CompilerParams(vmem_limit_bytes=32 * 1024 * 1024),
        name="outside",
    )(mob, pore, qx, qy, qz, low, high, mids, middle, early, hot, mask, weight, where)
    line = lax.all_to_all(shares.reshape(32, 4, wells), LINE, 0, 0)
    spreads = pl.pallas_call(
        line_kernel,
        out_shape=shape(16, 32, wells),
        in_specs=[VMEM],
        out_specs=VMEM,
        name="line_sums",
    )(line.reshape(128, wells))
    plane = lax.all_to_all(spreads, PLANE, 0, 0)
    rates, gram = pl.pallas_call(
        gram_kernel,
        out_shape=(shape(SUBSTEPS, 1, obs_error.shape[0]), shape(1, 32)),
        in_specs=[VMEM, SMEM],
        out_specs=(VMEM, VMEM),
        name="gram_row",
    )(plane, where)
    return (
        new_saturation.reshape(saturation.shape),
        jnp.transpose(rates, (1, 2, 0)),
        gram,
    )


def solution(mesh):
    split = Mesh(mesh.devices.reshape(SIZES), AXES)
    in_specs = (P(MEMBER, TILE, None, None),) * 6 + (P(TILE),) * 3 + (P(TILE, None),)
    out_specs = (P(MEMBER, TILE, None, None), P(MEMBER, TILE, None), P(MEMBER, None))
    return jax.shard_map(body, mesh=split, in_specs=in_specs, out_specs=out_specs, check_vma=False)
```

time: 99.1 us -> 88.1 us (0.89)
  Pallas kernels: 18.4 us -> 9.35 us
  waiting for transfers between devices: 16.8 us -> 13.9 us
    pallas_call x1, Pallas kernels: 12.2 us -> 2.5 us  [body(): pl.pallas_call(edge_kernel, out_shape=(shape(UP_ROWS, layers, columns), s...]
    ppermute x1, waiting for transfers between devices: 16.8 us -> 13.8 us  [body(): low = lax.ppermute(up, TILE, [(i, i + 1) for i in range(tiles - 1)])]
    pallas_call x1 -> x2, Pallas kernels: 2.72 us -> 3.41 us  [the longest x1 2.07 us: body(): pl.pallas_call(outside_kernel, out_shape=(shape(rows, layers, columns), s...]
  transfers between devices with their start and end apart: 2 -> 2, of which waited for: 1 -> 1; matrix products, arithmetic and copies ran while one was open for 0% -> 0% of each run, Pallas kernels for 0% -> 2%
where the time goes in v3:
time: 88.1 us; the launch traced here: 87.7 us
  blocking collectives  43.2 us (49%)
  starting transfers between devices  18.8 us (21%)
  waiting for transfers between devices  13.9 us (16%)
  Pallas kernels  9.35 us (11%)
  local copies, waits for them, and re-layouts  1.6 us (2%)
    all_to_all x1, blocking collectives, body(): line = lax.all_to_all(shares.reshape(32, 4, wells), LINE, 0, 0)  27.9 us
    all_to_all x1, blocking collectives, body(): plane = lax.all_to_all(spreads, PLANE, 0, 0)  15.3 us
    ppermute x1, waiting for transfers between devices, body(): low = lax.ppermute(up, TILE, [(i, i + 1) for i in range(tiles - 1)])  13.8 us
    ppermute x1, starting transfers between devices, body(): low = lax.ppermute(up, TILE, [(i, i + 1) for i in range(tiles - 1)])  9.97 us
    ppermute x1, starting transfers between devices, body(): high = lax.ppermute(down, TILE, [(i + 1, i) for i in range(tiles - 1)])  8.79 us
    pallas_call x1, Pallas kernels, body(): pl.pallas_call(edge_kernel, out_shape=(shape(UP_ROWS, layers, columns), s...  2.5 us
    pallas_call x1, Pallas kernels, body(): pl.pallas_call(outside_kernel, out_shape=(shape(rows, layers, columns), s...  2.07 us
    pallas_call x1, Pallas kernels, body(): pl.pallas_call(gram_kernel, out_shape=(shape(SUBSTEPS, 1, obs_error.shape...  1.87 us
  transfers between devices with their start and end apart: 2, of which 1 were waited for; matrix products, arithmetic and copies ran while one was open for 0% of the time, Pallas kernels for 2%

profile of v3, /device:TPU:1, one launch (start us, length us, event | category | flops | bytes accessed | tf_op | source)
XLA Modules:
  0.0 87.7 jit_solution(17692801307005981016)
XLA Ops:
  0.7 2.5 %edges.1 = (f32[7,64,128]{2,1,0:T(8,128)}, f32[8,64,128]{2,1,0:T(8,128)}) custom-call(f32[8,64,128]{2,1,0:T(8,128)} %bitcast.32, f32[8,64,128]{2,1,0:T(8,128)} %bitcast.17, f32[8,64,128]{2,1,0:T(8,128)} %bitcast.20, f32[8,64,128]{2,1,0:T(8,128)} %bitcast.23, f32[8,64,128]{2,1,0:T(8,128)} %bitcast.26, f32[8,64,128]{2,1,0:T(8,128)} %bitcast.29), custom_call_target="tpu_custom_call" | custom-call | tf_op jit(solution)/shard_map/edges/pallas_call | solution.py:338
  3.2 8.8 %collective-permute-start.1 = (f32[8,64,128]{2,1,0:T(8,128)}, f32[8,64,128]{2,1,0:T(8,128)S(1)}, u32[]{:S(2)}, u32[]{:S(2)}) collective-permute-start(f32[8,64,128]{2,1,0:T(8,128)} %get-tuple-element.16), channel_id=1, source_target_pairs={{1,0},{2,1},{3,2},{4,3},{5,4},{6,5},{7,6},{8,7},{9,8},{10,9},{11,1... | collective-permute-start | bytes 786440 | tf_op jit(solution)/shard_map/ppermute | solution.py:349
  12.0 10.0 %collective-permute-start = (f32[7,64,128]{2,1,0:T(8,128)}, f32[7,64,128]{2,1,0:T(8,128)S(1)}, u32[]{:S(2)}, u32[]{:S(2)}) collective-permute-start(f32[7,64,128]{2,1,0:T(8,128)} %get-tuple-element.15.after), channel_id=1, source_target_pairs={{0,1},{1,2},{2,3},{3,4},{4,5},{5,6},{6,7},{7,8},{8,9},{9,10},{10,1... | collective-permute-start | bytes 688136 | tf_op jit(solution)/shard_map/ppermute | solution.py:348
  22.0 0.0 copy-start.10
  22.0 0.0 copy-start.11
  22.0 0.0 copy-start.8
  22.0 0.0 copy-start.9
  22.0 0.0 copy-done
  22.0 0.0 copy-done.1
  22.0 0.0 copy-done.2
  22.1 0.6 copy-done.10
  22.7 0.0 copy-done.11
  22.7 0.0 copy-done.8
  22.7 0.0 copy-done.9
  22.7 0.9 %copy-done.6 = f32[7,64,128]{2,1,0:T(8,128)S(1)} copy-done((f32[7,64,128]{2,1,0:T(8,128)S(1)}, f32[7,64,128]{2,1,0:T(8,128)}, u32[]{:S(2)}) %copy-start.6) | copy-done | bytes 229400
  23.6 1.3 %inside.1 = (f32[12,64,128]{2,1,0:T(8,128)S(1)}, f32[2,64,128]{2,1,0:T(8,128)S(1)}, f32[4,128]{1,0:T(4,128)S(1)}, bf16[256,384]{1,0:T(8,128)(2,1)S(1)}, f32[256,128]{1,0:T(8,128)S(1)}, /*index=5*/f32[256,128]{1,0:T(8,128)S(1)}) custom-call(f32[8,64,128]{2,1,0:T(8,128)S(1)} %bitcast.33, f32[8,64,128]{2,1,0:T(8,128)S(1)} %bitcast.18, ...), custom_call_target="tpu_custom_call" | custom-call | tf_op jit(solution)/shard_map/inside/pallas_call | solution.py:353
  25.0 0.1 pad_add_fusion.where
  25.1 13.8 %collective-permute-done.low = f32[7,64,128]{2,1,0:T(8,128)S(1)} collective-permute-done((f32[7,64,128]{2,1,0:T(8,128)}, f32[7,64,128]{2,1,0:T(8,128)S(1)}, u32[]{:S(2)}, u32[]{:S(2)}) %collective-permute-start) | collective-permute-done | bytes 229408 | tf_op jit(solution)/shard_map/ppermute | solution.py:348
  38.9 0.0 collective-permute-done.1.high
  38.9 2.1 %outside.1 = (f32[8,64,128]{2,1,0:T(8,128)}, f32[128,128]{1,0:T(8,128)S(1)}) custom-call(f32[8,64,128]{2,1,0:T(8,128)S(1)} %bitcast.19, f32[8,64,128]{2,1,0:T(8,128)S(1)} %bitcast.22, f32[8,64,128]{2,1,0:T(8,128)S(1)} %bitcast.25, f32[8,64,128]{2,1,0:T(8,128)S(1)} %bitcast.28, f32[8,64,128]{2,1,0:T(8,128)S(1)} %bitcast.31, ...), custom_call_target="tpu_custom_call" | custom-call | tf_op jit(solution)/shard_map/outside/pallas_call | solution.py:375
  41.0 27.9 %all_to_all.10 = f32[32,4,128]{2,1,0:T(4,128)} all-to-all(f32[32,4,128]{2,1,0:T(4,128)S(1)} %bitcast.34), channel_id=1, replica_groups=mesh['x'=4,'zl'=8,'y'=4,'zh'=2,'c'=2] {'zl','zh','c'}, dimensions={0} | all-to-all | bytes 131072 | tf_op jit(solution)/shard_map/all_to_all | solution.py:383
  68.9 1.6 %line_sums.1 = f32[16,32,128]{2,1,0:T(8,128)} custom-call(f32[128,128]{1,0:T(8,128)} %bitcast.39), custom_call_target="tpu_custom_call" | custom-call | tf_op jit(solution)/shard_map/line_sums/pallas_call | solution.py:384
  70.5 15.3 %all_to_all.11.parts = f32[16,32,128]{2,1,0:T(8,128)} all-to-all(f32[16,32,128]{2,1,0:T(8,128)} %line_sums.1), channel_id=1, replica_groups=mesh['x'=4,'zl'=8,'y'=4,'zh'=2,'c'=2] {'x','y'}, dimensions={0} | all-to-all | bytes 524288 | tf_op jit(solution)/shard_map/all_to_all | solution.py:391
  85.8 1.9 %gram_row.1 = (f32[3,1,8]{2,1,0:T(1,128)}, f32[1,32]{1,0:T(1,128)}) custom-call(f32[16,32,128]{2,1,0:T(8,128)} %all_to_all.11.parts, s32[4]{0:T(128)} %copy-done.7), custom_call_target="tpu_custom_call" | custom-call | tf_op jit(solution)/shard_map/gram_row/pallas_call | solution.py:392
  (12 shorter events, 0.0 us)
Async XLA Ops:
  0.6 21.4 %copy-start = (f32[1,8,64,128]{3,2,1,0:T(8,128)S(1)}, f32[1,8,64,128]{3,2,1,0:T(8,128)}, u32[]{:S(2)}) copy-start(f32[1,8,64,128]{3,2,1,0:T(8,128)} %param.11) | copy-start | bytes 786436
  0.6 21.4 %copy-start.1 = (f32[1,8,64,128]{3,2,1,0:T(8,128)S(1)}, f32[1,8,64,128]{3,2,1,0:T(8,128)}, u32[]{:S(2)}) copy-start(f32[1,8,64,128]{3,2,1,0:T(8,128)} %param.12) | copy-start | bytes 786436
  0.7 21.4 %copy-start.2 = (f32[1,8,64,128]{3,2,1,0:T(8,128)S(1)}, f32[1,8,64,128]{3,2,1,0:T(8,128)}, u32[]{:S(2)}) copy-start(f32[1,8,64,128]{3,2,1,0:T(8,128)} %param.13) | copy-start | bytes 786436
  0.7 21.4 %copy-start.3 = (f32[1,8,64,128]{3,2,1,0:T(8,128)S(1)}, f32[1,8,64,128]{3,2,1,0:T(8,128)}, u32[]{:S(2)}) copy-start(f32[1,8,64,128]{3,2,1,0:T(8,128)} %param.14) | copy-start | bytes 786436
  0.7 21.4 %copy-start.4 = (f32[1,8,64,128]{3,2,1,0:T(8,128)S(1)}, f32[1,8,64,128]{3,2,1,0:T(8,128)}, u32[]{:S(2)}) copy-start(f32[1,8,64,128]{3,2,1,0:T(8,128)} %param.15) | copy-start | bytes 786436
  0.7 21.4 %copy-start.5 = (f32[1,8,64,128]{3,2,1,0:T(8,128)S(1)}, f32[1,8,64,128]{3,2,1,0:T(8,128)}, u32[]{:S(2)}) copy-start(f32[1,8,64,128]{3,2,1,0:T(8,128)} %param.10) | copy-start | bytes 786436
  3.2 35.7 %collective-permute-start.1 = (f32[8,64,128]{2,1,0:T(8,128)}, f32[8,64,128]{2,1,0:T(8,128)S(1)}, u32[]{:S(2)}, u32[]{:S(2)}) collective-permute-start(f32[8,64,128]{2,1,0:T(8,128)} %get-tuple-element.16), channel_id=1, source_target_pairs={{1,0},{2,1},{3,2},{4,3},{5,4},{6,5},{7,6},{8,7},{9,8},{10,9},{11,1... | collective-permute-start | bytes 786440 | tf_op jit(solution)/shard_map/ppermute | solution.py:349
  12.0 26.9 %collective-permute-start = (f32[7,64,128]{2,1,0:T(8,128)}, f32[7,64,128]{2,1,0:T(8,128)S(1)}, u32[]{:S(2)}, u32[]{:S(2)}) collective-permute-start(f32[7,64,128]{2,1,0:T(8,128)} %get-tuple-element.15.after), channel_id=1, source_target_pairs={{0,1},{1,2},{2,3},{3,4},{4,5},{5,6},{6,7},{7,8},{8,9},{9,10},{10,1... | collective-permute-start | bytes 688136 | tf_op jit(solution)/shard_map/ppermute | solution.py:348
  22.0 0.7 copy-start.10
  22.0 0.7 copy-start.11
  22.0 0.7 copy-start.8
  22.0 0.7 copy-start.9
  22.7 0.9 %copy-start.6 = (f32[7,64,128]{2,1,0:T(8,128)S(1)}, f32[7,64,128]{2,1,0:T(8,128)}, u32[]{:S(2)}) copy-start(f32[7,64,128]{2,1,0:T(8,128)} %get-tuple-element.15.after) | copy-start | bytes 688132
  25.1 13.9 %copy-start.7 = (s32[4]{0:T(128)}, s32[4]{0:T(128)S(1)}, u32[]{:S(2)}) copy-start(s32[4]{0:T(128)S(1)} %pad_add_fusion.where) | copy-start | bytes 52

commit v4 on v3

--- a/solution.py
+++ b/solution.py
@@ -43,40 +43,36 @@
     )
 
 
-def edge_kernel(sat, mob, pore, qx, qy, qz, up, down, s, m, p, x, y, z, made, in_sem, out_sem):
+def edge_kernel(sat, mob, pore, qx, qy, qz, up, down, s, m, p, x, y, z, in_sem):
     loads = []
-    for k, (field, held) in enumerate(((sat, s), (mob, m), (qx, x), (pore, p), (qy, y), (qz, z))):
-        for j, start in enumerate((0, 5)):
+    for j, start in enumerate((0, 5)):
+        for k, (field, near) in enumerate(
+            ((sat, s), (mob, m), (qx, x), (qy, y), (qz, z), (pore, p))
+        ):
             part = pl.ds(start, 3)
             loads.append(
-                pltpu.make_async_copy(field.at[part], held.at[part], in_sem.at[2 * k + j])
+                pltpu.make_async_copy(field.at[part], near.at[part], in_sem.at[6 * j + k])
             )
     for load in loads:
         load.start()
-    for load in loads:
+    for load in loads[:6]:
         load.wait()
-
     f = [frac(s[i], m[i]) for i in range(3)]
     face_1 = across(x[1], f[0], f[1])
     flow_1 = frac(moved(s[1], p[1], across(x[2], f[1], f[2]) - face_1, f[1], z[1], y[1]), m[1])
-    for k, held in enumerate((s, m, p, z, y, x)):
-        made[k] = held[0]
-    made[6] = face_1
-    made[7] = jnp.minimum(x[1], 0.0) * flow_1
-    down_copy = pltpu.make_async_copy(made.at[pl.ds(0, DOWN_ROWS)], down, out_sem.at[0])
-    down_copy.start()
-
+    for k, near in enumerate((s, m, p, z, y, x)):
+        down[k] = near[0]
+    down[6] = face_1
+    down[7] = jnp.minimum(x[1], 0.0) * flow_1
+    for load in loads[6:]:
+        load.wait()
     f = {i: frac(s[i], m[i]) for i in range(5, 8)}
     face_7 = across(x[7], f[6], f[7])
     flow_6 = frac(moved(s[6], p[6], face_7 - across(x[6], f[5], f[6]), f[6], z[6], y[6]), m[6])
-    for k, held in enumerate((s, m, p, z, y)):
-        made[DOWN_ROWS + k] = held[7]
-    made[DOWN_ROWS + 5] = face_7
-    made[DOWN_ROWS + 6] = jnp.maximum(x[7], 0.0) * flow_6
-    up_copy = pltpu.make_async_copy(made.at[pl.ds(DOWN_ROWS, UP_ROWS)], up, out_sem.at[1])
-    up_copy.start()
-    down_copy.wait()
-    up_copy.wait()
+    for k, near in enumerate((s, m, p, z, y)):
+        up[k] = near[7]
+    up[5] = face_7
+    up[6] = jnp.maximum(x[7], 0.0) * flow_6
 
 
 OUTER = ((0, 7), (1, 6), (2, 5))
@@ -313,6 +309,10 @@
     return jax.ShapeDtypeStruct(dims, jnp.float32)
 
 
+def held(*dims):
+    return pltpu.VMEM(dims, jnp.float32)
+
+
 def body(
     saturation,
     mobility,
@@ -337,12 +337,11 @@
     ).astype(jnp.int32)
     up, down = pl.pallas_call(
         edge_kernel,
-        out_shape=(shape(UP_ROWS, layers, columns), shape(DOWN_ROWS, layers, columns)),
+        out_shape=(held(UP_ROWS, layers, columns), held(DOWN_ROWS, layers, columns)),
         in_specs=[ANY] * 6,
-        out_specs=(ANY, ANY),
+        out_specs=(VMEM, VMEM),
         scratch_shapes=[pltpu.VMEM((rows, layers, columns), jnp.float32)] * 6
-        + [pltpu.VMEM((UP_ROWS + DOWN_ROWS, layers, columns), jnp.float32)]
-        + [pltpu.SemaphoreType.DMA((12,)), pltpu.SemaphoreType.DMA((2,))],
+        + [pltpu.SemaphoreType.DMA((12,))],
         name="edges",
     )(*fields)
     low = lax.ppermute(up, TILE, [(i, i + 1) for i in range(tiles - 1)])
@@ -374,21 +373,21 @@
     )
     new_saturation, shares = pl.pallas_call(
         outside_kernel,
-        out_shape=(shape(rows, layers, columns), shape(128, wells)),
+        out_shape=(held(rows, layers, columns), held(128, wells)),
         in_specs=[VMEM] * 13 + [SMEM],
         out_specs=(VMEM, VMEM),
         compiler_params=pltpu.CompilerParams(vmem_limit_bytes=32 * 1024 * 1024),
         name="outside",
     )(mob, pore, qx, qy, qz, low, high, mids, middle, early, hot, mask, weight, where)
     line = lax.all_to_all(shares.reshape(32, 4, wells), LINE, 0, 0)
-    spreads = pl.pallas_call(
+    (spreads,) = pl.pallas_call(
         line_kernel,
-        out_shape=shape(16, 32, wells),
+        out_shape=(held(16, 32, wells),),
         in_specs=[VMEM],
-        out_specs=VMEM,
+        out_specs=(VMEM,),
         name="line_sums",
     )(line.reshape(128, wells))
-    plane = lax.all_to_all(spreads, PLANE, 0, 0)
+    plane = pltpu.with_memory_space_constraint(lax.all_to_all(spreads, PLANE, 0, 0), pltpu.VMEM)
     rates, gram = pl.pallas_call(
         gram_kernel,
         out_shape=(shape(SUBSTEPS, 1, obs_error.shape[0]), shape(1, 32)),

time: 88.1 us -> 86.1 us (0.977)
  blocking collectives: 43.2 us -> 28.1 us
  waiting for transfers between devices: 13.9 us -> 21.6 us
  starting transfers between devices: 18.8 us -> 26.1 us
  Pallas kernels: 9.35 us -> 7.73 us
    all_to_all x1 -> x0, blocking collectives: 15.3 us -> none  [body(): plane = lax.all_to_all(spreads, PLANE, 0, 0)]
    all_to_all x0 -> x1, starting transfers between devices: none -> 7.38 us  [body(): lax.all_to_all(spreads, PLANE, 0, 0)]
    all_to_all x0 -> x1, waiting for transfers between devices: none -> 7.12 us  [body(): lax.all_to_all(spreads, PLANE, 0, 0)]
    pallas_call x3, Pallas kernels: 6.13 us -> 4.79 us  [the longest x1 1.72 us: body(): pl.pallas_call(edge_kernel, out_shape=(held(UP_ROWS, layers, columns), he...]
  transfers between devices with their start and end apart: 2 -> 3, of which waited for: 1 -> 2; matrix products, arithmetic and copies ran while one was open for 0% -> 1% of each run, Pallas kernels for 2% -> 2%
where the time goes in v4:
time: 86.1 us; the launch traced here: 85.7 us
  blocking collectives  28.1 us (33%)
  starting transfers between devices  26.1 us (30%)
  waiting for transfers between devices  21.6 us (25%)
  Pallas kernels  7.73 us (9%)
  local copies, waits for them, and re-layouts  1.37 us (2%)
    all_to_all x1, blocking collectives, body(): line = lax.all_to_all(shares.reshape(32, 4, wells), LINE, 0, 0)  28.1 us
    ppermute x1, waiting for transfers between devices, body(): low = lax.ppermute(up, TILE, [(i, i + 1) for i in range(tiles - 1)])  14.4 us
    ppermute x1, starting transfers between devices, body(): low = lax.ppermute(up, TILE, [(i, i + 1) for i in range(tiles - 1)])  9.97 us
    ppermute x1, starting transfers between devices, body(): high = lax.ppermute(down, TILE, [(i + 1, i) for i in range(tiles - 1)])  8.79 us
    all_to_all x1, starting transfers between devices, body(): lax.all_to_all(spreads, PLANE, 0, 0)  7.38 us
    all_to_all x1, waiting for transfers between devices, body(): lax.all_to_all(spreads, PLANE, 0, 0)  7.12 us
  transfers between devices with their start and end apart: 3, of which 2 were waited for; matrix products, arithmetic and copies ran while one was open for 1% of the time, Pallas kernels for 2%

profile of v4, /device:TPU:1, one launch (start us, length us, event | category | flops | bytes accessed | tf_op | source)
XLA Modules:
  0.0 85.7 jit_solution(14602721318873867740)
XLA Ops:
  0.6 0.0 copy-start
  0.6 0.0 copy-start.1
  0.7 1.7 %edges.1 = (f32[7,64,128]{2,1,0:T(8,128)S(1)}, f32[8,64,128]{2,1,0:T(8,128)S(1)}) custom-call(f32[8,64,128]{2,1,0:T(8,128)} %bitcast.33, f32[8,64,128]{2,1,0:T(8,128)} %bitcast.18, f32[8,64,128]{2,1,0:T(8,128)} %bitcast.21, f32[8,64,128]{2,1,0:T(8,128)} %bitcast.24, f32[8,64,128]{2,1,0:T(8,128)} %bitcast.27, f32[8,64,128]{2,1,0:T(8,128)} %bitcast.30), custom_call_target="tpu_custom_call" | custom-call | tf_op jit(solution)/shard_map/edges/pallas_call | solution.py:338
  2.4 8.8 %collective-permute-start.1 = (f32[8,64,128]{2,1,0:T(8,128)S(1)}, f32[8,64,128]{2,1,0:T(8,128)S(1)}, u32[]{:S(2)}, u32[]{:S(2)}) collective-permute-start(f32[8,64,128]{2,1,0:T(8,128)S(1)} %get-tuple-element.16), channel_id=1, source_target_pairs={{1,0},{2,1},{3,2},{4,3},{5,4},{6,5},{7,6},{8,7},{9,8},{10,9},{11,1... | collective-permute-start | bytes 786440 | tf_op jit(solution)/shard_map/ppermute | solution.py:348
  11.2 10.0 %collective-permute-start = (f32[7,64,128]{2,1,0:T(8,128)S(1)}, f32[7,64,128]{2,1,0:T(8,128)S(1)}, u32[]{:S(2)}, u32[]{:S(2)}) collective-permute-start(f32[7,64,128]{2,1,0:T(8,128)S(1)} %get-tuple-element.15.after), channel_id=1, source_target_pairs={{0,1},{1,2},{2,3},{3,4},{4,5},{5,6},{6,7},{7,8},{8,9},{9,10},{10,1... | collective-permute-start | bytes 688136 | tf_op jit(solution)/shard_map/ppermute | solution.py:347
  21.2 0.0 copy-start.9
  21.2 0.0 copy-start.10
  21.2 0.0 copy-start.7
  21.2 0.0 copy-start.8
  21.3 0.6 copy-done.9
  21.9 0.0 copy-done.10
  21.9 0.0 copy-done.7
  21.9 0.0 copy-done.8
  21.9 1.4 %inside.1 = (f32[12,64,128]{2,1,0:T(8,128)S(1)}, f32[2,64,128]{2,1,0:T(8,128)S(1)}, f32[4,128]{1,0:T(4,128)S(1)}, bf16[256,384]{1,0:T(8,128)(2,1)S(1)}, f32[256,128]{1,0:T(8,128)S(1)}, /*index=5*/f32[256,128]{1,0:T(8,128)S(1)}) custom-call(f32[8,64,128]{2,1,0:T(8,128)S(1)} %bitcast.34, f32[8,64,128]{2,1,0:T(8,128)S(1)} %bitcast.19, ...), custom_call_target="tpu_custom_call" | custom-call | tf_op jit(solution)/shard_map/inside/pallas_call | solution.py:352
  23.3 0.1 pad_add_fusion.where
  23.4 14.4 %collective-permute-done.low = f32[7,64,128]{2,1,0:T(8,128)S(1)} collective-permute-done((f32[7,64,128]{2,1,0:T(8,128)S(1)}, f32[7,64,128]{2,1,0:T(8,128)S(1)}, u32[]{:S(2)}, u32[]{:S(2)}) %collective-permute-start) | collective-permute-done | bytes 229408 | tf_op jit(solution)/shard_map/ppermute | solution.py:347
  37.8 0.0 collective-permute-done.1.high
  37.8 1.5 %outside.1 = (f32[8,64,128]{2,1,0:T(8,128)S(1)}, f32[128,128]{1,0:T(8,128)S(1)}) custom-call(f32[8,64,128]{2,1,0:T(8,128)S(1)} %bitcast.20, f32[8,64,128]{2,1,0:T(8,128)S(1)} %bitcast.23, f32[8,64,128]{2,1,0:T(8,128)S(1)} %bitcast.26, f32[8,64,128]{2,1,0:T(8,128)S(1)} %bitcast.29, f32[8,64,128]{2,1,0:T(8,128)S(1)} %bitcast.32, ...), custom_call_target="tpu_custom_call" | custom-call | tf_op jit(solution)/shard_map/outside/pallas_call | solution.py:374
  39.3 28.1 %all_to_all.10 = f32[32,4,128]{2,1,0:T(4,128)} all-to-all(f32[32,4,128]{2,1,0:T(4,128)S(1)} %bitcast.35), channel_id=1, replica_groups=mesh['x'=4,'zl'=8,'y'=4,'zh'=2,'c'=2] {'zl','zh','c'}, dimensions={0} | all-to-all | bytes 131072 | tf_op jit(solution)/shard_map/all_to_all | solution.py:382
  67.4 1.6 %line_sums.1 = f32[16,32,128]{2,1,0:T(8,128)} custom-call(f32[128,128]{1,0:T(8,128)} %bitcast.40), custom_call_target="tpu_custom_call" | custom-call | tf_op jit(solution)/shard_map/line_sums/pallas_call | solution.py:383
  68.9 7.4 %all-to-all-start.1 = ((f32[16,32,128]{2,1,0:T(8,128)}), f32[16,32,128]{2,1,0:T(8,128)S(1)}, u32[]{:S(2)}, u32[]{:S(2)}) async-start(f32[16,32,128]{2,1,0:T(8,128)} %line_sums.1), calls=%async_computation.1 | async-start | bytes 524288 | tf_op jit(solution)/shard_map/all_to_all | solution.py:390
  76.3 0.7 copy.13
  77.0 7.1 %all-to-all-done.1.parts = f32[16,32,128]{2,1,0:T(8,128)S(1)} async-done(((f32[16,32,128]{2,1,0:T(8,128)}), f32[16,32,128]{2,1,0:T(8,128)S(1)}, u32[]{:S(2)}, u32[]{:S(2)}) %all-to-all-start.1) | async-done | bytes 262176 | tf_op jit(solution)/shard_map/all_to_all | solution.py:390
  84.2 1.6 %gram_row.1 = (f32[3,1,8]{2,1,0:T(1,128)}, f32[1,32]{1,0:T(1,128)}) custom-call(f32[16,32,128]{2,1,0:T(8,128)S(1)} %all-to-all-done.1.parts, s32[4]{0:T(128)} %copy-done.6), custom_call_target="tpu_custom_call" | custom-call | tf_op jit(solution)/shard_map/gram_row/pallas_call | solution.py:391
  (12 shorter events, 0.0 us)
Async XLA Ops:
  0.6 20.6 %copy-start = (f32[1,8,64,128]{3,2,1,0:T(8,128)S(1)}, f32[1,8,64,128]{3,2,1,0:T(8,128)}, u32[]{:S(2)}) copy-start(f32[1,8,64,128]{3,2,1,0:T(8,128)} %param.11) | copy-start | bytes 786436
  0.6 20.6 %copy-start.1 = (f32[1,8,64,128]{3,2,1,0:T(8,128)S(1)}, f32[1,8,64,128]{3,2,1,0:T(8,128)}, u32[]{:S(2)}) copy-start(f32[1,8,64,128]{3,2,1,0:T(8,128)} %param.12) | copy-start | bytes 786436
  0.7 20.6 %copy-start.2 = (f32[1,8,64,128]{3,2,1,0:T(8,128)S(1)}, f32[1,8,64,128]{3,2,1,0:T(8,128)}, u32[]{:S(2)}) copy-start(f32[1,8,64,128]{3,2,1,0:T(8,128)} %param.13) | copy-start | bytes 786436
  0.7 20.6 %copy-start.3 = (f32[1,8,64,128]{3,2,1,0:T(8,128)S(1)}, f32[1,8,64,128]{3,2,1,0:T(8,128)}, u32[]{:S(2)}) copy-start(f32[1,8,64,128]{3,2,1,0:T(8,128)} %param.14) | copy-start | bytes 786436
  0.7 20.6 %copy-start.4 = (f32[1,8,64,128]{3,2,1,0:T(8,128)S(1)}, f32[1,8,64,128]{3,2,1,0:T(8,128)}, u32[]{:S(2)}) copy-start(f32[1,8,64,128]{3,2,1,0:T(8,128)} %param.15) | copy-start | bytes 786436
  0.7 20.6 %copy-start.5 = (f32[1,8,64,128]{3,2,1,0:T(8,128)S(1)}, f32[1,8,64,128]{3,2,1,0:T(8,128)}, u32[]{:S(2)}) copy-start(f32[1,8,64,128]{3,2,1,0:T(8,128)} %param.10) | copy-start | bytes 786436
  2.4 35.4 %collective-permute-start.1 = (f32[8,64,128]{2,1,0:T(8,128)S(1)}, f32[8,64,128]{2,1,0:T(8,128)S(1)}, u32[]{:S(2)}, u32[]{:S(2)}) collective-permute-start(f32[8,64,128]{2,1,0:T(8,128)S(1)} %get-tuple-element.16), channel_id=1, source_target_pairs={{1,0},{2,1},{3,2},{4,3},{5,4},{6,5},{7,6},{8,7},{9,8},{10,9},{11,1... | collective-permute-start | bytes 786440 | tf_op jit(solution)/shard_map/ppermute | solution.py:348
  11.2 26.6 %collective-permute-start = (f32[7,64,128]{2,1,0:T(8,128)S(1)}, f32[7,64,128]{2,1,0:T(8,128)S(1)}, u32[]{:S(2)}, u32[]{:S(2)}) collective-permute-start(f32[7,64,128]{2,1,0:T(8,128)S(1)} %get-tuple-element.15.after), channel_id=1, source_target_pairs={{0,1},{1,2},{2,3},{3,4},{4,5},{5,6},{6,7},{7,8},{8,9},{9,10},{10,1... | collective-permute-start | bytes 688136 | tf_op jit(solution)/shard_map/ppermute | solution.py:347
  21.2 0.7 copy-start.9
  21.2 0.7 copy-start.10
  21.2 0.7 copy-start.7
  21.2 0.7 copy-start.8
  23.4 14.4 %copy-start.6 = (s32[4]{0:T(128)}, s32[4]{0:T(128)S(1)}, u32[]{:S(2)}) copy-start(s32[4]{0:T(128)S(1)} %pad_add_fusion.where) | copy-start | bytes 52
  68.9 15.2 %all-to-all-start.1 = ((f32[16,32,128]{2,1,0:T(8,128)}), f32[16,32,128]{2,1,0:T(8,128)S(1)}, u32[]{:S(2)}, u32[]{:S(2)}) async-start(f32[16,32,128]{2,1,0:T(8,128)} %line_sums.1), calls=%async_computation.1 | async-start | bytes 524288 | tf_op jit(solution)/shard_map/all_to_all | solution.py:390

commit v5 on v4

--- a/solution.py
+++ b/solution.py
@@ -13,8 +13,7 @@
 TILE = ("y", "zh", "c")
 LINE = ("zl", "zh", "c")
 PLANE = ("x", "y")
-UP_ROWS = 7
-DOWN_ROWS = 8
+EDGE_ROWS = 8
 HIGHEST = lax.Precision.HIGHEST
 
 
@@ -43,7 +42,8 @@
     )
 
 
-def edge_kernel(sat, mob, pore, qx, qy, qz, up, down, s, m, p, x, y, z, in_sem):
+def edge_kernel(sat, mob, pore, qx, qy, qz, far_out, near_out, s, m, p, x, y, z, in_sem):
+    first_core = lax.axis_index("c") == 0
     loads = []
     for j, start in enumerate((0, 5)):
         for k, (field, near) in enumerate(
@@ -55,24 +55,21 @@
             )
     for load in loads:
         load.start()
-    for load in loads[:6]:
+    for load in loads:
         load.wait()
     f = [frac(s[i], m[i]) for i in range(3)]
     face_1 = across(x[1], f[0], f[1])
     flow_1 = frac(moved(s[1], p[1], across(x[2], f[1], f[2]) - face_1, f[1], z[1], y[1]), m[1])
-    for k, near in enumerate((s, m, p, z, y, x)):
-        down[k] = near[0]
-    down[6] = face_1
-    down[7] = jnp.minimum(x[1], 0.0) * flow_1
-    for load in loads[6:]:
-        load.wait()
+    down = [field[0] for field in (s, m, p, z, y, x)]
+    down += [face_1, jnp.minimum(x[1], 0.0) * flow_1]
     f = {i: frac(s[i], m[i]) for i in range(5, 8)}
     face_7 = across(x[7], f[6], f[7])
     flow_6 = frac(moved(s[6], p[6], face_7 - across(x[6], f[5], f[6]), f[6], z[6], y[6]), m[6])
-    for k, near in enumerate((s, m, p, z, y)):
-        up[k] = near[7]
-    up[5] = face_7
-    up[6] = jnp.maximum(x[7], 0.0) * flow_6
+    up = [field[7] for field in (s, m, p, z, y)]
+    up += [face_7, jnp.maximum(x[7], 0.0) * flow_6, jnp.zeros_like(face_7)]
+    for k in range(EDGE_ROWS):
+        near_out[k] = jnp.where(first_core, up[k], down[k])
+        far_out[k] = jnp.where(first_core, down[k], up[k])
 
 
 OUTER = ((0, 7), (1, 6), (2, 5))
@@ -103,7 +100,7 @@
 
 
 def inside_kernel(
-    sat, mob, pore, qx, qy, qz, cell, well, factor, obs, after, mids, middle, early, hot, mask, weight
+    sat, mob, pore, qx, qy, qz, cell, well, factor, obs, after, other, mids, middle, early, hot, mask, weight
 ):
     rows, layers, columns = sat.shape
     count = cell.shape[1]
@@ -161,12 +158,15 @@
 
 
 def outside_kernel(
-    mob, pore, qx, qy, qz, low, high, mids, middle, early, hot, mask, weight, where, new_sat, shares
+    mob, pore, qx, qy, qz, far, near, mids, middle, early, hot, mask, weight, where, new_sat, shares
 ):
     tile = where[0]
     last = where[1]
     has_low = tile > 0
     has_high = tile < last
+    first_core = where[4] == 0
+    low = [jnp.where(first_core, far[k], near[k]) for k in range(EDGE_ROWS - 1)]
+    high = [jnp.where(first_core, near[k], far[k]) for k in range(EDGE_ROWS)]
     below = jnp.where(has_low, low[0], 0.5)
     below_mob = jnp.where(has_low, low[1], 1.0)
     above = jnp.where(has_high, high[0], 0.5)
@@ -333,19 +333,26 @@
     tiles = lax.axis_size(TILE)
     tile = lax.axis_index(TILE)
     where = jnp.stack(
-        [tile, jnp.full_like(tile, tiles - 1), lax.axis_index("x"), lax.axis_index("zl")]
+        [
+            tile,
+            jnp.full_like(tile, tiles - 1),
+            lax.axis_index("x"),
+            lax.axis_index("zl"),
+            lax.axis_index("c"),
+        ]
     ).astype(jnp.int32)
-    up, down = pl.pallas_call(
+    far_out, near_out = pl.pallas_call(
         edge_kernel,
-        out_shape=(held(UP_ROWS, layers, columns), held(DOWN_ROWS, layers, columns)),
+        out_shape=(held(EDGE_ROWS, layers, columns),) * 2,
         in_specs=[ANY] * 6,
         out_specs=(VMEM, VMEM),
         scratch_shapes=[pltpu.VMEM((rows, layers, columns), jnp.float32)] * 6
         + [pltpu.SemaphoreType.DMA((12,))],
         name="edges",
     )(*fields)
-    low = lax.ppermute(up, TILE, [(i, i + 1) for i in range(tiles - 1)])
-    high = lax.ppermute(down, TILE, [(i + 1, i) for i in range(tiles - 1)])
+    pairs = [(i, i + 1) for i in range(1, tiles - 1, 2)]
+    near = lax.ppermute(near_out, TILE, [(i, i ^ 1) for i in range(tiles)])
+    far = lax.ppermute(far_out, TILE, pairs + [(j, i) for i, j in pairs])
     wells = obs_error.shape[0] * tiles
     count = conn_cell.shape[0]
     sat, mob, pore, qx, qy, qz = fields
@@ -359,7 +366,7 @@
             shape(count, columns),
             shape(count, wells),
         ),
-        in_specs=[VMEM] * 10 + [ANY],
+        in_specs=[VMEM] * 10 + [ANY] * 2,
         out_specs=(VMEM,) * 6,
         compiler_params=pltpu.CompilerParams(vmem_limit_bytes=32 * 1024 * 1024),
         name="inside",
@@ -369,7 +376,8 @@
         conn_well.reshape(1, count),
         conn_factor.reshape(1, count),
         obs_error.T,
-        up,
+        far_out,
+        near_out,
     )
     new_saturation, shares = pl.pallas_call(
         outside_kernel,
@@ -378,15 +386,16 @@
         out_specs=(VMEM, VMEM),
         compiler_params=pltpu.CompilerParams(vmem_limit_bytes=32 * 1024 * 1024),
         name="outside",
-    )(mob, pore, qx, qy, qz, low, high, mids, middle, early, hot, mask, weight, where)
+    )(mob, pore, qx, qy, qz, far, near, mids, middle, early, hot, mask, weight, where)
     line = lax.all_to_all(shares.reshape(32, 4, wells), LINE, 0, 0)
+    line = pltpu.with_memory_space_constraint(line.reshape(128, wells), pltpu.VMEM)
     (spreads,) = pl.pallas_call(
         line_kernel,
         out_shape=(held(16, 32, wells),),
         in_specs=[VMEM],
         out_specs=(VMEM,),
         name="line_sums",
-    )(line.reshape(128, wells))
+    )(line)
     plane = pltpu.with_memory_space_constraint(lax.all_to_all(spreads, PLANE, 0, 0), pltpu.VMEM)
     rates, gram = pl.pallas_call(
         gram_kernel,

time: 86.1 us -> 87.6 us (1.017)
  blocking collectives: 28.1 us -> 42.5 us
  waiting for transfers between devices: 21.6 us -> 8.7 us
  local copies, waits for them, and re-layouts: 1.37 us -> 2.91 us
    all_to_all x1, blocking collectives: 28.1 us -> 42.5 us  [body(): line = lax.all_to_all(shares.reshape(32, 4, wells), LINE, 0, 0)]
    ppermute x2, waiting for transfers between devices: 14.4 us -> 1.57 us  [the longest x1 1.57 us: body(): far = lax.ppermute(far_out, TILE, pairs + [(j, i) for i, j in pairs])]
    unnamed x23 -> x27, local copies, waits for them, and re-layouts: 1.37 us -> 2.83 us
where the time goes in v5:
time: 87.6 us; the launch traced here: 87.2 us
  blocking collectives  42.5 us (49%)
  starting transfers between devices  25.4 us (29%)
  waiting for transfers between devices  8.7 us (10%)
  Pallas kernels  6.89 us (8%)
  local copies, waits for them, and re-layouts  2.91 us (3%)
    all_to_all x1, blocking collectives, body(): line = lax.all_to_all(shares.reshape(32, 4, wells), LINE, 0, 0)  42.5 us
    ppermute x1, starting transfers between devices, body(): far = lax.ppermute(far_out, TILE, pairs + [(j, i) for i, j in pairs])  16.8 us
    all_to_all x1, waiting for transfers between devices, body(): lax.all_to_all(spreads, PLANE, 0, 0)  7.12 us
    all_to_all x1, starting transfers between devices, body(): lax.all_to_all(spreads, PLANE, 0, 0)  6.62 us
    unnamed x27, local copies, waits for them, and re-layouts  2.83 us
    ppermute x1, starting transfers between devices, body(): near = lax.ppermute(near_out, TILE, [(i, i ^ 1) for i in range(tiles)])  1.92 us
  transfers between devices with their start and end apart: 3, of which 2 were waited for; matrix products, arithmetic and copies ran while one was open for 1% of the time, Pallas kernels for 2%

profile of v5, /device:TPU:1, one launch (start us, length us, event | category | flops | bytes accessed | tf_op | source)
XLA Modules:
  0.0 87.2 jit_solution(979266732416351027)
XLA Ops:
  0.7 1.7 %edges.1 = (f32[8,64,128]{2,1,0:T(8,128)S(1)}, f32[8,64,128]{2,1,0:T(8,128)S(1)}) custom-call(f32[8,64,128]{2,1,0:T(8,128)} %bitcast.34, f32[8,64,128]{2,1,0:T(8,128)} %bitcast.19, f32[8,64,128]{2,1,0:T(8,128)} %bitcast.22, f32[8,64,128]{2,1,0:T(8,128)} %bitcast.25, f32[8,64,128]{2,1,0:T(8,128)} %bitcast.28, f32[8,64,128]{2,1,0:T(8,128)} %bitcast.31), custom_call_target="tpu_custom_call" | custom-call | tf_op jit(solution)/shard_map/edges/pallas_call | solution.py:344
  2.4 16.8 %collective-permute-start = (f32[8,64,128]{2,1,0:T(8,128)S(1)}, f32[8,64,128]{2,1,0:T(8,128)S(1)}, u32[]{:S(2)}, u32[]{:S(2)}) collective-permute-start(f32[8,64,128]{2,1,0:T(8,128)S(1)} %get-tuple-element.15.after), channel_id=1, source_target_pairs={{1,2},{3,4},{5,6},{7,8},{9,10},{11,12},{13,14},{2,1},{4,3},{6,5},{... | collective-permute-start | bytes 786440 | tf_op jit(solution)/shard_map/ppermute | solution.py:355
  19.3 1.9 %collective-permute-start.1 = (f32[8,64,128]{2,1,0:T(8,128)S(1)}, f32[8,64,128]{2,1,0:T(8,128)S(1)}, u32[]{:S(2)}, u32[]{:S(2)}) collective-permute-start(f32[8,64,128]{2,1,0:T(8,128)S(1)} %get-tuple-element.16.other), channel_id=1, source_target_pairs={{0,1},{1,0},{2,3},{3,2},{4,5},{5,4},{6,7},{7,6},{8,9},{9,8},{10,11... | collective-permute-start | bytes 786440 | tf_op jit(solution)/shard_map/ppermute | solution.py:354
  21.2 0.0 copy-start.11
  21.2 0.0 copy-start.12
  21.2 0.0 copy-start.9
  21.3 0.0 copy-start.10
  21.3 0.6 copy-done.11
  21.9 0.0 copy-done.12
  21.9 0.0 copy-done.9
  21.9 0.0 copy-done.10
  21.9 1.3 %inside.1 = (f32[12,64,128]{2,1,0:T(8,128)S(1)}, f32[2,64,128]{2,1,0:T(8,128)S(1)}, f32[4,128]{1,0:T(4,128)S(1)}, bf16[256,384]{1,0:T(8,128)(2,1)S(1)}, f32[256,128]{1,0:T(8,128)S(1)}, /*index=5*/f32[256,128]{1,0:T(8,128)S(1)}) custom-call(f32[8,64,128]{2,1,0:T(8,128)S(1)} %bitcast.35, f32[8,64,128]{2,1,0:T(8,128)S(1)} %bitcast.20, ...), custom_call_target="tpu_custom_call" | custom-call | tf_op jit(solution)/shard_map/inside/pallas_call | solution.py:359
  23.3 0.0 copy-start.6
  23.3 0.6 copy-done.6
  23.9 0.1 stack.19.where
  24.0 1.6 %collective-permute-done.far = f32[8,64,128]{2,1,0:T(8,128)S(1)} collective-permute-done((f32[8,64,128]{2,1,0:T(8,128)S(1)}, f32[8,64,128]{2,1,0:T(8,128)S(1)}, u32[]{:S(2)}, u32[]{:S(2)}) %collective-permute-start) | collective-permute-done | bytes 262176 | tf_op jit(solution)/shard_map/ppermute | solution.py:355
  25.6 0.8 copy-done.7
  26.4 1.5 %outside.1 = (f32[8,64,128]{2,1,0:T(8,128)S(1)}, f32[128,128]{1,0:T(8,128)S(1)}) custom-call(f32[8,64,128]{2,1,0:T(8,128)S(1)} %bitcast.21, f32[8,64,128]{2,1,0:T(8,128)S(1)} %bitcast.24, f32[8,64,128]{2,1,0:T(8,128)S(1)} %bitcast.27, f32[8,64,128]{2,1,0:T(8,128)S(1)} %bitcast.30, f32[8,64,128]{2,1,0:T(8,128)S(1)} %bitcast.33, ...), custom_call_target="tpu_custom_call" | custom-call | tf_op jit(solution)/shard_map/outside/pallas_call | solution.py:382
  27.9 42.5 %all_to_all.10 = f32[32,4,128]{2,1,0:T(4,128)S(1)} all-to-all(f32[32,4,128]{2,1,0:T(4,128)S(1)} %bitcast.37), channel_id=1, replica_groups=mesh['x'=4,'zl'=8,'y'=4,'zh'=2,'c'=2] {'zl','zh','c'}, dimensions={0} | all-to-all | bytes 131072 | tf_op jit(solution)/shard_map/all_to_all | solution.py:390
  70.4 0.7 line_sums.1
  71.2 6.6 %all-to-all-start.1 = ((f32[16,32,128]{2,1,0:T(8,128)}), f32[16,32,128]{2,1,0:T(8,128)S(1)}, u32[]{:S(2)}, u32[]{:S(2)}) async-start(f32[16,32,128]{2,1,0:T(8,128)} %line_sums.1), calls=%async_computation.1 | async-start | bytes 524288 | tf_op jit(solution)/shard_map/all_to_all | solution.py:399
  77.8 0.7 copy.13
  78.5 7.1 %all-to-all-done.1.parts = f32[16,32,128]{2,1,0:T(8,128)S(1)} async-done(((f32[16,32,128]{2,1,0:T(8,128)}), f32[16,32,128]{2,1,0:T(8,128)S(1)}, u32[]{:S(2)}, u32[]{:S(2)}) %all-to-all-start.1) | async-done | bytes 262176 | tf_op jit(solution)/shard_map/all_to_all | solution.py:399
  85.6 1.6 %gram_row.1 = (f32[3,1,8]{2,1,0:T(1,128)}, f32[1,32]{1,0:T(1,128)}) custom-call(f32[16,32,128]{2,1,0:T(8,128)S(1)} %all-to-all-done.1.parts, s32[5]{0:T(128)} %copy-done.8), custom_call_target="tpu_custom_call" | custom-call | tf_op jit(solution)/shard_map/gram_row/pallas_call | solution.py:400
  (16 shorter events, 0.0 us)
Async XLA Ops:
  0.6 20.6 %copy-start = (f32[1,8,64,128]{3,2,1,0:T(8,128)S(1)}, f32[1,8,64,128]{3,2,1,0:T(8,128)}, u32[]{:S(2)}) copy-start(f32[1,8,64,128]{3,2,1,0:T(8,128)} %param.11) | copy-start | bytes 786436
  0.6 20.6 %copy-start.1 = (f32[1,8,64,128]{3,2,1,0:T(8,128)S(1)}, f32[1,8,64,128]{3,2,1,0:T(8,128)}, u32[]{:S(2)}) copy-start(f32[1,8,64,128]{3,2,1,0:T(8,128)} %param.12) | copy-start | bytes 786436
  0.7 20.6 %copy-start.2 = (f32[1,8,64,128]{3,2,1,0:T(8,128)S(1)}, f32[1,8,64,128]{3,2,1,0:T(8,128)}, u32[]{:S(2)}) copy-start(f32[1,8,64,128]{3,2,1,0:T(8,128)} %param.13) | copy-start | bytes 786436
  0.7 20.6 %copy-start.3 = (f32[1,8,64,128]{3,2,1,0:T(8,128)S(1)}, f32[1,8,64,128]{3,2,1,0:T(8,128)}, u32[]{:S(2)}) copy-start(f32[1,8,64,128]{3,2,1,0:T(8,128)} %param.14) | copy-start | bytes 786436
  0.7 20.6 %copy-start.4 = (f32[1,8,64,128]{3,2,1,0:T(8,128)S(1)}, f32[1,8,64,128]{3,2,1,0:T(8,128)}, u32[]{:S(2)}) copy-start(f32[1,8,64,128]{3,2,1,0:T(8,128)} %param.15) | copy-start | bytes 786436
  0.7 20.6 %copy-start.5 = (f32[1,8,64,128]{3,2,1,0:T(8,128)S(1)}, f32[1,8,64,128]{3,2,1,0:T(8,128)}, u32[]{:S(2)}) copy-start(f32[1,8,64,128]{3,2,1,0:T(8,128)} %param.10) | copy-start | bytes 786436
  2.4 23.1 %collective-permute-start = (f32[8,64,128]{2,1,0:T(8,128)S(1)}, f32[8,64,128]{2,1,0:T(8,128)S(1)}, u32[]{:S(2)}, u32[]{:S(2)}) collective-permute-start(f32[8,64,128]{2,1,0:T(8,128)S(1)} %get-tuple-element.15.after), channel_id=1, source_target_pairs={{1,2},{3,4},{5,6},{7,8},{9,10},{11,12},{13,14},{2,1},{4,3},{6,5},{... | collective-permute-start | bytes 786440 | tf_op jit(solution)/shard_map/ppermute | solution.py:355
  19.3 6.3 %collective-permute-start.1 = (f32[8,64,128]{2,1,0:T(8,128)S(1)}, f32[8,64,128]{2,1,0:T(8,128)S(1)}, u32[]{:S(2)}, u32[]{:S(2)}) collective-permute-start(f32[8,64,128]{2,1,0:T(8,128)S(1)} %get-tuple-element.16.other), channel_id=1, source_target_pairs={{0,1},{1,0},{2,3},{3,2},{4,5},{5,4},{6,7},{7,6},{8,9},{9,8},{10,11... | collective-permute-start | bytes 786440 | tf_op jit(solution)/shard_map/ppermute | solution.py:354
  21.2 0.7 copy-start.11
  21.2 0.7 copy-start.12
  21.2 0.7 copy-start.9
  21.3 0.7 copy-start.10
  23.3 0.6 copy-start.6
  24.0 1.6 %copy-start.8 = (s32[5]{0:T(128)}, s32[5]{0:T(128)S(1)}, u32[]{:S(2)}) copy-start(s32[5]{0:T(128)S(1)} %stack.19.where) | copy-start | bytes 64
  25.6 0.8 copy-start.7
  71.2 14.5 %all-to-all-start.1 = ((f32[16,32,128]{2,1,0:T(8,128)}), f32[16,32,128]{2,1,0:T(8,128)S(1)}, u32[]{:S(2)}, u32[]{:S(2)}) async-start(f32[16,32,128]{2,1,0:T(8,128)} %line_sums.1), calls=%async_computation.1 | async-start | bytes 524288 | tf_op jit(solution)/shard_map/all_to_all | solution.py:399

commit v6 on v5

--- a/solution.py
+++ b/solution.py
@@ -13,7 +13,7 @@
 TILE = ("y", "zh", "c")
 LINE = ("zl", "zh", "c")
 PLANE = ("x", "y")
-EDGE_ROWS = 8
+EDGE_ROWS = 7
 HIGHEST = lax.Precision.HIGHEST
 
 
@@ -42,7 +42,7 @@
     )
 
 
-def edge_kernel(sat, mob, pore, qx, qy, qz, far_out, near_out, s, m, p, x, y, z, in_sem):
+def edge_kernel(sat, mob, pore, qx, qy, qz, far_out, near_out, extra_out, s, m, p, x, y, z, in_sem):
     first_core = lax.axis_index("c") == 0
     loads = []
     for j, start in enumerate((0, 5)):
@@ -60,16 +60,17 @@
     f = [frac(s[i], m[i]) for i in range(3)]
     face_1 = across(x[1], f[0], f[1])
     flow_1 = frac(moved(s[1], p[1], across(x[2], f[1], f[2]) - face_1, f[1], z[1], y[1]), m[1])
-    down = [field[0] for field in (s, m, p, z, y, x)]
-    down += [face_1, jnp.minimum(x[1], 0.0) * flow_1]
+    down = [field[0] for field in (s, m, p, z, y)]
+    down += [face_1, x[0]]
     f = {i: frac(s[i], m[i]) for i in range(5, 8)}
     face_7 = across(x[7], f[6], f[7])
     flow_6 = frac(moved(s[6], p[6], face_7 - across(x[6], f[5], f[6]), f[6], z[6], y[6]), m[6])
     up = [field[7] for field in (s, m, p, z, y)]
-    up += [face_7, jnp.maximum(x[7], 0.0) * flow_6, jnp.zeros_like(face_7)]
+    up += [face_7, jnp.maximum(x[7], 0.0) * flow_6]
     for k in range(EDGE_ROWS):
         near_out[k] = jnp.where(first_core, up[k], down[k])
         far_out[k] = jnp.where(first_core, down[k], up[k])
+    extra_out[0] = jnp.minimum(x[1], 0.0) * flow_1
 
 
 OUTER = ((0, 7), (1, 6), (2, 5))
@@ -100,7 +101,7 @@
 
 
 def inside_kernel(
-    sat, mob, pore, qx, qy, qz, cell, well, factor, obs, after, other, mids, middle, early, hot, mask, weight
+    sat, mob, pore, qx, qy, qz, cell, well, factor, obs, after, other, third, mids, middle, early, hot, mask, weight
 ):
     rows, layers, columns = sat.shape
     count = cell.shape[1]
@@ -158,14 +159,17 @@
 
 
 def outside_kernel(
-    mob, pore, qx, qy, qz, far, near, mids, middle, early, hot, mask, weight, where, new_sat, shares
+    mob, pore, qx, qy, qz, far, near, extra, mids, middle, early, hot, mask, weight, where,
+    new_sat, shares, last_term, sem,
 ):
+    extra_copy = pltpu.make_async_copy(extra, last_term, sem)
+    extra_copy.start()
     tile = where[0]
     last = where[1]
     has_low = tile > 0
     has_high = tile < last
     first_core = where[4] == 0
-    low = [jnp.where(first_core, far[k], near[k]) for k in range(EDGE_ROWS - 1)]
+    low = [jnp.where(first_core, far[k], near[k]) for k in range(EDGE_ROWS)]
     high = [jnp.where(first_core, near[k], far[k]) for k in range(EDGE_ROWS)]
     below = jnp.where(has_low, low[0], 0.5)
     below_mob = jnp.where(has_low, low[1], 1.0)
@@ -173,7 +177,7 @@
     above_mob = jnp.where(has_high, high[1], 1.0)
     x = {i: qx[i] for i in range(1, 8)}
     x[0] = jnp.where(has_low, qx[0], 0.0)
-    x[8] = high[5]
+    x[8] = high[6]
     z = {i: qz[i] for i in (0, 1, 6, 7)}
     z[-1], z[8] = low[3], high[3]
     y = {i: qy[i] for i in (0, 1, 6, 7)}
@@ -185,13 +189,13 @@
 
     f = {-1: frac(below, below_mob), 0: mids[0], 7: mids[1], 8: frac(above, above_mob)}
     out_low = jnp.minimum(low[5], 0.0) / f[-1]
-    out_high = jnp.maximum(high[6], 0.0) / f[8]
+    out_high = jnp.maximum(high[5], 0.0) / f[8]
     face = {i: across(x[i], f[i - 1], f[i]) for i in (0, 8)}
     s = {
         -1: moved(below, p[-1], face[0] - low[5], f[-1], z[-1], y[-1]),
         0: mids[2] + p[0] * face[0],
         7: mids[3] - p[7] * face[8],
-        8: moved(above, p[8], high[6] - face[8], f[8], z[8], y[8]),
+        8: moved(above, p[8], high[5] - face[8], f[8], z[8], y[8]),
     }
 
     f = {i: frac(s[i], m[i]) for i in (-1, 0, 7, 8)}
@@ -199,7 +203,8 @@
     f[1], f[6] = mids[4], mids[5]
     face = {i: across(x[i], f[i - 1], f[i]) for i in (0, 1, 7, 8)}
     face[-1] = low[6] + out_low * f[-1]
-    face[9] = out_high * f[8] + high[7]
+    extra_copy.wait()
+    face[9] = out_high * f[8] + last_term[0]
     s = {i: moved(s[i], p[i], face[i + 1] - face[i], f[i], z[i], y[i]) for i in (-1, 0, 7, 8)}
     s[1] = mids[6] + p[1] * face[1]
     s[6] = mids[7] - p[6] * face[7]
@@ -302,6 +307,7 @@
 
 VMEM = pl.BlockSpec(memory_space=pltpu.VMEM)
 ANY = pl.BlockSpec(memory_space=pl.ANY)
+HBM = pl.BlockSpec(memory_space=pltpu.HBM)
 SMEM = pl.BlockSpec(memory_space=pltpu.SMEM)
 
 
@@ -341,18 +347,28 @@
             lax.axis_index("c"),
         ]
     ).astype(jnp.int32)
-    far_out, near_out = pl.pallas_call(
+    far_out, near_out, extra_out = pl.pallas_call(
         edge_kernel,
-        out_shape=(held(EDGE_ROWS, layers, columns),) * 2,
+        out_shape=(
+            held(EDGE_ROWS, layers, columns),
+            held(EDGE_ROWS, layers, columns),
+            held(1, layers, columns),
+        ),
         in_specs=[ANY] * 6,
-        out_specs=(VMEM, VMEM),
+        out_specs=(VMEM,) * 3,
         scratch_shapes=[pltpu.VMEM((rows, layers, columns), jnp.float32)] * 6
         + [pltpu.SemaphoreType.DMA((12,))],
         name="edges",
     )(*fields)
     pairs = [(i, i + 1) for i in range(1, tiles - 1, 2)]
-    near = lax.ppermute(near_out, TILE, [(i, i ^ 1) for i in range(tiles)])
-    far = lax.ppermute(far_out, TILE, pairs + [(j, i) for i, j in pairs])
+    far, near, extra = (
+        lax.ppermute(rows_out, TILE, moves)
+        for rows_out, moves in (
+            (far_out, pairs + [(j, i) for i, j in pairs]),
+            (near_out, [(i, i ^ 1) for i in range(tiles)]),
+            (extra_out, [(i + 1, i) for i in range(tiles - 1)]),
+        )
+    )
     wells = obs_error.shape[0] * tiles
     count = conn_cell.shape[0]
     sat, mob, pore, qx, qy, qz = fields
@@ -366,7 +382,7 @@
             shape(count, columns),
             shape(count, wells),
         ),
-        in_specs=[VMEM] * 10 + [ANY] * 2,
+        in_specs=[VMEM] * 10 + [ANY] * 3,
         out_specs=(VMEM,) * 6,
         compiler_params=pltpu.CompilerParams(vmem_limit_bytes=32 * 1024 * 1024),
         name="inside",
@@ -378,15 +394,20 @@
         obs_error.T,
         far_out,
         near_out,
+        extra_out,
     )
     new_saturation, shares = pl.pallas_call(
         outside_kernel,
         out_shape=(held(rows, layers, columns), held(128, wells)),
-        in_specs=[VMEM] * 13 + [SMEM],
+        in_specs=[VMEM] * 7 + [HBM] + [VMEM] * 6 + [SMEM],
         out_specs=(VMEM, VMEM),
+        scratch_shapes=[
+            pltpu.VMEM((1, layers, columns), jnp.float32),
+            pltpu.SemaphoreType.DMA,
+        ],
         compiler_params=pltpu.CompilerParams(vmem_limit_bytes=32 * 1024 * 1024),
         name="outside",
-    )(mob, pore, qx, qy, qz, far, near, mids, middle, early, hot, mask, weight, where)
+    )(mob, pore, qx, qy, qz, far, near, extra, mids, middle, early, hot, mask, weight, where)
     line = lax.all_to_all(shares.reshape(32, 4, wells), LINE, 0, 0)
     line = pltpu.with_memory_space_constraint(line.reshape(128, wells), pltpu.VMEM)
     (spreads,) = pl.pallas_call(

time: 87.6 us -> 87.7 us (level)
  blocking collectives: 42.5 us -> 30.3 us
  waiting for transfers between devices: 8.7 us -> 17.8 us
  starting transfers between devices: 25.4 us -> 27.7 us
    all_to_all x1, blocking collectives: 42.5 us -> 30.3 us  [body(): line = lax.all_to_all(shares.reshape(32, 4, wells), LINE, 0, 0)]
    ppermute x2 -> x3, waiting for transfers between devices: 1.57 us -> 10.7 us  [body(): lax.ppermute(rows_out, TILE, moves)]
    ppermute x2 -> x3, starting transfers between devices: 18.8 us -> 21.2 us  [body(): lax.ppermute(rows_out, TILE, moves)]
  transfers between devices with their start and end apart: 3 -> 4, of which waited for: 2 -> 2; matrix products, arithmetic and copies ran while one was open for 1% -> 1% of each run, Pallas kernels for 2% -> 2%
where the time goes in v6:
time: 87.7 us; the launch traced here: 87.3 us
  blocking collectives  30.3 us (35%)
  starting transfers between devices  27.7 us (32%)
  waiting for transfers between devices  17.8 us (20%)
  Pallas kernels  7.25 us (8%)
  local copies, waits for them, and re-layouts  3.39 us (4%)
    all_to_all x1, blocking collectives, body(): line = lax.all_to_all(shares.reshape(32, 4, wells), LINE, 0, 0)  30.3 us
    ppermute x3, starting transfers between devices, body(): lax.ppermute(rows_out, TILE, moves)  21.2 us
    ppermute x3, waiting for transfers between devices, body(): lax.ppermute(rows_out, TILE, moves)  10.7 us
    all_to_all x1, waiting for transfers between devices, body(): lax.all_to_all(spreads, PLANE, 0, 0)  7.12 us
    all_to_all x1, starting transfers between devices, body(): lax.all_to_all(spreads, PLANE, 0, 0)  6.52 us
    unnamed x27, local copies, waits for them, and re-layouts  3.3 us
    pallas_call x1, Pallas kernels, body(): pl.pallas_call(outside_kernel, out_shape=(held(rows, layers, columns), he...  1.86 us
  transfers between devices with their start and end apart: 4, of which 2 were waited for; matrix products, arithmetic and copies ran while one was open for 1% of the time, Pallas kernels for 2%

profile of v6, /device:TPU:1, one launch (start us, length us, event | category | flops | bytes accessed | tf_op | source)
XLA Modules:
  0.0 87.3 jit_solution(12306752395000983031)
XLA Ops:
  0.7 1.7 %edges.1 = (f32[7,64,128]{2,1,0:T(8,128)S(1)}, f32[7,64,128]{2,1,0:T(8,128)S(1)}, f32[1,64,128]{2,1,0:T(8,128)S(1)}) custom-call(f32[8,64,128]{2,1,0:T(8,128)} %bitcast.34, f32[8,64,128]{2,1,0:T(8,128)} %bitcast.19, f32[8,64,128]{2,1,0:T(8,128)} %bitcast.22, f32[8,64,128]{2,1,0:T(8,128)} %bitcast.25, f32[8,64,128]{2,1,0:T(8,128)} %bitcast.28, ...), custom_call_target="tpu_custom_call" | custom-call | tf_op jit(solution)/shard_map/edges/pallas_call | solution.py:350
  2.4 16.8 %collective-permute-start = (f32[7,64,128]{2,1,0:T(8,128)S(1)}, f32[7,64,128]{2,1,0:T(8,128)S(1)}, u32[]{:S(2)}, u32[]{:S(2)}) collective-permute-start(f32[7,64,128]{2,1,0:T(8,128)S(1)} %get-tuple-element.16.after), channel_id=1, source_target_pairs={{1,2},{3,4},{5,6},{7,8},{9,10},{11,12},{13,14},{2,1},{4,3},{6,5},{... | collective-permute-start | bytes 688136 | tf_op jit(solution)/shard_map/ppermute | solution.py:365
  19.3 1.9 %collective-permute-start.1 = (f32[7,64,128]{2,1,0:T(8,128)S(1)}, f32[7,64,128]{2,1,0:T(8,128)S(1)}, u32[]{:S(2)}, u32[]{:S(2)}) collective-permute-start(f32[7,64,128]{2,1,0:T(8,128)S(1)} %get-tuple-element.17.other), channel_id=1, source_target_pairs={{0,1},{1,0},{2,3},{3,2},{4,5},{5,4},{6,7},{7,6},{8,9},{9,8},{10,11... | collective-permute-start | bytes 688136 | tf_op jit(solution)/shard_map/ppermute | solution.py:365
  21.2 2.4 %collective-permute-start.2 = (f32[1,64,128]{2,1,0:T(8,128)S(1)}, f32[1,64,128]{2,1,0:T(8,128)S(1)}, u32[]{:S(2)}, u32[]{:S(2)}) collective-permute-start(f32[1,64,128]{2,1,0:T(8,128)S(1)} %get-tuple-element.18.third), channel_id=1, source_target_pairs={{1,0},{2,1},{3,2},{4,3},{5,4},{6,5},{7,6},{8,7},{9,8},{10,9},{11,1... | collective-permute-start | bytes 98312 | tf_op jit(solution)/shard_map/ppermute | solution.py:365
  23.6 0.0 copy-start.11
  23.6 0.0 copy-start.12
  23.7 0.0 copy-start.9
  23.7 0.6 copy-done.11
  24.3 0.0 copy-done.12
  24.3 0.0 copy-done.9
  24.3 0.0 copy-done.10
  24.4 1.3 %inside.1 = (f32[12,64,128]{2,1,0:T(8,128)S(1)}, f32[2,64,128]{2,1,0:T(8,128)S(1)}, f32[4,128]{1,0:T(4,128)S(1)}, bf16[256,384]{1,0:T(8,128)(2,1)S(1)}, f32[256,128]{1,0:T(8,128)S(1)}, /*index=5*/f32[256,128]{1,0:T(8,128)S(1)}) custom-call(f32[8,64,128]{2,1,0:T(8,128)S(1)} %bitcast.35, f32[8,64,128]{2,1,0:T(8,128)S(1)} %bitcast.20, ...), custom_call_target="tpu_custom_call" | custom-call | tf_op jit(solution)/shard_map/inside/pallas_call | solution.py:375
  25.7 0.1 stack.19.where
  25.8 10.7 %collective-permute-done.2.extra = f32[1,64,128]{2,1,0:T(8,128)S(1)} collective-permute-done((f32[1,64,128]{2,1,0:T(8,128)S(1)}, f32[1,64,128]{2,1,0:T(8,128)S(1)}, u32[]{:S(2)}, u32[]{:S(2)}) %collective-permute-start.2) | collective-permute-done | bytes 32800 | tf_op jit(solution)/shard_map/ppermute | solution.py:365
  36.5 0.6 copy-done.6
  37.1 0.8 copy-done.7
  37.9 1.9 %outside.1 = (f32[8,64,128]{2,1,0:T(8,128)S(1)}, f32[128,128]{1,0:T(8,128)S(1)}) custom-call(f32[8,64,128]{2,1,0:T(8,128)S(1)} %bitcast.21, f32[8,64,128]{2,1,0:T(8,128)S(1)} %bitcast.24, f32[8,64,128]{2,1,0:T(8,128)S(1)} %bitcast.27, f32[8,64,128]{2,1,0:T(8,128)S(1)} %bitcast.30, f32[8,64,128]{2,1,0:T(8,128)S(1)} %bitcast.33, ...), custom_call_target="tpu_custom_call" | custom-call | tf_op jit(solution)/shard_map/outside/pallas_call | solution.py:399
  39.7 0.6 copy-done.8
  40.3 30.3 %all_to_all.10 = f32[32,4,128]{2,1,0:T(4,128)S(1)} all-to-all(f32[32,4,128]{2,1,0:T(4,128)S(1)} %bitcast.37), channel_id=1, replica_groups=mesh['x'=4,'zl'=8,'y'=4,'zh'=2,'c'=2] {'zl','zh','c'}, dimensions={0} | all-to-all | bytes 131072 | tf_op jit(solution)/shard_map/all_to_all | solution.py:411
  70.6 0.7 line_sums.1
  71.3 6.5 %all-to-all-start.1 = ((f32[16,32,128]{2,1,0:T(8,128)}), f32[16,32,128]{2,1,0:T(8,128)S(1)}, u32[]{:S(2)}, u32[]{:S(2)}) async-start(f32[16,32,128]{2,1,0:T(8,128)} %line_sums.1), calls=%async_computation.1 | async-start | bytes 524288 | tf_op jit(solution)/shard_map/all_to_all | solution.py:420
  77.8 0.7 copy.13
  78.5 7.1 %all-to-all-done.1.parts = f32[16,32,128]{2,1,0:T(8,128)S(1)} async-done(((f32[16,32,128]{2,1,0:T(8,128)}), f32[16,32,128]{2,1,0:T(8,128)S(1)}, u32[]{:S(2)}, u32[]{:S(2)}) %all-to-all-start.1) | async-done | bytes 262176 | tf_op jit(solution)/shard_map/all_to_all | solution.py:420
  85.7 1.6 %gram_row.1 = (f32[3,1,8]{2,1,0:T(1,128)}, f32[1,32]{1,0:T(1,128)}) custom-call(f32[16,32,128]{2,1,0:T(8,128)S(1)} %all-to-all-done.1.parts, s32[5]{0:T(128)} %copy-done.8), custom_call_target="tpu_custom_call" | custom-call | tf_op jit(solution)/shard_map/gram_row/pallas_call | solution.py:421
  (18 shorter events, 0.0 us)
Async XLA Ops:
  0.6 23.1 %copy-start = (f32[1,8,64,128]{3,2,1,0:T(8,128)S(1)}, f32[1,8,64,128]{3,2,1,0:T(8,128)}, u32[]{:S(2)}) copy-start(f32[1,8,64,128]{3,2,1,0:T(8,128)} %param.11) | copy-start | bytes 786436
  0.6 23.1 %copy-start.1 = (f32[1,8,64,128]{3,2,1,0:T(8,128)S(1)}, f32[1,8,64,128]{3,2,1,0:T(8,128)}, u32[]{:S(2)}) copy-start(f32[1,8,64,128]{3,2,1,0:T(8,128)} %param.12) | copy-start | bytes 786436
  0.7 23.1 %copy-start.2 = (f32[1,8,64,128]{3,2,1,0:T(8,128)S(1)}, f32[1,8,64,128]{3,2,1,0:T(8,128)}, u32[]{:S(2)}) copy-start(f32[1,8,64,128]{3,2,1,0:T(8,128)} %param.13) | copy-start | bytes 786436
  0.7 23.1 %copy-start.3 = (f32[1,8,64,128]{3,2,1,0:T(8,128)S(1)}, f32[1,8,64,128]{3,2,1,0:T(8,128)}, u32[]{:S(2)}) copy-start(f32[1,8,64,128]{3,2,1,0:T(8,128)} %param.14) | copy-start | bytes 786436
  0.7 23.1 %copy-start.4 = (f32[1,8,64,128]{3,2,1,0:T(8,128)S(1)}, f32[1,8,64,128]{3,2,1,0:T(8,128)}, u32[]{:S(2)}) copy-start(f32[1,8,64,128]{3,2,1,0:T(8,128)} %param.15) | copy-start | bytes 786436
  0.7 23.1 %copy-start.5 = (f32[1,8,64,128]{3,2,1,0:T(8,128)S(1)}, f32[1,8,64,128]{3,2,1,0:T(8,128)}, u32[]{:S(2)}) copy-start(f32[1,8,64,128]{3,2,1,0:T(8,128)} %param.10) | copy-start | bytes 786436
  2.4 34.6 %collective-permute-start = (f32[7,64,128]{2,1,0:T(8,128)S(1)}, f32[7,64,128]{2,1,0:T(8,128)S(1)}, u32[]{:S(2)}, u32[]{:S(2)}) collective-permute-start(f32[7,64,128]{2,1,0:T(8,128)S(1)} %get-tuple-element.16.after), channel_id=1, source_target_pairs={{1,2},{3,4},{5,6},{7,8},{9,10},{11,12},{13,14},{2,1},{4,3},{6,5},{... | collective-permute-start | bytes 688136 | tf_op jit(solution)/shard_map/ppermute | solution.py:365
  19.3 17.8 %collective-permute-start.1 = (f32[7,64,128]{2,1,0:T(8,128)S(1)}, f32[7,64,128]{2,1,0:T(8,128)S(1)}, u32[]{:S(2)}, u32[]{:S(2)}) collective-permute-start(f32[7,64,128]{2,1,0:T(8,128)S(1)} %get-tuple-element.17.other), channel_id=1, source_target_pairs={{0,1},{1,0},{2,3},{3,2},{4,5},{5,4},{6,7},{7,6},{8,9},{9,8},{10,11... | collective-permute-start | bytes 688136 | tf_op jit(solution)/shard_map/ppermute | solution.py:365
  21.2 15.3 %collective-permute-start.2 = (f32[1,64,128]{2,1,0:T(8,128)S(1)}, f32[1,64,128]{2,1,0:T(8,128)S(1)}, u32[]{:S(2)}, u32[]{:S(2)}) collective-permute-start(f32[1,64,128]{2,1,0:T(8,128)S(1)} %get-tuple-element.18.third), channel_id=1, source_target_pairs={{1,0},{2,1},{3,2},{4,3},{5,4},{6,5},{7,6},{8,7},{9,8},{10,9},{11,1... | collective-permute-start | bytes 98312 | tf_op jit(solution)/shard_map/ppermute | solution.py:365
  23.6 0.7 copy-start.11
  23.6 0.7 copy-start.12
  23.7 0.7 copy-start.9
  23.7 0.7 copy-start.10
  36.5 0.6 copy-start.6
  37.1 0.8 copy-start.7
  39.7 0.6 copy-start.8
  71.3 14.4 %all-to-all-start.1 = ((f32[16,32,128]{2,1,0:T(8,128)}), f32[16,32,128]{2,1,0:T(8,128)S(1)}, u32[]{:S(2)}, u32[]{:S(2)}) async-start(f32[16,32,128]{2,1,0:T(8,128)} %line_sums.1), calls=%async_computation.1 | async-start | bytes 524288 | tf_op jit(solution)/shard_map/all_to_all | solution.py:420

commit v7 on v4

--- a/solution.py
+++ b/solution.py
@@ -55,7 +55,7 @@
             )
     for load in loads:
         load.start()
-    for load in loads[:6]:
+    for load in loads:
         load.wait()
     f = [frac(s[i], m[i]) for i in range(3)]
     face_1 = across(x[1], f[0], f[1])
@@ -64,8 +64,6 @@
         down[k] = near[0]
     down[6] = face_1
     down[7] = jnp.minimum(x[1], 0.0) * flow_1
-    for load in loads[6:]:
-        load.wait()
     f = {i: frac(s[i], m[i]) for i in range(5, 8)}
     face_7 = across(x[7], f[6], f[7])
     flow_6 = frac(moved(s[6], p[6], face_7 - across(x[6], f[5], f[6]), f[6], z[6], y[6]), m[6])
@@ -380,13 +378,14 @@
         name="outside",
     )(mob, pore, qx, qy, qz, low, high, mids, middle, early, hot, mask, weight, where)
     line = lax.all_to_all(shares.reshape(32, 4, wells), LINE, 0, 0)
+    line = pltpu.with_memory_space_constraint(line.reshape(128, wells), pltpu.VMEM)
     (spreads,) = pl.pallas_call(
         line_kernel,
         out_shape=(held(16, 32, wells),),
         in_specs=[VMEM],
         out_specs=(VMEM,),
         name="line_sums",
-    )(line.reshape(128, wells))
+    )(line)
     plane = pltpu.with_memory_space_constraint(lax.all_to_all(spreads, PLANE, 0, 0), pltpu.VMEM)
     rates, gram = pl.pallas_call(
         gram_kernel,

time: 86.1 us -> 85.2 us (0.990)
  no operation moved by 1% of the time
where the time goes in v7:
time: 85.2 us; the launch traced here: 84.8 us
  blocking collectives  28 us (33%)
  starting transfers between devices  26.1 us (31%)
  waiting for transfers between devices  21.6 us (25%)
  Pallas kernels  6.91 us (8%)
  local copies, waits for them, and re-layouts  1.37 us (2%)
    all_to_all x1, blocking collectives, body(): line = lax.all_to_all(shares.reshape(32, 4, wells), LINE, 0, 0)  28 us
    ppermute x1, waiting for transfers between devices, body(): low = lax.ppermute(up, TILE, [(i, i + 1) for i in range(tiles - 1)])  14.4 us
    ppermute x1, starting transfers between devices, body(): low = lax.ppermute(up, TILE, [(i, i + 1) for i in range(tiles - 1)])  9.97 us
    ppermute x1, starting transfers between devices, body(): high = lax.ppermute(down, TILE, [(i + 1, i) for i in range(tiles - 1)])  8.79 us
    all_to_all x1, starting transfers between devices, body(): lax.all_to_all(spreads, PLANE, 0, 0)  7.38 us
    all_to_all x1, waiting for transfers between devices, body(): lax.all_to_all(spreads, PLANE, 0, 0)  7.12 us
    pallas_call x1, Pallas kernels, body(): pl.pallas_call(edge_kernel, out_shape=(held(UP_ROWS, layers, columns), he...  1.74 us
  transfers between devices with their start and end apart: 3, of which 2 were waited for; matrix products, arithmetic and copies ran while one was open for 1% of the time, Pallas kernels for 2%

profile of v7, /device:TPU:1, one launch (start us, length us, event | category | flops | bytes accessed | tf_op | source)
XLA Modules:
  0.0 84.8 jit_solution(8496711700663586927)
XLA Ops:
  0.6 0.0 copy-start
  0.7 1.7 %edges.1 = (f32[7,64,128]{2,1,0:T(8,128)S(1)}, f32[8,64,128]{2,1,0:T(8,128)S(1)}) custom-call(f32[8,64,128]{2,1,0:T(8,128)} %bitcast.33, f32[8,64,128]{2,1,0:T(8,128)} %bitcast.18, f32[8,64,128]{2,1,0:T(8,128)} %bitcast.21, f32[8,64,128]{2,1,0:T(8,128)} %bitcast.24, f32[8,64,128]{2,1,0:T(8,128)} %bitcast.27, f32[8,64,128]{2,1,0:T(8,128)} %bitcast.30), custom_call_target="tpu_custom_call" | custom-call | tf_op jit(solution)/shard_map/edges/pallas_call | solution.py:336
  2.4 8.8 %collective-permute-start.1 = (f32[8,64,128]{2,1,0:T(8,128)S(1)}, f32[8,64,128]{2,1,0:T(8,128)S(1)}, u32[]{:S(2)}, u32[]{:S(2)}) collective-permute-start(f32[8,64,128]{2,1,0:T(8,128)S(1)} %get-tuple-element.16), channel_id=1, source_target_pairs={{1,0},{2,1},{3,2},{4,3},{5,4},{6,5},{7,6},{8,7},{9,8},{10,9},{11,1... | collective-permute-start | bytes 786440 | tf_op jit(solution)/shard_map/ppermute | solution.py:346
  11.2 10.0 %collective-permute-start = (f32[7,64,128]{2,1,0:T(8,128)S(1)}, f32[7,64,128]{2,1,0:T(8,128)S(1)}, u32[]{:S(2)}, u32[]{:S(2)}) collective-permute-start(f32[7,64,128]{2,1,0:T(8,128)S(1)} %get-tuple-element.15.after), channel_id=1, source_target_pairs={{0,1},{1,2},{2,3},{3,4},{4,5},{5,6},{6,7},{7,8},{8,9},{9,10},{10,1... | collective-permute-start | bytes 688136 | tf_op jit(solution)/shard_map/ppermute | solution.py:345
  21.2 0.0 copy-start.9
  21.2 0.0 copy-start.10
  21.2 0.0 copy-start.7
  21.3 0.0 copy-start.8
  21.3 0.6 copy-done.9
  21.9 0.0 copy-done.10
  21.9 0.0 copy-done.7
  21.9 0.0 copy-done.8
  22.0 1.4 %inside.1 = (f32[12,64,128]{2,1,0:T(8,128)S(1)}, f32[2,64,128]{2,1,0:T(8,128)S(1)}, f32[4,128]{1,0:T(4,128)S(1)}, bf16[256,384]{1,0:T(8,128)(2,1)S(1)}, f32[256,128]{1,0:T(8,128)S(1)}, /*index=5*/f32[256,128]{1,0:T(8,128)S(1)}) custom-call(f32[8,64,128]{2,1,0:T(8,128)S(1)} %bitcast.34, f32[8,64,128]{2,1,0:T(8,128)S(1)} %bitcast.19, ...), custom_call_target="tpu_custom_call" | custom-call | tf_op jit(solution)/shard_map/inside/pallas_call | solution.py:350
  23.3 0.1 pad_add_fusion.where
  23.4 14.4 %collective-permute-done.low = f32[7,64,128]{2,1,0:T(8,128)S(1)} collective-permute-done((f32[7,64,128]{2,1,0:T(8,128)S(1)}, f32[7,64,128]{2,1,0:T(8,128)S(1)}, u32[]{:S(2)}, u32[]{:S(2)}) %collective-permute-start) | collective-permute-done | bytes 229408 | tf_op jit(solution)/shard_map/ppermute | solution.py:345
  37.8 0.0 collective-permute-done.1.high
  37.8 0.0 copy-done.6
  37.8 1.5 %outside.1 = (f32[8,64,128]{2,1,0:T(8,128)S(1)}, f32[128,128]{1,0:T(8,128)S(1)}) custom-call(f32[8,64,128]{2,1,0:T(8,128)S(1)} %bitcast.20, f32[8,64,128]{2,1,0:T(8,128)S(1)} %bitcast.23, f32[8,64,128]{2,1,0:T(8,128)S(1)} %bitcast.26, f32[8,64,128]{2,1,0:T(8,128)S(1)} %bitcast.29, f32[8,64,128]{2,1,0:T(8,128)S(1)} %bitcast.32, ...), custom_call_target="tpu_custom_call" | custom-call | tf_op jit(solution)/shard_map/outside/pallas_call | solution.py:372
  39.3 28.0 %all_to_all.10 = f32[32,4,128]{2,1,0:T(4,128)S(1)} all-to-all(f32[32,4,128]{2,1,0:T(4,128)S(1)} %bitcast.36), channel_id=1, replica_groups=mesh['x'=4,'zl'=8,'y'=4,'zh'=2,'c'=2] {'zl','zh','c'}, dimensions={0} | all-to-all | bytes 131072 | tf_op jit(solution)/shard_map/all_to_all | solution.py:380
  67.3 0.7 line_sums.1
  68.0 7.4 %all-to-all-start.1 = ((f32[16,32,128]{2,1,0:T(8,128)}), f32[16,32,128]{2,1,0:T(8,128)S(1)}, u32[]{:S(2)}, u32[]{:S(2)}) async-start(f32[16,32,128]{2,1,0:T(8,128)} %line_sums.1), calls=%async_computation.1 | async-start | bytes 524288 | tf_op jit(solution)/shard_map/all_to_all | solution.py:389
  75.4 0.7 copy.13
  76.1 7.1 %all-to-all-done.1.parts = f32[16,32,128]{2,1,0:T(8,128)S(1)} async-done(((f32[16,32,128]{2,1,0:T(8,128)}), f32[16,32,128]{2,1,0:T(8,128)S(1)}, u32[]{:S(2)}, u32[]{:S(2)}) %all-to-all-start.1) | async-done | bytes 262176 | tf_op jit(solution)/shard_map/all_to_all | solution.py:389
  83.3 1.6 %gram_row.1 = (f32[3,1,8]{2,1,0:T(1,128)}, f32[1,32]{1,0:T(1,128)}) custom-call(f32[16,32,128]{2,1,0:T(8,128)S(1)} %all-to-all-done.1.parts, s32[4]{0:T(128)} %copy-done.6), custom_call_target="tpu_custom_call" | custom-call | tf_op jit(solution)/shard_map/gram_row/pallas_call | solution.py:390
  (12 shorter events, 0.0 us)
Async XLA Ops:
  0.6 20.6 %copy-start = (f32[1,8,64,128]{3,2,1,0:T(8,128)S(1)}, f32[1,8,64,128]{3,2,1,0:T(8,128)}, u32[]{:S(2)}) copy-start(f32[1,8,64,128]{3,2,1,0:T(8,128)} %param.11) | copy-start | bytes 786436
  0.6 20.6 %copy-start.1 = (f32[1,8,64,128]{3,2,1,0:T(8,128)S(1)}, f32[1,8,64,128]{3,2,1,0:T(8,128)}, u32[]{:S(2)}) copy-start(f32[1,8,64,128]{3,2,1,0:T(8,128)} %param.12) | copy-start | bytes 786436
  0.7 20.6 %copy-start.2 = (f32[1,8,64,128]{3,2,1,0:T(8,128)S(1)}, f32[1,8,64,128]{3,2,1,0:T(8,128)}, u32[]{:S(2)}) copy-start(f32[1,8,64,128]{3,2,1,0:T(8,128)} %param.13) | copy-start | bytes 786436
  0.7 20.6 %copy-start.3 = (f32[1,8,64,128]{3,2,1,0:T(8,128)S(1)}, f32[1,8,64,128]{3,2,1,0:T(8,128)}, u32[]{:S(2)}) copy-start(f32[1,8,64,128]{3,2,1,0:T(8,128)} %param.14) | copy-start | bytes 786436
  0.7 20.6 %copy-start.4 = (f32[1,8,64,128]{3,2,1,0:T(8,128)S(1)}, f32[1,8,64,128]{3,2,1,0:T(8,128)}, u32[]{:S(2)}) copy-start(f32[1,8,64,128]{3,2,1,0:T(8,128)} %param.15) | copy-start | bytes 786436
  0.7 20.6 %copy-start.5 = (f32[1,8,64,128]{3,2,1,0:T(8,128)S(1)}, f32[1,8,64,128]{3,2,1,0:T(8,128)}, u32[]{:S(2)}) copy-start(f32[1,8,64,128]{3,2,1,0:T(8,128)} %param.10) | copy-start | bytes 786436
  2.4 35.4 %collective-permute-start.1 = (f32[8,64,128]{2,1,0:T(8,128)S(1)}, f32[8,64,128]{2,1,0:T(8,128)S(1)}, u32[]{:S(2)}, u32[]{:S(2)}) collective-permute-start(f32[8,64,128]{2,1,0:T(8,128)S(1)} %get-tuple-element.16), channel_id=1, source_target_pairs={{1,0},{2,1},{3,2},{4,3},{5,4},{6,5},{7,6},{8,7},{9,8},{10,9},{11,1... | collective-permute-start | bytes 786440 | tf_op jit(solution)/shard_map/ppermute | solution.py:346
  11.2 26.6 %collective-permute-start = (f32[7,64,128]{2,1,0:T(8,128)S(1)}, f32[7,64,128]{2,1,0:T(8,128)S(1)}, u32[]{:S(2)}, u32[]{:S(2)}) collective-permute-start(f32[7,64,128]{2,1,0:T(8,128)S(1)} %get-tuple-element.15.after), channel_id=1, source_target_pairs={{0,1},{1,2},{2,3},{3,4},{4,5},{5,6},{6,7},{7,8},{8,9},{9,10},{10,1... | collective-permute-start | bytes 688136 | tf_op jit(solution)/shard_map/ppermute | solution.py:345
  21.2 0.7 copy-start.9
  21.2 0.7 copy-start.10
  21.2 0.7 copy-start.7
  21.3 0.7 copy-start.8
  23.4 14.4 %copy-start.6 = (s32[4]{0:T(128)}, s32[4]{0:T(128)S(1)}, u32[]{:S(2)}) copy-start(s32[4]{0:T(128)S(1)} %pad_add_fusion.where) | copy-start | bytes 52
  68.0 15.2 %all-to-all-start.1 = ((f32[16,32,128]{2,1,0:T(8,128)}), f32[16,32,128]{2,1,0:T(8,128)S(1)}, u32[]{:S(2)}, u32[]{:S(2)}) async-start(f32[16,32,128]{2,1,0:T(8,128)} %line_sums.1), calls=%async_computation.1 | async-start | bytes 524288 | tf_op jit(solution)/shard_map/all_to_all | solution.py:389

commit v8 on v7

--- a/solution.py
+++ b/solution.py
@@ -43,19 +43,18 @@
     )
 
 
-def edge_kernel(sat, mob, pore, qx, qy, qz, up, down, s, m, p, x, y, z, in_sem):
+def edge_kernel(sat, mob, pore, qx, qy, qz, up, down, s, m, p, x, y, z, sem):
+    pieces = ((0, 3), (5, 3), (3, 2))
     loads = []
-    for j, start in enumerate((0, 5)):
+    for j, (start, size) in enumerate(pieces):
         for k, (field, near) in enumerate(
             ((sat, s), (mob, m), (qx, x), (qy, y), (qz, z), (pore, p))
         ):
-            part = pl.ds(start, 3)
-            loads.append(
-                pltpu.make_async_copy(field.at[part], near.at[part], in_sem.at[6 * j + k])
-            )
+            part = pl.ds(start, size)
+            loads.append(pltpu.make_async_copy(field.at[part], near.at[part], sem.at[6 * j + k]))
     for load in loads:
         load.start()
-    for load in loads:
+    for load in loads[:12]:
         load.wait()
     f = [frac(s[i], m[i]) for i in range(3)]
     face_1 = across(x[1], f[0], f[1])
@@ -71,6 +70,8 @@
         up[k] = near[7]
     up[5] = face_7
     up[6] = jnp.maximum(x[7], 0.0) * flow_6
+    for load in loads[12:]:
+        load.wait()
 
 
 OUTER = ((0, 7), (1, 6), (2, 5))
@@ -90,11 +91,10 @@
     stack = jnp.concatenate(flows, axis=0)
     big = stack.astype(jnp.bfloat16)
     rest = stack - big.astype(jnp.float32)
-    middle = rest.astype(jnp.bfloat16)
-    small = (rest - middle.astype(jnp.float32)).astype(jnp.bfloat16)
+    small = rest.astype(jnp.bfloat16)
     found = mask * sum(
         jnp.dot(hot[:, : stack.shape[0]], part, preferred_element_type=jnp.float32)
-        for part in (small, middle, big)
+        for part in (small, big)
     )
     picked = jnp.sum(found, axis=1, keepdims=True)
     return jnp.sum(weight * picked, axis=0, keepdims=True)
@@ -267,35 +267,28 @@
     own = sums[0]
     for g in range(1, groups):
         own = jnp.where(own_x == g, sums[g], own)
-    mask_z = lax.broadcasted_iota(jnp.int32, (layer, wells), 0) == own_z
+    lane = lax.broadcasted_iota(jnp.int32, (layer, wells), 1)
+    sublane = lax.broadcasted_iota(jnp.int32, (layer, wells), 0)
+    products = [jnp.zeros((layer, wells), jnp.float32)] * groups
     own_rates = []
-    own_centered = []
-    centered = []
     for k in range(SUBSTEPS):
         part = slice(k * layer, (k + 1) * layer)
         data = [total[part] / errors[k] for total in sums]
         mean = jnp.sum(data[0] + data[1] + data[2] + data[3], axis=0, keepdims=True) / ensemble
-        centered.append(jnp.concatenate([d - mean for d in data], axis=0))
-        row = jnp.sum(jnp.where(mask_z, own[part], 0.0), axis=0, keepdims=True)
+        row = jnp.sum(jnp.where(sublane == own_z, own[part], 0.0), axis=0, keepdims=True)
         own_rates.append(row)
-        own_centered.append(row / errors[k] - mean)
-    gram[...] = lax.dot_general(
-        jnp.concatenate(own_centered, axis=1),
-        jnp.concatenate(centered, axis=1),
-        (((1,), (1,)), ((), ())),
-        precision=HIGHEST,
-        preferred_element_type=jnp.float32,
-    ) / (ensemble - 1.0)
-    select = (
-        lax.broadcasted_iota(jnp.int32, (mine, wells), 1)
-        == lax.broadcasted_iota(jnp.int32, (mine, wells), 0) + tile * mine
-    ).astype(jnp.float32)
-    chosen = lax.dot_general(
-        jnp.concatenate(own_rates, axis=0), select, (((1,), (1,)), ((), ())), precision=HIGHEST,
-        preferred_element_type=jnp.float32,
-    )
+        centered = row / errors[k] - mean
+        products = [total + (d - mean) * centered for total, d in zip(products, data)]
+    line = jnp.zeros((layer, wells), jnp.float32)
+    for g in range(groups):
+        dots = jnp.sum(products[g], axis=1, keepdims=True)
+        line = line + jnp.where(lane == sublane + g * layer, dots, 0.0)
+    line = jnp.sum(line, axis=0, keepdims=True) / (ensemble - 1.0)
+    gram[...] = line[:, :ensemble]
+    front = jnp.concatenate(own_rates + [jnp.zeros((layer - SUBSTEPS, wells), jnp.float32)], axis=0)
+    front = pltpu.roll(front, lax.rem(wells - tile * mine, wells), 1)
     for k in range(SUBSTEPS):
-        rates_out[k] = chosen[k : k + 1]
+        rates_out[k] = front[k : k + 1, :mine]
 
 
 VMEM = pl.BlockSpec(memory_space=pltpu.VMEM)
@@ -333,13 +326,13 @@
     where = jnp.stack(
         [tile, jnp.full_like(tile, tiles - 1), lax.axis_index("x"), lax.axis_index("zl")]
     ).astype(jnp.int32)
-    up, down = pl.pallas_call(
+    up, down, *fields = pl.pallas_call(
         edge_kernel,
-        out_shape=(held(UP_ROWS, layers, columns), held(DOWN_ROWS, layers, columns)),
+        out_shape=(held(UP_ROWS, layers, columns), held(DOWN_ROWS, layers, columns))
+        + (held(rows, layers, columns),) * 6,
         in_specs=[ANY] * 6,
-        out_specs=(VMEM, VMEM),
-        scratch_shapes=[pltpu.VMEM((rows, layers, columns), jnp.float32)] * 6
-        + [pltpu.SemaphoreType.DMA((12,))],
+        out_specs=(VMEM,) * 8,
+        scratch_shapes=[pltpu.SemaphoreType.DMA((18,))],
         name="edges",
     )(*fields)
     low = lax.ppermute(up, TILE, [(i, i + 1) for i in range(tiles - 1)])

time: 85.2 us -> 84.8 us (level)
  no operation moved by 1% of the time
where the time goes in v8:
time: 84.8 us; the launch traced here: 84.5 us
  blocking collectives  28 us (33%)
  starting transfers between devices  26.1 us (31%)
  waiting for transfers between devices  21.5 us (25%)
  Pallas kernels  6.68 us (8%)
  local copies, waits for them, and re-layouts  1.41 us (2%)
    all_to_all x1, blocking collectives, body(): line = lax.all_to_all(shares.reshape(32, 4, wells), LINE, 0, 0)  28 us
    ppermute x1, waiting for transfers between devices, body(): low = lax.ppermute(up, TILE, [(i, i + 1) for i in range(tiles - 1)])  14.4 us
    ppermute x1, starting transfers between devices, body(): low = lax.ppermute(up, TILE, [(i, i + 1) for i in range(tiles - 1)])  9.97 us
    ppermute x1, starting transfers between devices, body(): high = lax.ppermute(down, TILE, [(i + 1, i) for i in range(tiles - 1)])  8.79 us
    all_to_all x1, starting transfers between devices, body(): lax.all_to_all(spreads, PLANE, 0, 0)  7.38 us
    all_to_all x1, waiting for transfers between devices, body(): lax.all_to_all(spreads, PLANE, 0, 0)  7.12 us
    pallas_call x1, Pallas kernels, body(): pl.pallas_call(edge_kernel, out_shape=(held(UP_ROWS, layers, columns), he...  1.71 us
  transfers between devices with their start and end apart: 3, of which 2 were waited for; matrix products, arithmetic and copies ran while one was open for 1% of the time, Pallas kernels for 2%

profile of v8, /device:TPU:1, one launch (start us, length us, event | category | flops | bytes accessed | tf_op | source)
XLA Modules:
  0.0 84.5 jit_solution(4316237745551621400)
XLA Ops:
  0.6 1.7 %edges.1 = (f32[7,64,128]{2,1,0:T(8,128)S(1)}, f32[8,64,128]{2,1,0:T(8,128)S(1)}, f32[8,64,128]{2,1,0:T(8,128)S(1)}, f32[8,64,128]{2,1,0:T(8,128)S(1)}, f32[8,64...) custom-call(f32[8,64,128]{2,1,0:T(8,128)} %bitcast.24, ...), custom_call_target="tpu_custom_call" | custom-call | tf_op jit(solution)/shard_map/edges/pallas_call | solution.py:329
  2.3 8.8 %collective-permute-start.1 = (f32[8,64,128]{2,1,0:T(8,128)S(1)}, f32[8,64,128]{2,1,0:T(8,128)S(1)}, u32[]{:S(2)}, u32[]{:S(2)}) collective-permute-start(f32[8,64,128]{2,1,0:T(8,128)S(1)} %get-tuple-element.27), channel_id=1, source_target_pairs={{1,0},{2,1},{3,2},{4,3},{5,4},{6,5},{7,6},{8,7},{9,8},{10,9},{11,1... | collective-permute-start | bytes 786440 | tf_op jit(solution)/shard_map/ppermute | solution.py:339
  11.1 10.0 %collective-permute-start = (f32[7,64,128]{2,1,0:T(8,128)S(1)}, f32[7,64,128]{2,1,0:T(8,128)S(1)}, u32[]{:S(2)}, u32[]{:S(2)}) collective-permute-start(f32[7,64,128]{2,1,0:T(8,128)S(1)} %get-tuple-element.26.after), channel_id=1, source_target_pairs={{0,1},{1,2},{2,3},{3,4},{4,5},{5,6},{6,7},{7,8},{8,9},{9,10},{10,1... | collective-permute-start | bytes 688136 | tf_op jit(solution)/shard_map/ppermute | solution.py:338
  21.1 0.0 copy-start.3
  21.1 0.0 copy-start.4
  21.2 0.0 copy-start.1
  21.2 0.0 copy-start.2
  21.2 0.6 copy-done.3
  21.8 0.0 copy-done.4
  21.8 0.0 copy-done.1
  21.8 0.0 copy-done.2
  21.9 1.4 %inside.1 = (f32[12,64,128]{2,1,0:T(8,128)S(1)}, f32[2,64,128]{2,1,0:T(8,128)S(1)}, f32[4,128]{1,0:T(4,128)S(1)}, bf16[256,384]{1,0:T(8,128)(2,1)S(1)}, f32[256,128]{1,0:T(8,128)S(1)}, /*index=5*/f32[256,128]{1,0:T(8,128)S(1)}) custom-call(f32[8,64,128]{2,1,0:T(8,128)S(1)} %get-tuple-element.28.sat, f32[8,64,128]{2,1,0:T(8,128)S(1)} %get-tuple-element.21.mob, ...), custom_call_target="tpu_custom_call" | custom-call | tf_op jit(solution)/shard_map/inside/pallas_call | solution.py:343
  23.3 0.1 pad_add_fusion.where
  23.3 0.0 copy-start
  23.3 14.4 %collective-permute-done.low = f32[7,64,128]{2,1,0:T(8,128)S(1)} collective-permute-done((f32[7,64,128]{2,1,0:T(8,128)S(1)}, f32[7,64,128]{2,1,0:T(8,128)S(1)}, u32[]{:S(2)}, u32[]{:S(2)}) %collective-permute-start) | collective-permute-done | bytes 229408 | tf_op jit(solution)/shard_map/ppermute | solution.py:338
  37.7 0.0 collective-permute-done.1.high
  37.7 0.0 copy-done
  37.7 1.4 %outside.1 = (f32[8,64,128]{2,1,0:T(8,128)S(1)}, f32[128,128]{1,0:T(8,128)S(1)}) custom-call(f32[8,64,128]{2,1,0:T(8,128)S(1)} %get-tuple-element.21.mob, f32[8,64,128]{2,1,0:T(8,128)S(1)} %get-tuple-element.22.pore, f32[8,64,128]{2,1,0:T(8,128)S(1)} %get-tuple-element.23.qx, f32[8,64,128]{2,1,0:T(8,128)S(1)} %get-tuple-element.24.qy, ...), custom_call_target="tpu_custom_call" | custom-call | tf_op jit(solution)/shard_map/outside/pallas_call | solution.py:365
  39.1 28.0 %all_to_all.10 = f32[32,4,128]{2,1,0:T(4,128)S(1)} all-to-all(f32[32,4,128]{2,1,0:T(4,128)S(1)} %bitcast.19), channel_id=1, replica_groups=mesh['x'=4,'zl'=8,'y'=4,'zh'=2,'c'=2] {'zl','zh','c'}, dimensions={0} | all-to-all | bytes 131072 | tf_op jit(solution)/shard_map/all_to_all | solution.py:373
  67.1 0.7 line_sums.1
  67.8 7.4 %all-to-all-start.1 = ((f32[16,32,128]{2,1,0:T(8,128)}), f32[16,32,128]{2,1,0:T(8,128)S(1)}, u32[]{:S(2)}, u32[]{:S(2)}) async-start(f32[16,32,128]{2,1,0:T(8,128)} %line_sums.1), calls=%async_computation.1 | async-start | bytes 524288 | tf_op jit(solution)/shard_map/all_to_all | solution.py:382
  75.2 0.7 copy.13
  75.9 7.1 %all-to-all-done.1.parts = f32[16,32,128]{2,1,0:T(8,128)S(1)} async-done(((f32[16,32,128]{2,1,0:T(8,128)}), f32[16,32,128]{2,1,0:T(8,128)S(1)}, u32[]{:S(2)}, u32[]{:S(2)}) %all-to-all-start.1) | async-done | bytes 262176 | tf_op jit(solution)/shard_map/all_to_all | solution.py:382
  83.0 1.5 %gram_row.1 = (f32[3,1,8]{2,1,0:T(1,128)}, f32[1,32]{1,0:T(1,128)}) custom-call(f32[16,32,128]{2,1,0:T(8,128)S(1)} %all-to-all-done.1.parts, s32[4]{0:T(128)} %copy-done), custom_call_target="tpu_custom_call" | custom-call | tf_op jit(solution)/shard_map/gram_row/pallas_call | solution.py:383
Async XLA Ops:
  2.3 35.4 %collective-permute-start.1 = (f32[8,64,128]{2,1,0:T(8,128)S(1)}, f32[8,64,128]{2,1,0:T(8,128)S(1)}, u32[]{:S(2)}, u32[]{:S(2)}) collective-permute-start(f32[8,64,128]{2,1,0:T(8,128)S(1)} %get-tuple-element.27), channel_id=1, source_target_pairs={{1,0},{2,1},{3,2},{4,3},{5,4},{6,5},{7,6},{8,7},{9,8},{10,9},{11,1... | collective-permute-start | bytes 786440 | tf_op jit(solution)/shard_map/ppermute | solution.py:339
  11.1 26.6 %collective-permute-start = (f32[7,64,128]{2,1,0:T(8,128)S(1)}, f32[7,64,128]{2,1,0:T(8,128)S(1)}, u32[]{:S(2)}, u32[]{:S(2)}) collective-permute-start(f32[7,64,128]{2,1,0:T(8,128)S(1)} %get-tuple-element.26.after), channel_id=1, source_target_pairs={{0,1},{1,2},{2,3},{3,4},{4,5},{5,6},{6,7},{7,8},{8,9},{9,10},{10,1... | collective-permute-start | bytes 688136 | tf_op jit(solution)/shard_map/ppermute | solution.py:338
  21.1 0.7 copy-start.3
  21.1 0.7 copy-start.4
  21.2 0.7 copy-start.1
  21.2 0.7 copy-start.2
  23.3 14.4 %copy-start = (s32[4]{0:T(128)}, s32[4]{0:T(128)S(1)}, u32[]{:S(2)}) copy-start(s32[4]{0:T(128)S(1)} %pad_add_fusion.where) | copy-start | bytes 52
  67.8 15.2 %all-to-all-start.1 = ((f32[16,32,128]{2,1,0:T(8,128)}), f32[16,32,128]{2,1,0:T(8,128)S(1)}, u32[]{:S(2)}, u32[]{:S(2)}) async-start(f32[16,32,128]{2,1,0:T(8,128)} %line_sums.1), calls=%async_computation.1 | async-start | bytes 524288 | tf_op jit(solution)/shard_map/all_to_all | solution.py:382

commit v9 on v8

--- a/solution.py
+++ b/solution.py
@@ -44,17 +44,23 @@
 
 
 def edge_kernel(sat, mob, pore, qx, qy, qz, up, down, s, m, p, x, y, z, sem):
-    pieces = ((0, 3), (5, 3), (3, 2))
+    fields = ((sat, s), (mob, m), (qx, x), (qy, y), (qz, z), (pore, p))
+    wide, narrow = (0, 1, 2, 5, 6, 7), (0, 1, 6, 7)
+    needed = (wide, wide, (0, 1, 2, 6, 7), narrow, narrow, narrow)
     loads = []
-    for j, (start, size) in enumerate(pieces):
-        for k, (field, near) in enumerate(
-            ((sat, s), (mob, m), (qx, x), (qy, y), (qz, z), (pore, p))
-        ):
-            part = pl.ds(start, size)
-            loads.append(pltpu.make_async_copy(field.at[part], near.at[part], sem.at[6 * j + k]))
+    rest = []
+    for (field, near), rows in zip(fields, needed):
+        for row in rows:
+            index = len(loads)
+            loads.append(pltpu.make_async_copy(field.at[row], near.at[row], sem.at[index]))
+    for (field, near), rows in zip(fields, needed):
+        index = len(loads) + len(rest)
+        start = rows[len(rows) // 2 - 1] + 1 if len(rows) % 2 == 0 else rows[2] + 1
+        part = pl.ds(start, 8 - len(rows))
+        rest.append(pltpu.make_async_copy(field.at[part], near.at[part], sem.at[index]))
+    for load in loads + rest:
+        load.start()
     for load in loads:
-        load.start()
-    for load in loads[:12]:
         load.wait()
     f = [frac(s[i], m[i]) for i in range(3)]
     face_1 = across(x[1], f[0], f[1])
@@ -70,7 +76,7 @@
         up[k] = near[7]
     up[5] = face_7
     up[6] = jnp.maximum(x[7], 0.0) * flow_6
-    for load in loads[12:]:
+    for load in rest:
         load.wait()
 
 
@@ -234,10 +240,11 @@
             total = total + parts[pl.ds(width * j + k, members, stride=per * width), :]
         rows.append(total)
     errors = [parts[width * j + SUBSTEPS : width * j + SUBSTEPS + 1, :] for j in range(per)]
-    rows.append(jnp.concatenate(errors * 2, axis=0))
-    for j in range(out.shape[0]):
-        for k, row in enumerate(rows):
-            out[j, members * k : members * (k + 1), :] = row
+    rows.append(jnp.concatenate(errors, axis=0))
+    block = jnp.concatenate(rows, axis=0)
+    size = block.shape[0]
+    for j in range(out.shape[0] // size):
+        out[size * j : size * (j + 1), :] = block
 
 
 def gram_kernel(parts, where, rates_out, gram):
@@ -246,15 +253,19 @@
     own_z = where[3]
     groups, per, layer = 4, 4, 8
     rows = SUBSTEPS * layer
-    wells = parts.shape[2]
+    wells = parts.shape[1]
     mine = rates_out.shape[2]
+    size = rows + per
     sums = []
     for g in range(groups):
-        total = parts[g * per, :rows]
-        for j in range(1, per):
-            total = total + parts[g * per + j, :rows]
+        starts = [(g * per + j) * size for j in range(per)]
+        total = parts[starts[0] : starts[0] + rows]
+        for start in starts[1:]:
+            total = total + parts[start : start + rows]
         sums.append(total)
-    packed = jnp.concatenate([parts[y, rows : rows + per] for y in range(per)], axis=0)
+    packed = jnp.concatenate(
+        [parts[y * size + rows : (y + 1) * size] for y in range(per)], axis=0
+    )
     tiles = packed.shape[0]
     lane = lax.broadcasted_iota(jnp.int32, packed.shape, 1)
     home = lane // mine == lax.broadcasted_iota(jnp.int32, packed.shape, 0)
@@ -332,7 +343,7 @@
         + (held(rows, layers, columns),) * 6,
         in_specs=[ANY] * 6,
         out_specs=(VMEM,) * 8,
-        scratch_shapes=[pltpu.SemaphoreType.DMA((18,))],
+        scratch_shapes=[pltpu.SemaphoreType.DMA((35,))],
         name="edges",
     )(*fields)
     low = lax.ppermute(up, TILE, [(i, i + 1) for i in range(tiles - 1)])
@@ -374,12 +385,13 @@
     line = pltpu.with_memory_space_constraint(line.reshape(128, wells), pltpu.VMEM)
     (spreads,) = pl.pallas_call(
         line_kernel,
-        out_shape=(held(16, 32, wells),),
+        out_shape=(held(16 * 28, wells),),
         in_specs=[VMEM],
         out_specs=(VMEM,),
         name="line_sums",
     )(line)
-    plane = pltpu.with_memory_space_constraint(lax.all_to_all(spreads, PLANE, 0, 0), pltpu.VMEM)
+    plane = lax.all_to_all(spreads.reshape(16, 7, 4, wells), PLANE, 0, 0)
+    plane = pltpu.with_memory_space_constraint(plane.reshape(16 * 28, wells), pltpu.VMEM)
     rates, gram = pl.pallas_call(
         gram_kernel,
         out_shape=(shape(SUBSTEPS, 1, obs_error.shape[0]), shape(1, 32)),

time: 84.8 us -> 84.6 us (level)
  no operation moved by 1% of the time
where the time goes in v9:
time: 84.6 us; the launch traced here: 84.2 us
  blocking collectives  28 us (33%)
  starting transfers between devices  26.1 us (31%)
  waiting for transfers between devices  21.2 us (25%)
  Pallas kernels  6.74 us (8%)
  local copies, waits for them, and re-layouts  1.41 us (2%)
    all_to_all x1, blocking collectives, body(): line = lax.all_to_all(shares.reshape(32, 4, wells), LINE, 0, 0)  28 us
    ppermute x1, waiting for transfers between devices, body(): low = lax.ppermute(up, TILE, [(i, i + 1) for i in range(tiles - 1)])  14.4 us
    ppermute x1, starting transfers between devices, body(): low = lax.ppermute(up, TILE, [(i, i + 1) for i in range(tiles - 1)])  9.97 us
    ppermute x1, starting transfers between devices, body(): high = lax.ppermute(down, TILE, [(i + 1, i) for i in range(tiles - 1)])  8.79 us
    all_to_all x1, starting transfers between devices, body(): plane = lax.all_to_all(spreads.reshape(16, 7, 4, wells), PLANE, 0, 0)  7.38 us
    all_to_all x1, waiting for transfers between devices, body(): plane = lax.all_to_all(spreads.reshape(16, 7, 4, wells), PLANE, 0, 0)  6.8 us
    pallas_call x1, Pallas kernels, body(): pl.pallas_call(edge_kernel, out_shape=(held(UP_ROWS, layers, columns), he...  1.78 us
  transfers between devices with their start and end apart: 3, of which 2 were waited for; matrix products, arithmetic and copies ran while one was open for 1% of the time, Pallas kernels for 2%

profile of v9, /device:TPU:1, one launch (start us, length us, event | category | flops | bytes accessed | tf_op | source)
XLA Modules:
  0.0 84.2 jit_solution(7088606793767145267)
XLA Ops:
  0.6 1.8 %edges.1 = (f32[7,64,128]{2,1,0:T(8,128)S(1)}, f32[8,64,128]{2,1,0:T(8,128)S(1)}, f32[8,64,128]{2,1,0:T(8,128)S(1)}, f32[8,64,128]{2,1,0:T(8,128)S(1)}, f32[8,64...) custom-call(f32[8,64,128]{2,1,0:T(8,128)} %bitcast.27, ...), custom_call_target="tpu_custom_call" | custom-call | tf_op jit(solution)/shard_map/edges/pallas_call | solution.py:340
  2.4 8.8 %collective-permute-start.1 = (f32[8,64,128]{2,1,0:T(8,128)S(1)}, f32[8,64,128]{2,1,0:T(8,128)S(1)}, u32[]{:S(2)}, u32[]{:S(2)}) collective-permute-start(f32[8,64,128]{2,1,0:T(8,128)S(1)} %get-tuple-element.27), channel_id=1, source_target_pairs={{1,0},{2,1},{3,2},{4,3},{5,4},{6,5},{7,6},{8,7},{9,8},{10,9},{11,1... | collective-permute-start | bytes 786440 | tf_op jit(solution)/shard_map/ppermute | solution.py:350
  11.2 10.0 %collective-permute-start = (f32[7,64,128]{2,1,0:T(8,128)S(1)}, f32[7,64,128]{2,1,0:T(8,128)S(1)}, u32[]{:S(2)}, u32[]{:S(2)}) collective-permute-start(f32[7,64,128]{2,1,0:T(8,128)S(1)} %get-tuple-element.26.after), channel_id=1, source_target_pairs={{0,1},{1,2},{2,3},{3,4},{4,5},{5,6},{6,7},{7,8},{8,9},{9,10},{10,1... | collective-permute-start | bytes 688136 | tf_op jit(solution)/shard_map/ppermute | solution.py:349
  21.2 0.0 copy-start.3
  21.2 0.0 copy-start.4
  21.2 0.0 copy-start.1
  21.2 0.0 copy-start.2
  21.2 0.6 copy-done.3
  21.9 0.0 copy-done.4
  21.9 0.0 copy-done.1
  21.9 0.0 copy-done.2
  21.9 1.4 %inside.1 = (f32[12,64,128]{2,1,0:T(8,128)S(1)}, f32[2,64,128]{2,1,0:T(8,128)S(1)}, f32[4,128]{1,0:T(4,128)S(1)}, bf16[256,384]{1,0:T(8,128)(2,1)S(1)}, f32[256,128]{1,0:T(8,128)S(1)}, /*index=5*/f32[256,128]{1,0:T(8,128)S(1)}) custom-call(f32[8,64,128]{2,1,0:T(8,128)S(1)} %get-tuple-element.28.sat, f32[8,64,128]{2,1,0:T(8,128)S(1)} %get-tuple-element.21.mob, ...), custom_call_target="tpu_custom_call" | custom-call | tf_op jit(solution)/shard_map/inside/pallas_call | solution.py:354
  23.3 0.1 pad_add_fusion.where
  23.4 0.0 copy-start
  23.4 14.4 %collective-permute-done.low = f32[7,64,128]{2,1,0:T(8,128)S(1)} collective-permute-done((f32[7,64,128]{2,1,0:T(8,128)S(1)}, f32[7,64,128]{2,1,0:T(8,128)S(1)}, u32[]{:S(2)}, u32[]{:S(2)}) %collective-permute-start) | collective-permute-done | bytes 229408 | tf_op jit(solution)/shard_map/ppermute | solution.py:349
  37.8 0.0 collective-permute-done.1.high
  37.8 0.0 copy-done
  37.8 1.4 %outside.1 = (f32[8,64,128]{2,1,0:T(8,128)S(1)}, f32[128,128]{1,0:T(8,128)S(1)}) custom-call(f32[8,64,128]{2,1,0:T(8,128)S(1)} %get-tuple-element.21.mob, f32[8,64,128]{2,1,0:T(8,128)S(1)} %get-tuple-element.22.pore, f32[8,64,128]{2,1,0:T(8,128)S(1)} %get-tuple-element.23.qx, f32[8,64,128]{2,1,0:T(8,128)S(1)} %get-tuple-element.24.qy, ...), custom_call_target="tpu_custom_call" | custom-call | tf_op jit(solution)/shard_map/outside/pallas_call | solution.py:376
  39.2 28.0 %all_to_all.10 = f32[32,4,128]{2,1,0:T(4,128)S(1)} all-to-all(f32[32,4,128]{2,1,0:T(4,128)S(1)} %bitcast.22), channel_id=1, replica_groups=mesh['x'=4,'zl'=8,'y'=4,'zh'=2,'c'=2] {'zl','zh','c'}, dimensions={0} | all-to-all | bytes 131072 | tf_op jit(solution)/shard_map/all_to_all | solution.py:384
  67.1 0.7 line_sums.1
  67.9 7.4 %all-to-all-start.1 = ((f32[16,7,4,128]{3,2,1,0:T(4,128)}), f32[16,7,4,128]{3,2,1,0:T(4,128)S(1)}, u32[]{:S(2)}, u32[]{:S(2)}) async-start(f32[16,7,4,128]{3,2,1,0:T(4,128)} %bitcast.16), calls=%async_computation.1 | async-start | bytes 458752 | tf_op jit(solution)/shard_map/all_to_all | solution.py:393
  75.3 0.7 copy.13
  76.0 6.8 %all-to-all-done.1 = f32[16,7,4,128]{3,2,1,0:T(4,128)S(1)} async-done(((f32[16,7,4,128]{3,2,1,0:T(4,128)}), f32[16,7,4,128]{3,2,1,0:T(4,128)S(1)}, u32[]{:S(2)}, u32[]{:S(2)}) %all-to-all-start.1) | async-done | bytes 229408 | tf_op jit(solution)/shard_map/all_to_all | solution.py:393
  82.8 1.5 %gram_row.1 = (f32[3,1,8]{2,1,0:T(1,128)}, f32[1,32]{1,0:T(1,128)}) custom-call(f32[448,128]{1,0:T(8,128)S(1)} %bitcast.20, s32[4]{0:T(128)} %copy-done), custom_call_target="tpu_custom_call" | custom-call | tf_op jit(solution)/shard_map/gram_row/pallas_call | solution.py:395
Async XLA Ops:
  2.4 35.4 %collective-permute-start.1 = (f32[8,64,128]{2,1,0:T(8,128)S(1)}, f32[8,64,128]{2,1,0:T(8,128)S(1)}, u32[]{:S(2)}, u32[]{:S(2)}) collective-permute-start(f32[8,64,128]{2,1,0:T(8,128)S(1)} %get-tuple-element.27), channel_id=1, source_target_pairs={{1,0},{2,1},{3,2},{4,3},{5,4},{6,5},{7,6},{8,7},{9,8},{10,9},{11,1... | collective-permute-start | bytes 786440 | tf_op jit(solution)/shard_map/ppermute | solution.py:350
  11.2 26.6 %collective-permute-start = (f32[7,64,128]{2,1,0:T(8,128)S(1)}, f32[7,64,128]{2,1,0:T(8,128)S(1)}, u32[]{:S(2)}, u32[]{:S(2)}) collective-permute-start(f32[7,64,128]{2,1,0:T(8,128)S(1)} %get-tuple-element.26.after), channel_id=1, source_target_pairs={{0,1},{1,2},{2,3},{3,4},{4,5},{5,6},{6,7},{7,8},{8,9},{9,10},{10,1... | collective-permute-start | bytes 688136 | tf_op jit(solution)/shard_map/ppermute | solution.py:349
  21.2 0.7 copy-start.3
  21.2 0.7 copy-start.4
  21.2 0.7 copy-start.1
  21.2 0.7 copy-start.2
  23.4 14.4 %copy-start = (s32[4]{0:T(128)}, s32[4]{0:T(128)S(1)}, u32[]{:S(2)}) copy-start(s32[4]{0:T(128)S(1)} %pad_add_fusion.where) | copy-start | bytes 52
  67.9 14.9 %all-to-all-start.1 = ((f32[16,7,4,128]{3,2,1,0:T(4,128)}), f32[16,7,4,128]{3,2,1,0:T(4,128)S(1)}, u32[]{:S(2)}, u32[]{:S(2)}) async-start(f32[16,7,4,128]{3,2,1,0:T(4,128)} %bitcast.16), calls=%async_computation.1 | async-start | bytes 458752 | tf_op jit(solution)/shard_map/all_to_all | solution.py:393

commit v10 on v8

--- a/solution.py
+++ b/solution.py
@@ -7,12 +7,13 @@
 from jax.sharding import PartitionSpec as P
 
 SUBSTEPS = 3
+WELLS_DEV = 8
 AXES = ("x", "zl", "y", "zh", "c")
 SIZES = (4, 8, 4, 2, 2)
 MEMBER = ("x", "zl")
 TILE = ("y", "zh", "c")
-LINE = ("zl", "zh", "c")
-PLANE = ("x", "y")
+PLANE = ("x", "y", "c")
+LINE = ("zl", "zh")
 UP_ROWS = 7
 DOWN_ROWS = 8
 HIGHEST = lax.Precision.HIGHEST
@@ -217,52 +218,56 @@
     rates.append(
         rates_of([f[i] for pair in OUTER for i in pair], hot, mask[...], weight[...])
     )
-    zero = jnp.zeros_like(rates[0])
-    share = early[...] + jnp.concatenate(rates + [zero], axis=0)
-    share = jnp.concatenate([share, share], axis=0)
+    wells = shares.shape[1]
+    home = lax.broadcasted_iota(jnp.int32, (1, wells), 1) // WELLS_DEV == tile
+    errors = []
+    for k in range(SUBSTEPS):
+        shift = lax.rem(WELLS_DEV * (tile + 16 - k), wells)
+        errors.append(jnp.where(home, pltpu.roll(early[SUBSTEPS : SUBSTEPS + 1], shift, 1), 0.0))
+    rates = [early[k : k + 1] + rates[k] for k in range(SUBSTEPS)]
+    share = jnp.concatenate(rates + errors + [jnp.zeros((2, wells), jnp.float32)], axis=0)
     for j in range(shares.shape[0] // 8):
         shares[8 * j : 8 * j + 8, :] = share
 
 
-def line_kernel(parts, out):
-    members, per = 8, 4
-    width = SUBSTEPS + 1
+def plane_kernel(parts, out):
+    groups, per, width = 4, 8, 8
     rows = []
     for k in range(SUBSTEPS):
-        total = parts[pl.ds(k, members, stride=per * width), :]
+        total = parts[pl.ds(k, groups, stride=per * width), :]
         for j in range(1, per):
-            total = total + parts[pl.ds(width * j + k, members, stride=per * width), :]
+            total = total + parts[pl.ds(width * j + k, groups, stride=per * width), :]
         rows.append(total)
-    errors = [parts[width * j + SUBSTEPS : width * j + SUBSTEPS + 1, :] for j in range(per)]
-    rows.append(jnp.concatenate(errors * 2, axis=0))
-    for j in range(out.shape[0]):
-        for k, row in enumerate(rows):
-            out[j, members * k : members * (k + 1), :] = row
+    errors = parts[SUBSTEPS : SUBSTEPS + 4]
+    for j in range(1, per):
+        errors = errors + parts[width * j + SUBSTEPS : width * j + SUBSTEPS + 4]
+    block = jnp.concatenate(rows + [errors], axis=0)
+    size = block.shape[0]
+    for j in range(out.shape[0] // size):
+        out[size * j : size * (j + 1), :] = block
 
 
 def gram_kernel(parts, where, rates_out, gram):
     tile = where[0]
     own_x = where[2]
     own_z = where[3]
-    groups, per, layer = 4, 4, 8
-    rows = SUBSTEPS * layer
-    wells = parts.shape[2]
+    groups, per, layer, size = 4, 2, 8, 16
+    wells = parts.shape[1]
     mine = rates_out.shape[2]
-    sums = []
-    for g in range(groups):
-        total = parts[g * per, :rows]
-        for j in range(1, per):
-            total = total + parts[g * per + j, :rows]
-        sums.append(total)
-    packed = jnp.concatenate([parts[y, rows : rows + per] for y in range(per)], axis=0)
-    tiles = packed.shape[0]
-    lane = lax.broadcasted_iota(jnp.int32, packed.shape, 1)
-    home = lane // mine == lax.broadcasted_iota(jnp.int32, packed.shape, 0)
-    errors = []
-    for k in range(SUBSTEPS):
-        front = packed if k == 0 else pltpu.roll(packed, wells - mine * k, 1)
-        moved = pltpu.roll(front, 0, 1, stride=mine, stride_axis=0)
-        errors.append(jnp.sum(jnp.where(home, moved, 0.0), axis=0, keepdims=True))
+
+    def member_rows(row):
+        total = parts[pl.ds(row, layer, stride=per * size), :]
+        return total + parts[pl.ds(size + row, layer, stride=per * size), :]
+
+    sums = [
+        jnp.concatenate([member_rows(groups * k + g) for k in range(SUBSTEPS)], axis=0)
+        for g in range(groups)
+    ]
+    first = groups * SUBSTEPS
+    errors = [
+        parts[first + k : first + k + 1] + parts[size + first + k : size + first + k + 1]
+        for k in range(SUBSTEPS)
+    ]
     ensemble = groups * layer
     own = sums[0]
     for g in range(1, groups):
@@ -364,29 +369,30 @@
     )
     new_saturation, shares = pl.pallas_call(
         outside_kernel,
-        out_shape=(held(rows, layers, columns), held(128, wells)),
+        out_shape=(held(rows, layers, columns), held(256, wells)),
         in_specs=[VMEM] * 13 + [SMEM],
         out_specs=(VMEM, VMEM),
         compiler_params=pltpu.CompilerParams(vmem_limit_bytes=32 * 1024 * 1024),
         name="outside",
     )(mob, pore, qx, qy, qz, low, high, mids, middle, early, hot, mask, weight, where)
-    line = lax.all_to_all(shares.reshape(32, 4, wells), LINE, 0, 0)
-    line = pltpu.with_memory_space_constraint(line.reshape(128, wells), pltpu.VMEM)
+    plane = lax.all_to_all(shares.reshape(32, 8, wells), PLANE, 0, 0)
+    plane = pltpu.with_memory_space_constraint(plane.reshape(256, wells), pltpu.VMEM)
     (spreads,) = pl.pallas_call(
-        line_kernel,
-        out_shape=(held(16, 32, wells),),
+        plane_kernel,
+        out_shape=(held(256, wells),),
         in_specs=[VMEM],
         out_specs=(VMEM,),
-        name="line_sums",
-    )(line)
-    plane = pltpu.with_memory_space_constraint(lax.all_to_all(spreads, PLANE, 0, 0), pltpu.VMEM)
+        name="plane_sums",
+    )(plane)
+    line = lax.all_to_all(spreads.reshape(16, 16, wells), LINE, 0, 0)
+    line = pltpu.with_memory_space_constraint(line.reshape(256, wells), pltpu.VMEM)
     rates, gram = pl.pallas_call(
         gram_kernel,
         out_shape=(shape(SUBSTEPS, 1, obs_error.shape[0]), shape(1, 32)),
         in_specs=[VMEM, SMEM],
         out_specs=(VMEM, VMEM),
         name="gram_row",
-    )(plane, where)
+    )(line, where)
     return (
         new_saturation.reshape(saturation.shape),
         jnp.transpose(rates, (1, 2, 0)),

time: 84.8 us -> 86.1 us (1.015); the launches traced: 84.5 us -> 84.4 us
  waiting for transfers between devices: 21.5 us -> 27.1 us
  blocking collectives: 28 us -> 24.2 us
  starting transfers between devices: 26.1 us -> 24.4 us
    all_to_all x1, waiting for transfers between devices: 7.12 us -> 12.7 us  [body(): line = lax.all_to_all(spreads.reshape(16, 16, wells), LINE, 0, 0)]
    all_to_all x1, blocking collectives: 28 us -> 24.2 us  [body(): plane = lax.all_to_all(shares.reshape(32, 8, wells), PLANE, 0, 0)]
    all_to_all x1, starting transfers between devices: 7.38 us -> 5.67 us  [body(): line = lax.all_to_all(spreads.reshape(16, 16, wells), LINE, 0, 0)]
where the time goes in v10:
time: 86.1 us; the launch traced here: 84.4 us
  waiting for transfers between devices  27.1 us (31%)
  starting transfers between devices  24.4 us (28%)
  blocking collectives  24.2 us (28%)
  Pallas kernels  6.55 us (8%)
  local copies, waits for them, and re-layouts  1.41 us (2%)
    all_to_all x1, blocking collectives, body(): plane = lax.all_to_all(shares.reshape(32, 8, wells), PLANE, 0, 0)  24.2 us
    ppermute x1, waiting for transfers between devices, body(): low = lax.ppermute(up, TILE, [(i, i + 1) for i in range(tiles - 1)])  14.4 us
    all_to_all x1, waiting for transfers between devices, body(): line = lax.all_to_all(spreads.reshape(16, 16, wells), LINE, 0, 0)  12.7 us
    ppermute x1, starting transfers between devices, body(): low = lax.ppermute(up, TILE, [(i, i + 1) for i in range(tiles - 1)])  9.97 us
    ppermute x1, starting transfers between devices, body(): high = lax.ppermute(down, TILE, [(i + 1, i) for i in range(tiles - 1)])  8.79 us
    all_to_all x1, starting transfers between devices, body(): line = lax.all_to_all(spreads.reshape(16, 16, wells), LINE, 0, 0)  5.67 us
  transfers between devices with their start and end apart: 3, of which 2 were waited for; matrix products, arithmetic and copies ran while one was open for 1% of the time, Pallas kernels for 2%

profile of v10, /device:TPU:1, one launch (start us, length us, event | category | flops | bytes accessed | tf_op | source)
XLA Modules:
  0.0 84.4 jit_solution(4177005021069035128)
XLA Ops:
  0.6 1.7 %edges.1 = (f32[7,64,128]{2,1,0:T(8,128)S(1)}, f32[8,64,128]{2,1,0:T(8,128)S(1)}, f32[8,64,128]{2,1,0:T(8,128)S(1)}, f32[8,64,128]{2,1,0:T(8,128)S(1)}, f32[8,64...) custom-call(f32[8,64,128]{2,1,0:T(8,128)} %bitcast.27, ...), custom_call_target="tpu_custom_call" | custom-call | tf_op jit(solution)/shard_map/edges/pallas_call | solution.py:334
  2.3 8.8 %collective-permute-start.1 = (f32[8,64,128]{2,1,0:T(8,128)S(1)}, f32[8,64,128]{2,1,0:T(8,128)S(1)}, u32[]{:S(2)}, u32[]{:S(2)}) collective-permute-start(f32[8,64,128]{2,1,0:T(8,128)S(1)} %get-tuple-element.27), channel_id=1, source_target_pairs={{1,0},{2,1},{3,2},{4,3},{5,4},{6,5},{7,6},{8,7},{9,8},{10,9},{11,1... | collective-permute-start | bytes 786440 | tf_op jit(solution)/shard_map/ppermute | solution.py:344
  11.1 10.0 %collective-permute-start = (f32[7,64,128]{2,1,0:T(8,128)S(1)}, f32[7,64,128]{2,1,0:T(8,128)S(1)}, u32[]{:S(2)}, u32[]{:S(2)}) collective-permute-start(f32[7,64,128]{2,1,0:T(8,128)S(1)} %get-tuple-element.26.after), channel_id=1, source_target_pairs={{0,1},{1,2},{2,3},{3,4},{4,5},{5,6},{6,7},{7,8},{8,9},{9,10},{10,1... | collective-permute-start | bytes 688136 | tf_op jit(solution)/shard_map/ppermute | solution.py:343
  21.1 0.0 copy-start.3
  21.1 0.0 copy-start.4
  21.2 0.0 copy-start.1
  21.2 0.0 copy-start.2
  21.2 0.6 copy-done.3
  21.8 0.0 copy-done.4
  21.8 0.0 copy-done.1
  21.8 0.0 copy-done.2
  21.9 1.4 %inside.1 = (f32[12,64,128]{2,1,0:T(8,128)S(1)}, f32[2,64,128]{2,1,0:T(8,128)S(1)}, f32[4,128]{1,0:T(4,128)S(1)}, bf16[256,384]{1,0:T(8,128)(2,1)S(1)}, f32[256,128]{1,0:T(8,128)S(1)}, /*index=5*/f32[256,128]{1,0:T(8,128)S(1)}) custom-call(f32[8,64,128]{2,1,0:T(8,128)S(1)} %get-tuple-element.28.sat, f32[8,64,128]{2,1,0:T(8,128)S(1)} %get-tuple-element.21.mob, ...), custom_call_target="tpu_custom_call" | custom-call | tf_op jit(solution)/shard_map/inside/pallas_call | solution.py:348
  23.3 0.1 pad_add_fusion.where
  23.3 0.0 copy-start
  23.3 14.4 %collective-permute-done.low = f32[7,64,128]{2,1,0:T(8,128)S(1)} collective-permute-done((f32[7,64,128]{2,1,0:T(8,128)S(1)}, f32[7,64,128]{2,1,0:T(8,128)S(1)}, u32[]{:S(2)}, u32[]{:S(2)}) %collective-permute-start) | collective-permute-done | bytes 229408 | tf_op jit(solution)/shard_map/ppermute | solution.py:343
  37.7 0.0 collective-permute-done.1.high
  37.7 0.0 copy-done
  37.7 1.4 %outside.1 = (f32[8,64,128]{2,1,0:T(8,128)S(1)}, f32[256,128]{1,0:T(8,128)S(1)}) custom-call(f32[8,64,128]{2,1,0:T(8,128)S(1)} %get-tuple-element.21.mob, f32[8,64,128]{2,1,0:T(8,128)S(1)} %get-tuple-element.22.pore, f32[8,64,128]{2,1,0:T(8,128)S(1)} %get-tuple-element.23.qx, f32[8,64,128]{2,1,0:T(8,128)S(1)} %get-tuple-element.24.qy, ...), custom_call_target="tpu_custom_call" | custom-call | tf_op jit(solution)/shard_map/outside/pallas_call | solution.py:370
  39.1 24.2 %all_to_all.10 = f32[32,8,128]{2,1,0:T(8,128)S(1)} all-to-all(f32[32,8,128]{2,1,0:T(8,128)S(1)} %bitcast.22), channel_id=1, replica_groups=mesh['x'=4,'zl'=8,'y'=4,'zh'=2,'c'=2] {'x','y','c'}, dimensions={0} | all-to-all | bytes 262144 | tf_op jit(solution)/shard_map/all_to_all | solution.py:378
  63.3 0.7 plane_sums.1
  64.0 5.7 %all-to-all-start.1 = ((f32[16,16,128]{2,1,0:T(8,128)}), f32[16,16,128]{2,1,0:T(8,128)S(1)}, u32[]{:S(2)}, u32[]{:S(2)}) async-start(f32[16,16,128]{2,1,0:T(8,128)} %bitcast.16), calls=%async_computation.1 | async-start | bytes 262144 | tf_op jit(solution)/shard_map/all_to_all | solution.py:387
  69.7 0.7 copy.13
  70.4 12.7 %all-to-all-done.1 = f32[16,16,128]{2,1,0:T(8,128)S(1)} async-done(((f32[16,16,128]{2,1,0:T(8,128)}), f32[16,16,128]{2,1,0:T(8,128)S(1)}, u32[]{:S(2)}, u32[]{:S(2)}) %all-to-all-start.1) | async-done | bytes 131104 | tf_op jit(solution)/shard_map/all_to_all | solution.py:387
  83.0 1.4 %gram_row.1 = (f32[3,1,8]{2,1,0:T(1,128)}, f32[1,32]{1,0:T(1,128)}) custom-call(f32[256,128]{1,0:T(8,128)S(1)} %bitcast.20, s32[4]{0:T(128)} %copy-done), custom_call_target="tpu_custom_call" | custom-call | tf_op jit(solution)/shard_map/gram_row/pallas_call | solution.py:389
Async XLA Ops:
  2.3 35.4 %collective-permute-start.1 = (f32[8,64,128]{2,1,0:T(8,128)S(1)}, f32[8,64,128]{2,1,0:T(8,128)S(1)}, u32[]{:S(2)}, u32[]{:S(2)}) collective-permute-start(f32[8,64,128]{2,1,0:T(8,128)S(1)} %get-tuple-element.27), channel_id=1, source_target_pairs={{1,0},{2,1},{3,2},{4,3},{5,4},{6,5},{7,6},{8,7},{9,8},{10,9},{11,1... | collective-permute-start | bytes 786440 | tf_op jit(solution)/shard_map/ppermute | solution.py:344
  11.1 26.6 %collective-permute-start = (f32[7,64,128]{2,1,0:T(8,128)S(1)}, f32[7,64,128]{2,1,0:T(8,128)S(1)}, u32[]{:S(2)}, u32[]{:S(2)}) collective-permute-start(f32[7,64,128]{2,1,0:T(8,128)S(1)} %get-tuple-element.26.after), channel_id=1, source_target_pairs={{0,1},{1,2},{2,3},{3,4},{4,5},{5,6},{6,7},{7,8},{8,9},{9,10},{10,1... | collective-permute-start | bytes 688136 | tf_op jit(solution)/shard_map/ppermute | solution.py:343
  21.1 0.7 copy-start.3
  21.1 0.7 copy-start.4
  21.2 0.7 copy-start.1
  21.2 0.7 copy-start.2
  23.3 14.4 %copy-start = (s32[4]{0:T(128)}, s32[4]{0:T(128)S(1)}, u32[]{:S(2)}) copy-start(s32[4]{0:T(128)S(1)} %pad_add_fusion.where) | copy-start | bytes 52
  64.0 19.1 %all-to-all-start.1 = ((f32[16,16,128]{2,1,0:T(8,128)}), f32[16,16,128]{2,1,0:T(8,128)S(1)}, u32[]{:S(2)}, u32[]{:S(2)}) async-start(f32[16,16,128]{2,1,0:T(8,128)} %bitcast.16), calls=%async_computation.1 | async-start | bytes 262144 | tf_op jit(solution)/shard_map/all_to_all | solution.py:387

commit v11 on v9

--- a/solution.py
+++ b/solution.py
@@ -44,23 +44,17 @@
 
 
 def edge_kernel(sat, mob, pore, qx, qy, qz, up, down, s, m, p, x, y, z, sem):
-    fields = ((sat, s), (mob, m), (qx, x), (qy, y), (qz, z), (pore, p))
-    wide, narrow = (0, 1, 2, 5, 6, 7), (0, 1, 6, 7)
-    needed = (wide, wide, (0, 1, 2, 6, 7), narrow, narrow, narrow)
+    pieces = ((0, 3), (5, 3), (3, 2))
     loads = []
-    rest = []
-    for (field, near), rows in zip(fields, needed):
-        for row in rows:
-            index = len(loads)
-            loads.append(pltpu.make_async_copy(field.at[row], near.at[row], sem.at[index]))
-    for (field, near), rows in zip(fields, needed):
-        index = len(loads) + len(rest)
-        start = rows[len(rows) // 2 - 1] + 1 if len(rows) % 2 == 0 else rows[2] + 1
-        part = pl.ds(start, 8 - len(rows))
-        rest.append(pltpu.make_async_copy(field.at[part], near.at[part], sem.at[index]))
-    for load in loads + rest:
+    for j, (start, size) in enumerate(pieces):
+        for k, (field, near) in enumerate(
+            ((sat, s), (mob, m), (qx, x), (qy, y), (qz, z), (pore, p))
+        ):
+            part = pl.ds(start, size)
+            loads.append(pltpu.make_async_copy(field.at[part], near.at[part], sem.at[6 * j + k]))
+    for load in loads:
         load.start()
-    for load in loads:
+    for load in loads[:12]:
         load.wait()
     f = [frac(s[i], m[i]) for i in range(3)]
     face_1 = across(x[1], f[0], f[1])
@@ -76,7 +70,7 @@
         up[k] = near[7]
     up[5] = face_7
     up[6] = jnp.maximum(x[7], 0.0) * flow_6
-    for load in rest:
+    for load in loads[12:]:
         load.wait()
 
 
@@ -284,17 +278,18 @@
     own_rates = []
     for k in range(SUBSTEPS):
         part = slice(k * layer, (k + 1) * layer)
-        data = [total[part] / errors[k] for total in sums]
-        mean = jnp.sum(data[0] + data[1] + data[2] + data[3], axis=0, keepdims=True) / ensemble
+        scale = 1.0 / errors[k]
+        data = [total[part] * scale for total in sums]
+        mean = jnp.sum(data[0] + data[1] + data[2] + data[3], axis=0, keepdims=True) * (1.0 / ensemble)
         row = jnp.sum(jnp.where(sublane == own_z, own[part], 0.0), axis=0, keepdims=True)
         own_rates.append(row)
-        centered = row / errors[k] - mean
+        centered = row * scale - mean
         products = [total + (d - mean) * centered for total, d in zip(products, data)]
     line = jnp.zeros((layer, wells), jnp.float32)
     for g in range(groups):
         dots = jnp.sum(products[g], axis=1, keepdims=True)
         line = line + jnp.where(lane == sublane + g * layer, dots, 0.0)
-    line = jnp.sum(line, axis=0, keepdims=True) / (ensemble - 1.0)
+    line = jnp.sum(line, axis=0, keepdims=True) * (1.0 / (ensemble - 1.0))
     gram[...] = line[:, :ensemble]
     front = jnp.concatenate(own_rates + [jnp.zeros((layer - SUBSTEPS, wells), jnp.float32)], axis=0)
     front = pltpu.roll(front, lax.rem(wells - tile * mine, wells), 1)
@@ -343,7 +338,7 @@
         + (held(rows, layers, columns),) * 6,
         in_specs=[ANY] * 6,
         out_specs=(VMEM,) * 8,
-        scratch_shapes=[pltpu.SemaphoreType.DMA((35,))],
+        scratch_shapes=[pltpu.SemaphoreType.DMA((18,))],
         name="edges",
     )(*fields)
     low = lax.ppermute(up, TILE, [(i, i + 1) for i in range(tiles - 1)])

time: 84.6 us -> 84.5 us (level)
  no operation moved by 1% of the time
where the time goes in v11:
time: 84.5 us; the launch traced here: 84.2 us
  blocking collectives  28 us (33%)
  starting transfers between devices  26.1 us (31%)
  waiting for transfers between devices  21.2 us (25%)
  Pallas kernels  6.68 us (8%)
  local copies, waits for them, and re-layouts  1.41 us (2%)
    all_to_all x1, blocking collectives, body(): line = lax.all_to_all(shares.reshape(32, 4, wells), LINE, 0, 0)  28 us
    ppermute x1, waiting for transfers between devices, body(): low = lax.ppermute(up, TILE, [(i, i + 1) for i in range(tiles - 1)])  14.4 us
    ppermute x1, starting transfers between devices, body(): low = lax.ppermute(up, TILE, [(i, i + 1) for i in range(tiles - 1)])  9.97 us
    ppermute x1, starting transfers between devices, body(): high = lax.ppermute(down, TILE, [(i + 1, i) for i in range(tiles - 1)])  8.79 us
    all_to_all x1, starting transfers between devices, body(): plane = lax.all_to_all(spreads.reshape(16, 7, 4, wells), PLANE, 0, 0)  7.38 us
    all_to_all x1, waiting for transfers between devices, body(): plane = lax.all_to_all(spreads.reshape(16, 7, 4, wells), PLANE, 0, 0)  6.8 us
    pallas_call x1, Pallas kernels, body(): pl.pallas_call(edge_kernel, out_shape=(held(UP_ROWS, layers, columns), he...  1.71 us
  transfers between devices with their start and end apart: 3, of which 2 were waited for; matrix products, arithmetic and copies ran while one was open for 1% of the time, Pallas kernels for 2%

profile of v11, /device:TPU:1, one launch (start us, length us, event | category | flops | bytes accessed | tf_op | source)
XLA Modules:
  0.0 84.2 jit_solution(5254491615887675565)
XLA Ops:
  0.6 1.7 %edges.1 = (f32[7,64,128]{2,1,0:T(8,128)S(1)}, f32[8,64,128]{2,1,0:T(8,128)S(1)}, f32[8,64,128]{2,1,0:T(8,128)S(1)}, f32[8,64,128]{2,1,0:T(8,128)S(1)}, f32[8,64...) custom-call(f32[8,64,128]{2,1,0:T(8,128)} %bitcast.27, ...), custom_call_target="tpu_custom_call" | custom-call | tf_op jit(solution)/shard_map/edges/pallas_call | solution.py:335
  2.3 8.8 %collective-permute-start.1 = (f32[8,64,128]{2,1,0:T(8,128)S(1)}, f32[8,64,128]{2,1,0:T(8,128)S(1)}, u32[]{:S(2)}, u32[]{:S(2)}) collective-permute-start(f32[8,64,128]{2,1,0:T(8,128)S(1)} %get-tuple-element.27), channel_id=1, source_target_pairs={{1,0},{2,1},{3,2},{4,3},{5,4},{6,5},{7,6},{8,7},{9,8},{10,9},{11,1... | collective-permute-start | bytes 786440 | tf_op jit(solution)/shard_map/ppermute | solution.py:345
  11.1 10.0 %collective-permute-start = (f32[7,64,128]{2,1,0:T(8,128)S(1)}, f32[7,64,128]{2,1,0:T(8,128)S(1)}, u32[]{:S(2)}, u32[]{:S(2)}) collective-permute-start(f32[7,64,128]{2,1,0:T(8,128)S(1)} %get-tuple-element.26.after), channel_id=1, source_target_pairs={{0,1},{1,2},{2,3},{3,4},{4,5},{5,6},{6,7},{7,8},{8,9},{9,10},{10,1... | collective-permute-start | bytes 688136 | tf_op jit(solution)/shard_map/ppermute | solution.py:344
  21.1 0.0 copy-start.3
  21.1 0.0 copy-start.4
  21.2 0.0 copy-start.1
  21.2 0.0 copy-start.2
  21.2 0.6 copy-done.3
  21.8 0.0 copy-done.4
  21.8 0.0 copy-done.1
  21.8 0.0 copy-done.2
  21.9 1.4 %inside.1 = (f32[12,64,128]{2,1,0:T(8,128)S(1)}, f32[2,64,128]{2,1,0:T(8,128)S(1)}, f32[4,128]{1,0:T(4,128)S(1)}, bf16[256,384]{1,0:T(8,128)(2,1)S(1)}, f32[256,128]{1,0:T(8,128)S(1)}, /*index=5*/f32[256,128]{1,0:T(8,128)S(1)}) custom-call(f32[8,64,128]{2,1,0:T(8,128)S(1)} %get-tuple-element.28.sat, f32[8,64,128]{2,1,0:T(8,128)S(1)} %get-tuple-element.21.mob, ...), custom_call_target="tpu_custom_call" | custom-call | tf_op jit(solution)/shard_map/inside/pallas_call | solution.py:349
  23.3 0.1 pad_add_fusion.where
  23.3 0.0 copy-start
  23.3 14.4 %collective-permute-done.low = f32[7,64,128]{2,1,0:T(8,128)S(1)} collective-permute-done((f32[7,64,128]{2,1,0:T(8,128)S(1)}, f32[7,64,128]{2,1,0:T(8,128)S(1)}, u32[]{:S(2)}, u32[]{:S(2)}) %collective-permute-start) | collective-permute-done | bytes 229408 | tf_op jit(solution)/shard_map/ppermute | solution.py:344
  37.7 0.0 collective-permute-done.1.high
  37.7 0.0 copy-done
  37.7 1.4 %outside.1 = (f32[8,64,128]{2,1,0:T(8,128)S(1)}, f32[128,128]{1,0:T(8,128)S(1)}) custom-call(f32[8,64,128]{2,1,0:T(8,128)S(1)} %get-tuple-element.21.mob, f32[8,64,128]{2,1,0:T(8,128)S(1)} %get-tuple-element.22.pore, f32[8,64,128]{2,1,0:T(8,128)S(1)} %get-tuple-element.23.qx, f32[8,64,128]{2,1,0:T(8,128)S(1)} %get-tuple-element.24.qy, ...), custom_call_target="tpu_custom_call" | custom-call | tf_op jit(solution)/shard_map/outside/pallas_call | solution.py:371
  39.1 28.0 %all_to_all.10 = f32[32,4,128]{2,1,0:T(4,128)S(1)} all-to-all(f32[32,4,128]{2,1,0:T(4,128)S(1)} %bitcast.22), channel_id=1, replica_groups=mesh['x'=4,'zl'=8,'y'=4,'zh'=2,'c'=2] {'zl','zh','c'}, dimensions={0} | all-to-all | bytes 131072 | tf_op jit(solution)/shard_map/all_to_all | solution.py:379
  67.1 0.7 line_sums.1
  67.8 7.4 %all-to-all-start.1 = ((f32[16,7,4,128]{3,2,1,0:T(4,128)}), f32[16,7,4,128]{3,2,1,0:T(4,128)S(1)}, u32[]{:S(2)}, u32[]{:S(2)}) async-start(f32[16,7,4,128]{3,2,1,0:T(4,128)} %bitcast.16), calls=%async_computation.1 | async-start | bytes 458752 | tf_op jit(solution)/shard_map/all_to_all | solution.py:388
  75.2 0.7 copy.13
  75.9 6.8 %all-to-all-done.1 = f32[16,7,4,128]{3,2,1,0:T(4,128)S(1)} async-done(((f32[16,7,4,128]{3,2,1,0:T(4,128)}), f32[16,7,4,128]{3,2,1,0:T(4,128)S(1)}, u32[]{:S(2)}, u32[]{:S(2)}) %all-to-all-start.1) | async-done | bytes 229408 | tf_op jit(solution)/shard_map/all_to_all | solution.py:388
  82.7 1.5 %gram_row.1 = (f32[3,1,8]{2,1,0:T(1,128)}, f32[1,32]{1,0:T(1,128)}) custom-call(f32[448,128]{1,0:T(8,128)S(1)} %bitcast.20, s32[4]{0:T(128)} %copy-done), custom_call_target="tpu_custom_call" | custom-call | tf_op jit(solution)/shard_map/gram_row/pallas_call | solution.py:390
Async XLA Ops:
  2.3 35.4 %collective-permute-start.1 = (f32[8,64,128]{2,1,0:T(8,128)S(1)}, f32[8,64,128]{2,1,0:T(8,128)S(1)}, u32[]{:S(2)}, u32[]{:S(2)}) collective-permute-start(f32[8,64,128]{2,1,0:T(8,128)S(1)} %get-tuple-element.27), channel_id=1, source_target_pairs={{1,0},{2,1},{3,2},{4,3},{5,4},{6,5},{7,6},{8,7},{9,8},{10,9},{11,1... | collective-permute-start | bytes 786440 | tf_op jit(solution)/shard_map/ppermute | solution.py:345
  11.1 26.6 %collective-permute-start = (f32[7,64,128]{2,1,0:T(8,128)S(1)}, f32[7,64,128]{2,1,0:T(8,128)S(1)}, u32[]{:S(2)}, u32[]{:S(2)}) collective-permute-start(f32[7,64,128]{2,1,0:T(8,128)S(1)} %get-tuple-element.26.after), channel_id=1, source_target_pairs={{0,1},{1,2},{2,3},{3,4},{4,5},{5,6},{6,7},{7,8},{8,9},{9,10},{10,1... | collective-permute-start | bytes 688136 | tf_op jit(solution)/shard_map/ppermute | solution.py:344
  21.1 0.7 copy-start.3
  21.1 0.7 copy-start.4
  21.2 0.7 copy-start.1
  21.2 0.7 copy-start.2
  23.3 14.4 %copy-start = (s32[4]{0:T(128)}, s32[4]{0:T(128)S(1)}, u32[]{:S(2)}) copy-start(s32[4]{0:T(128)S(1)} %pad_add_fusion.where) | copy-start | bytes 52
  67.8 14.9 %all-to-all-start.1 = ((f32[16,7,4,128]{3,2,1,0:T(4,128)}), f32[16,7,4,128]{3,2,1,0:T(4,128)S(1)}, u32[]{:S(2)}, u32[]{:S(2)}) async-start(f32[16,7,4,128]{3,2,1,0:T(4,128)} %bitcast.16), calls=%async_computation.1 | async-start | bytes 458752 | tf_op jit(solution)/shard_map/all_to_all | solution.py:388

commit v12 on v11

--- a/solution.py
+++ b/solution.py
@@ -241,7 +241,9 @@
         out[size * j : size * (j + 1), :] = block
 
 
-def gram_kernel(parts, where, rates_out, gram):
+def gram_kernel(parts, where, sat, rates_out, gram, sat_out, sem):
+    writing = pltpu.make_async_copy(sat, sat_out, sem)
+    writing.start()
     tile = where[0]
     own_x = where[2]
     own_z = where[3]
@@ -295,6 +297,7 @@
     front = pltpu.roll(front, lax.rem(wells - tile * mine, wells), 1)
     for k in range(SUBSTEPS):
         rates_out[k] = front[k : k + 1, :mine]
+    writing.wait()
 
 
 VMEM = pl.BlockSpec(memory_space=pltpu.VMEM)
@@ -387,13 +390,18 @@
     )(line)
     plane = lax.all_to_all(spreads.reshape(16, 7, 4, wells), PLANE, 0, 0)
     plane = pltpu.with_memory_space_constraint(plane.reshape(16 * 28, wells), pltpu.VMEM)
-    rates, gram = pl.pallas_call(
+    rates, gram, new_saturation = pl.pallas_call(
         gram_kernel,
-        out_shape=(shape(SUBSTEPS, 1, obs_error.shape[0]), shape(1, 32)),
-        in_specs=[VMEM, SMEM],
-        out_specs=(VMEM, VMEM),
+        out_shape=(
+            shape(SUBSTEPS, 1, obs_error.shape[0]),
+            shape(1, 32),
+            shape(rows, layers, columns),
+        ),
+        in_specs=[VMEM, SMEM, VMEM],
+        out_specs=(VMEM, VMEM, ANY),
+        scratch_shapes=[pltpu.SemaphoreType.DMA],
         name="gram_row",
-    )(plane, where)
+    )(plane, where, pltpu.with_memory_space_constraint(new_saturation, pltpu.VMEM))
     return (
         new_saturation.reshape(saturation.shape),
         jnp.transpose(rates, (1, 2, 0)),

time: 84.5 us -> 84 us (level)
  blocking collectives: 28 us -> 42.6 us
  starting transfers between devices: 26.1 us -> 18.8 us
  waiting for transfers between devices: 21.2 us -> 14.4 us
    all_to_all x0 -> x1, blocking collectives: none -> 14.7 us  [body(): plane = lax.all_to_all(spreads.reshape(16, 7, 4, wells), PLANE, 0, 0)]
    all_to_all x1 -> x0, starting transfers between devices: 7.38 us -> none  [body(): plane = lax.all_to_all(spreads.reshape(16, 7, 4, wells), PLANE, 0, 0)]
    all_to_all x1 -> x0, waiting for transfers between devices: 6.8 us -> none  [body(): plane = lax.all_to_all(spreads.reshape(16, 7, 4, wells), PLANE, 0, 0)]
  transfers between devices with their start and end apart: 3 -> 2, of which waited for: 2 -> 1; matrix products, arithmetic and copies ran while one was open for 1% -> 0% of each run, Pallas kernels for 2% -> 2%
where the time goes in v12:
time: 84 us; the launch traced here: 83.7 us
  blocking collectives  42.6 us (51%)
  starting transfers between devices  18.8 us (22%)
  waiting for transfers between devices  14.4 us (17%)
  Pallas kernels  6.44 us (8%)
    all_to_all x1, blocking collectives, body(): line = lax.all_to_all(shares.reshape(32, 4, wells), LINE, 0, 0)  28 us
    all_to_all x1, blocking collectives, body(): plane = lax.all_to_all(spreads.reshape(16, 7, 4, wells), PLANE, 0, 0)  14.7 us
    ppermute x1, waiting for transfers between devices, body(): low = lax.ppermute(up, TILE, [(i, i + 1) for i in range(tiles - 1)])  14.4 us
    ppermute x1, starting transfers between devices, body(): low = lax.ppermute(up, TILE, [(i, i + 1) for i in range(tiles - 1)])  9.97 us
    ppermute x1, starting transfers between devices, body(): high = lax.ppermute(down, TILE, [(i + 1, i) for i in range(tiles - 1)])  8.79 us
    pallas_call x1, Pallas kernels, body(): pl.pallas_call(gram_kernel, out_shape=(shape(SUBSTEPS, 1, obs_error.shape...  1.94 us
    pallas_call x1, Pallas kernels, body(): pl.pallas_call(edge_kernel, out_shape=(held(UP_ROWS, layers, columns), he...  1.71 us
  transfers between devices with their start and end apart: 2, of which 1 were waited for; matrix products, arithmetic and copies ran while one was open for 0% of the time, Pallas kernels for 2%

profile of v12, /device:TPU:1, one launch (start us, length us, event | category | flops | bytes accessed | tf_op | source)
XLA Modules:
  0.0 83.7 jit_solution(4774612004727801023)
XLA Ops:
  0.6 1.7 %edges.1 = (f32[7,64,128]{2,1,0:T(8,128)S(1)}, f32[8,64,128]{2,1,0:T(8,128)S(1)}, f32[8,64,128]{2,1,0:T(8,128)S(1)}, f32[8,64,128]{2,1,0:T(8,128)S(1)}, f32[8,64...) custom-call(f32[8,64,128]{2,1,0:T(8,128)} %bitcast.27, ...), custom_call_target="tpu_custom_call" | custom-call | tf_op jit(solution)/shard_map/edges/pallas_call | solution.py:338
  2.3 8.8 %collective-permute-start.1 = (f32[8,64,128]{2,1,0:T(8,128)S(1)}, f32[8,64,128]{2,1,0:T(8,128)S(1)}, u32[]{:S(2)}, u32[]{:S(2)}) collective-permute-start(f32[8,64,128]{2,1,0:T(8,128)S(1)} %get-tuple-element.28), channel_id=1, source_target_pairs={{1,0},{2,1},{3,2},{4,3},{5,4},{6,5},{7,6},{8,7},{9,8},{10,9},{11,1... | collective-permute-start | bytes 786440 | tf_op jit(solution)/shard_map/ppermute | solution.py:348
  11.1 10.0 %collective-permute-start = (f32[7,64,128]{2,1,0:T(8,128)S(1)}, f32[7,64,128]{2,1,0:T(8,128)S(1)}, u32[]{:S(2)}, u32[]{:S(2)}) collective-permute-start(f32[7,64,128]{2,1,0:T(8,128)S(1)} %get-tuple-element.27.after), channel_id=1, source_target_pairs={{0,1},{1,2},{2,3},{3,4},{4,5},{5,6},{6,7},{7,8},{8,9},{9,10},{10,1... | collective-permute-start | bytes 688136 | tf_op jit(solution)/shard_map/ppermute | solution.py:347
  21.1 0.0 copy-start.3
  21.1 0.0 copy-start.4
  21.2 0.0 copy-start.1
  21.2 0.0 copy-start.2
  21.2 0.6 copy-done.3
  21.8 0.0 copy-done.4
  21.8 0.0 copy-done.1
  21.8 0.0 copy-done.2
  21.9 1.4 %inside.1 = (f32[12,64,128]{2,1,0:T(8,128)S(1)}, f32[2,64,128]{2,1,0:T(8,128)S(1)}, f32[4,128]{1,0:T(4,128)S(1)}, bf16[256,384]{1,0:T(8,128)(2,1)S(1)}, f32[256,128]{1,0:T(8,128)S(1)}, /*index=5*/f32[256,128]{1,0:T(8,128)S(1)}) custom-call(f32[8,64,128]{2,1,0:T(8,128)S(1)} %get-tuple-element.29.sat, f32[8,64,128]{2,1,0:T(8,128)S(1)} %get-tuple-element.22.mob, ...), custom_call_target="tpu_custom_call" | custom-call | tf_op jit(solution)/shard_map/inside/pallas_call | solution.py:352
  23.3 0.1 pad_add_fusion.where
  23.3 0.0 copy-start
  23.3 14.4 %collective-permute-done.low = f32[7,64,128]{2,1,0:T(8,128)S(1)} collective-permute-done((f32[7,64,128]{2,1,0:T(8,128)S(1)}, f32[7,64,128]{2,1,0:T(8,128)S(1)}, u32[]{:S(2)}, u32[]{:S(2)}) %collective-permute-start) | collective-permute-done | bytes 229408 | tf_op jit(solution)/shard_map/ppermute | solution.py:347
  37.7 0.0 collective-permute-done.1.high
  37.7 0.0 copy-done
  37.7 1.4 %outside.1 = (f32[8,64,128]{2,1,0:T(8,128)S(1)}, f32[128,128]{1,0:T(8,128)S(1)}) custom-call(f32[8,64,128]{2,1,0:T(8,128)S(1)} %get-tuple-element.22.mob, f32[8,64,128]{2,1,0:T(8,128)S(1)} %get-tuple-element.23.pore, f32[8,64,128]{2,1,0:T(8,128)S(1)} %get-tuple-element.24.qx, f32[8,64,128]{2,1,0:T(8,128)S(1)} %get-tuple-element.25.qy, ...), custom_call_target="tpu_custom_call" | custom-call | tf_op jit(solution)/shard_map/outside/pallas_call | solution.py:374
  39.1 28.0 %all_to_all.10 = f32[32,4,128]{2,1,0:T(4,128)S(1)} all-to-all(f32[32,4,128]{2,1,0:T(4,128)S(1)} %bitcast.22), channel_id=1, replica_groups=mesh['x'=4,'zl'=8,'y'=4,'zh'=2,'c'=2] {'zl','zh','c'}, dimensions={0} | all-to-all | bytes 131072 | tf_op jit(solution)/shard_map/all_to_all | solution.py:382
  67.1 14.7 %all_to_all.11 = f32[16,7,4,128]{3,2,1,0:T(4,128)S(1)} all-to-all(f32[16,7,4,128]{3,2,1,0:T(4,128)S(1)} %bitcast.20), channel_id=1, replica_groups=mesh['x'=4,'zl'=8,'y'=4,'zh'=2,'c'=2] {'x','y'}, dimensions={0} | all-to-all | bytes 458752 | tf_op jit(solution)/shard_map/all_to_all | solution.py:391
  81.8 1.9 %gram_row.1 = (f32[3,1,8]{2,1,0:T(1,128)}, f32[1,32]{1,0:T(1,128)}, f32[8,64,128]{2,1,0:T(8,128)}) custom-call(f32[448,128]{1,0:T(8,128)S(1)} %bitcast.19, s32[4]{0:T(128)} %copy-done, f32[8,64,128]{2,1,0:T(8,128)S(1)} %get-tuple-element.37.sat), custom_call_target="tpu_custom_call" | custom-call | tf_op jit(solution)/shard_map/gram_row/pallas_call | solution.py:393
  (1 shorter events, 0.0 us)
Async XLA Ops:
  2.3 35.4 %collective-permute-start.1 = (f32[8,64,128]{2,1,0:T(8,128)S(1)}, f32[8,64,128]{2,1,0:T(8,128)S(1)}, u32[]{:S(2)}, u32[]{:S(2)}) collective-permute-start(f32[8,64,128]{2,1,0:T(8,128)S(1)} %get-tuple-element.28), channel_id=1, source_target_pairs={{1,0},{2,1},{3,2},{4,3},{5,4},{6,5},{7,6},{8,7},{9,8},{10,9},{11,1... | collective-permute-start | bytes 786440 | tf_op jit(solution)/shard_map/ppermute | solution.py:348
  11.1 26.6 %collective-permute-start = (f32[7,64,128]{2,1,0:T(8,128)S(1)}, f32[7,64,128]{2,1,0:T(8,128)S(1)}, u32[]{:S(2)}, u32[]{:S(2)}) collective-permute-start(f32[7,64,128]{2,1,0:T(8,128)S(1)} %get-tuple-element.27.after), channel_id=1, source_target_pairs={{0,1},{1,2},{2,3},{3,4},{4,5},{5,6},{6,7},{7,8},{8,9},{9,10},{10,1... | collective-permute-start | bytes 688136 | tf_op jit(solution)/shard_map/ppermute | solution.py:347
  21.1 0.7 copy-start.3
  21.1 0.7 copy-start.4
  21.2 0.7 copy-start.1
  21.2 0.7 copy-start.2
  23.3 14.4 %copy-start = (s32[4]{0:T(128)}, s32[4]{0:T(128)S(1)}, u32[]{:S(2)}) copy-start(s32[4]{0:T(128)S(1)} %pad_add_fusion.where) | copy-start | bytes 52

commit v13 on v12

--- a/solution.py
+++ b/solution.py
@@ -241,8 +241,8 @@
         out[size * j : size * (j + 1), :] = block
 
 
-def gram_kernel(parts, where, sat, rates_out, gram, sat_out, sem):
-    writing = pltpu.make_async_copy(sat, sat_out, sem)
+def gram_kernel(parts, where, sat, rates_hbm, gram_hbm, sat_out, rates_out, gram, sem):
+    writing = pltpu.make_async_copy(sat, sat_out, sem.at[0])
     writing.start()
     tile = where[0]
     own_x = where[2]
@@ -297,7 +297,15 @@
     front = pltpu.roll(front, lax.rem(wells - tile * mine, wells), 1)
     for k in range(SUBSTEPS):
         rates_out[k] = front[k : k + 1, :mine]
+    results = [
+        pltpu.make_async_copy(rates_out, rates_hbm, sem.at[1]),
+        pltpu.make_async_copy(gram, gram_hbm, sem.at[2]),
+    ]
+    for result in results:
+        result.start()
     writing.wait()
+    for result in results:
+        result.wait()
 
 
 VMEM = pl.BlockSpec(memory_space=pltpu.VMEM)
@@ -398,8 +406,12 @@
             shape(rows, layers, columns),
         ),
         in_specs=[VMEM, SMEM, VMEM],
-        out_specs=(VMEM, VMEM, ANY),
-        scratch_shapes=[pltpu.SemaphoreType.DMA],
+        out_specs=(ANY,) * 3,
+        scratch_shapes=[
+            pltpu.VMEM((SUBSTEPS, 1, obs_error.shape[0]), jnp.float32),
+            pltpu.VMEM((1, 32), jnp.float32),
+            pltpu.SemaphoreType.DMA((3,)),
+        ],
         name="gram_row",
     )(plane, where, pltpu.with_memory_space_constraint(new_saturation, pltpu.VMEM))
     return (

time: 84 us -> 83.6 us (level)
  no operation moved by 1% of the time
where the time goes in v13:
time: 83.6 us; the launch traced here: 83.3 us
  blocking collectives  42.6 us (51%)
  starting transfers between devices  18.8 us (22%)
  waiting for transfers between devices  14.4 us (17%)
  Pallas kernels  6 us (7%)
    all_to_all x1, blocking collectives, body(): line = lax.all_to_all(shares.reshape(32, 4, wells), LINE, 0, 0)  28 us
    all_to_all x1, blocking collectives, body(): plane = lax.all_to_all(spreads.reshape(16, 7, 4, wells), PLANE, 0, 0)  14.7 us
    ppermute x1, waiting for transfers between devices, body(): low = lax.ppermute(up, TILE, [(i, i + 1) for i in range(tiles - 1)])  14.4 us
    ppermute x1, starting transfers between devices, body(): low = lax.ppermute(up, TILE, [(i, i + 1) for i in range(tiles - 1)])  9.97 us
    ppermute x1, starting transfers between devices, body(): high = lax.ppermute(down, TILE, [(i + 1, i) for i in range(tiles - 1)])  8.79 us
    pallas_call x1, Pallas kernels, body(): pl.pallas_call(edge_kernel, out_shape=(held(UP_ROWS, layers, columns), he...  1.71 us
  transfers between devices with their start and end apart: 2, of which 1 were waited for; matrix products, arithmetic and copies ran while one was open for 0% of the time, Pallas kernels for 2%

profile of v13, /device:TPU:1, one launch (start us, length us, event | category | flops | bytes accessed | tf_op | source)
XLA Modules:
  0.0 83.3 jit_solution(3195318358628983552)
XLA Ops:
  0.6 1.7 %edges.1 = (f32[7,64,128]{2,1,0:T(8,128)S(1)}, f32[8,64,128]{2,1,0:T(8,128)S(1)}, f32[8,64,128]{2,1,0:T(8,128)S(1)}, f32[8,64,128]{2,1,0:T(8,128)S(1)}, f32[8,64...) custom-call(f32[8,64,128]{2,1,0:T(8,128)} %bitcast.27, ...), custom_call_target="tpu_custom_call" | custom-call | tf_op jit(solution)/shard_map/edges/pallas_call | solution.py:346
  2.3 8.8 %collective-permute-start.1 = (f32[8,64,128]{2,1,0:T(8,128)S(1)}, f32[8,64,128]{2,1,0:T(8,128)S(1)}, u32[]{:S(2)}, u32[]{:S(2)}) collective-permute-start(f32[8,64,128]{2,1,0:T(8,128)S(1)} %get-tuple-element.28), channel_id=1, source_target_pairs={{1,0},{2,1},{3,2},{4,3},{5,4},{6,5},{7,6},{8,7},{9,8},{10,9},{11,1... | collective-permute-start | bytes 786440 | tf_op jit(solution)/shard_map/ppermute | solution.py:356
  11.1 10.0 %collective-permute-start = (f32[7,64,128]{2,1,0:T(8,128)S(1)}, f32[7,64,128]{2,1,0:T(8,128)S(1)}, u32[]{:S(2)}, u32[]{:S(2)}) collective-permute-start(f32[7,64,128]{2,1,0:T(8,128)S(1)} %get-tuple-element.27.after), channel_id=1, source_target_pairs={{0,1},{1,2},{2,3},{3,4},{4,5},{5,6},{6,7},{7,8},{8,9},{9,10},{10,1... | collective-permute-start | bytes 688136 | tf_op jit(solution)/shard_map/ppermute | solution.py:355
  21.1 0.0 copy-start.3
  21.1 0.0 copy-start.4
  21.2 0.0 copy-start.1
  21.2 0.0 copy-start.2
  21.2 0.6 copy-done.3
  21.8 0.0 copy-done.4
  21.8 0.0 copy-done.1
  21.8 0.0 copy-done.2
  21.9 1.4 %inside.1 = (f32[12,64,128]{2,1,0:T(8,128)S(1)}, f32[2,64,128]{2,1,0:T(8,128)S(1)}, f32[4,128]{1,0:T(4,128)S(1)}, bf16[256,384]{1,0:T(8,128)(2,1)S(1)}, f32[256,128]{1,0:T(8,128)S(1)}, /*index=5*/f32[256,128]{1,0:T(8,128)S(1)}) custom-call(f32[8,64,128]{2,1,0:T(8,128)S(1)} %get-tuple-element.29.sat, f32[8,64,128]{2,1,0:T(8,128)S(1)} %get-tuple-element.22.mob, ...), custom_call_target="tpu_custom_call" | custom-call | tf_op jit(solution)/shard_map/inside/pallas_call | solution.py:360
  23.3 0.1 pad_add_fusion.where
  23.3 0.0 copy-start
  23.3 14.4 %collective-permute-done.low = f32[7,64,128]{2,1,0:T(8,128)S(1)} collective-permute-done((f32[7,64,128]{2,1,0:T(8,128)S(1)}, f32[7,64,128]{2,1,0:T(8,128)S(1)}, u32[]{:S(2)}, u32[]{:S(2)}) %collective-permute-start) | collective-permute-done | bytes 229408 | tf_op jit(solution)/shard_map/ppermute | solution.py:355
  37.7 0.0 collective-permute-done.1.high
  37.7 0.0 copy-done
  37.7 1.4 %outside.1 = (f32[8,64,128]{2,1,0:T(8,128)S(1)}, f32[128,128]{1,0:T(8,128)S(1)}) custom-call(f32[8,64,128]{2,1,0:T(8,128)S(1)} %get-tuple-element.22.mob, f32[8,64,128]{2,1,0:T(8,128)S(1)} %get-tuple-element.23.pore, f32[8,64,128]{2,1,0:T(8,128)S(1)} %get-tuple-element.24.qx, f32[8,64,128]{2,1,0:T(8,128)S(1)} %get-tuple-element.25.qy, ...), custom_call_target="tpu_custom_call" | custom-call | tf_op jit(solution)/shard_map/outside/pallas_call | solution.py:382
  39.1 28.0 %all_to_all.10 = f32[32,4,128]{2,1,0:T(4,128)S(1)} all-to-all(f32[32,4,128]{2,1,0:T(4,128)S(1)} %bitcast.22), channel_id=1, replica_groups=mesh['x'=4,'zl'=8,'y'=4,'zh'=2,'c'=2] {'zl','zh','c'}, dimensions={0} | all-to-all | bytes 131072 | tf_op jit(solution)/shard_map/all_to_all | solution.py:390
  67.1 14.7 %all_to_all.11 = f32[16,7,4,128]{3,2,1,0:T(4,128)S(1)} all-to-all(f32[16,7,4,128]{3,2,1,0:T(4,128)S(1)} %bitcast.20), channel_id=1, replica_groups=mesh['x'=4,'zl'=8,'y'=4,'zh'=2,'c'=2] {'x','y'}, dimensions={0} | all-to-all | bytes 458752 | tf_op jit(solution)/shard_map/all_to_all | solution.py:399
  81.8 1.5 %gram_row.1 = (f32[3,1,8]{2,1,0:T(1,128)}, f32[1,32]{1,0:T(1,128)}, f32[8,64,128]{2,1,0:T(8,128)}) custom-call(f32[448,128]{1,0:T(8,128)S(1)} %bitcast.19, s32[4]{0:T(128)} %copy-done, f32[8,64,128]{2,1,0:T(8,128)S(1)} %get-tuple-element.37.sat), custom_call_target="tpu_custom_call" | custom-call | tf_op jit(solution)/shard_map/gram_row/pallas_call | solution.py:401
  (1 shorter events, 0.0 us)
Async XLA Ops:
  2.3 35.4 %collective-permute-start.1 = (f32[8,64,128]{2,1,0:T(8,128)S(1)}, f32[8,64,128]{2,1,0:T(8,128)S(1)}, u32[]{:S(2)}, u32[]{:S(2)}) collective-permute-start(f32[8,64,128]{2,1,0:T(8,128)S(1)} %get-tuple-element.28), channel_id=1, source_target_pairs={{1,0},{2,1},{3,2},{4,3},{5,4},{6,5},{7,6},{8,7},{9,8},{10,9},{11,1... | collective-permute-start | bytes 786440 | tf_op jit(solution)/shard_map/ppermute | solution.py:356
  11.1 26.6 %collective-permute-start = (f32[7,64,128]{2,1,0:T(8,128)S(1)}, f32[7,64,128]{2,1,0:T(8,128)S(1)}, u32[]{:S(2)}, u32[]{:S(2)}) collective-permute-start(f32[7,64,128]{2,1,0:T(8,128)S(1)} %get-tuple-element.27.after), channel_id=1, source_target_pairs={{0,1},{1,2},{2,3},{3,4},{4,5},{5,6},{6,7},{7,8},{8,9},{9,10},{10,1... | collective-permute-start | bytes 688136 | tf_op jit(solution)/shard_map/ppermute | solution.py:355
  21.1 0.7 copy-start.3
  21.1 0.7 copy-start.4
  21.2 0.7 copy-start.1
  21.2 0.7 copy-start.2
  23.3 14.4 %copy-start = (s32[4]{0:T(128)}, s32[4]{0:T(128)S(1)}, u32[]{:S(2)}) copy-start(s32[4]{0:T(128)S(1)} %pad_add_fusion.where) | copy-start | bytes 52
